TPU v7x, 128 devices: a whole 4x4x4 slice. The times are simulated.
128 devices in a mesh: req: 32 (over x, z, core), head: 4 (over y).
Axes of the slice: x: 4, y: 4, z: 4, core: 2. Of those that a mesh axis runs over, the one named last changes fastest.
Arguments:
- streams: bfloat16 [128, 64, 4, 2048], P('req'), may hold values from -6 to 6
- w_query: bfloat16 [2048, 2048], P(None, 'head'), may hold values from -0.125 to 0.125
- w_key: bfloat16 [2048, 2048], P(None, 'head'), may hold values from -0.125 to 0.125
- w_value: bfloat16 [2048, 2048], P(None, 'head'), may hold values from -0.125 to 0.125
- w_output: bfloat16 [2048, 2048], P('head'), may hold values from -0.125 to 0.125
- w_gate: bfloat16 [2048, 8192], P(None, 'req'), may hold values from -0.125 to 0.125
- w_up: bfloat16 [2048, 8192], P(None, 'req'), may hold values from -0.125 to 0.125
- w_down: bfloat16 [8192, 2048], P('req'), may hold values from -0.0625 to 0.0625
- cache_keys: bfloat16 [128, 1024, 2048], P('req', None, 'head'), may hold values from -250 to 250
- cache_values: bfloat16 [128, 1024, 2048], P('req', None, 'head'), may hold values from -6 to 6
- hc_in: float32 [2, 4], replicated, may hold values from 0.1 to 0.6
- hc_res: float32 [2, 4, 4], replicated, may hold values from -0.4 to 0.8
- hc_out: float32 [2, 4], replicated, may hold values from 0.5 to 1.5
- parents: int32 [128, 64], replicated, may hold values from 0 to 62, as said below
- draft_len: int32 [128], replicated, may hold values from 1 to 64, 6144 in all
- cache_len: int32 [128], replicated, may hold values from 1 to 1024, 65536 in all
- accept_pick: int32 [128], replicated, may hold values from 0 to 63
- slot_owner: int32 [128], replicated, may hold values from 0 to 127, each once
Outputs:
- new_streams: bfloat16 [128, 64, 4, 2048], P('req', 'head')
- accepted_kv: bfloat16 [128, 64, 2, 2048], P('req', None, None, 'head')
Inputs may be any that keep to these rules, and one draw needn't show every extreme that they name: parents[r, 0] = 0 and 0 <= parents[r, p] < p for p >= 1. `draft_len`: the live draft nodes of all requests sum to exactly 6144.
All inputs are finite; a program needn't handle non-finite values.
Results may differ from a plain program's by a relative error of at most 0.024.
Values may be sent and summed in bfloat16 or wider, within the bound.
No kernel may reach another device: no remote copies, remote signals or barrier semaphores. Data moves between devices by JAX's collectives and lax.ppermute only.
A program may use at most 128 MiB of HBM per device.

v0:
```python
import jax
import jax.numpy as jnp
from jax import lax
from jax.sharding import PartitionSpec as P

HD = 128


def ancestry(parent_ids):
    count = parent_ids.shape[-1]
    nodes = jnp.arange(count, dtype=jnp.int32)
    links = (parent_ids[..., :, None] == nodes).astype(jnp.float32)
    unit = (nodes[:, None] == nodes[None, :]).astype(jnp.float32)
    above = jnp.minimum(links + unit, 1.0)
    for rounds in range((count - 1).bit_length()):
        above = jnp.minimum(jnp.matmul(above, above, precision=lax.Precision.HIGHEST), 1.0)
    depth = jnp.sum(above, axis=-1) - 1.0
    return (above, depth)


def normalize(values):
    center = jnp.mean(values, axis=-1, keepdims=True)
    spread = jnp.mean(jnp.square(values - center), axis=-1, keepdims=True)
    return (values - center) * lax.rsqrt(spread + 1e-05)


def rotate(values, position, head_size):
    half = head_size // 2
    freq = jnp.power(10000.0, -(jnp.arange(half, dtype=jnp.float32) * 2.0 / head_size))
    angle = position[..., None] * freq
    shaped = values.reshape(values.shape[:-1] + (-1, head_size))
    first, second = (shaped[..., :half], shaped[..., half:])
    cosine = jnp.cos(angle)[..., None, :]
    sine = jnp.sin(angle)[..., None, :]
    turned = jnp.concatenate(
        [first * cosine - second * sine, second * cosine + first * sine], axis=-1
    )
    return turned.reshape(values.shape)


def body(
    streams,
    w_query,
    w_key,
    w_value,
    w_output,
    w_gate,
    w_up,
    w_down,
    cache_keys,
    cache_values,
    hc_in,
    hc_res,
    hc_out,
    parents,
    draft_len,
    cache_len,
    accept_pick,
    slot_owner,
):
    highest = lax.Precision.HIGHEST
    local_slots, draft, stream_count, width = streams.shape
    local_width = w_query.shape[1]
    local_heads = local_width // HD
    cache_size = cache_keys.shape[1]
    groups = lax.axis_size("head")
    quarter = draft // groups
    requests = slot_owner.shape[0]
    scale = HD ** (-0.5)
    req_index = lax.axis_index("req")
    everyone = jnp.arange(requests, dtype=jnp.int32)
    my_slots = req_index * local_slots + jnp.arange(local_slots, dtype=jnp.int32)
    slot_pick = everyone[None, :] == my_slots[:, None]
    owner = jnp.sum(jnp.where(slot_pick, slot_owner[None, :], 0), axis=1)
    owner_pick = everyone[None, :] == owner[:, None]

    def lookup(table):
        return jnp.sum(jnp.where(owner_pick, table[None, :], 0), axis=1)

    parent_ids = jnp.sum(jnp.where(owner_pick[:, :, None], parents[None, :, :], 0), axis=1)
    draft_count = lookup(draft_len)
    cache_count = lookup(cache_len)
    accepted = jnp.minimum(lookup(accept_pick), draft_count - 1)
    above, depth = ancestry(parent_ids)
    hidden = streams.astype(jnp.float32)
    mixed_in = jnp.einsum("spmd,m->spd", hidden, hc_in[0], precision=highest)
    normed = normalize(mixed_in).astype(jnp.bfloat16).reshape(local_slots * draft, width)
    position = (cache_count.astype(jnp.float32)[:, None] + depth).reshape(-1)
    query = rotate(
        jnp.dot(normed, w_query, preferred_element_type=jnp.float32), position, HD
    ).astype(jnp.bfloat16)
    keys = rotate(jnp.dot(normed, w_key, preferred_element_type=jnp.float32), position, HD).astype(
        jnp.bfloat16
    )
    values = jnp.dot(normed, w_value, preferred_element_type=jnp.float32).astype(jnp.bfloat16)
    query_h = query.reshape(local_slots, draft, local_heads, HD)
    keys_h = keys.reshape(local_slots, draft, local_heads, HD)
    values_h = values.reshape(local_slots, draft, local_heads, HD)
    stored_keys = cache_keys.reshape(local_slots, cache_size, local_heads, HD)
    stored_values = cache_values.reshape(local_slots, cache_size, local_heads, HD)
    cached = (
        jnp.einsum("sphe,sche->shpc", query_h, stored_keys, preferred_element_type=jnp.float32)
        * scale
    )
    live = jnp.arange(cache_size, dtype=jnp.int32)[None, :] < cache_count[:, None]
    cached = jnp.where(live[:, None, None, :], cached, -1e30)
    local = (
        jnp.einsum("sphe,sqhe->shpq", query_h, keys_h, preferred_element_type=jnp.float32) * scale
    )
    local = jnp.where((above > 0.5)[:, None, :, :], local, -1e30)
    top = jnp.maximum(jnp.max(cached, axis=-1), jnp.max(local, axis=-1))[..., None]
    cached_exp = jnp.exp(cached - top)
    local_exp = jnp.exp(local - top)
    total = jnp.sum(cached_exp, axis=-1, keepdims=True) + jnp.sum(local_exp, axis=-1, keepdims=True)
    weight_cache = (cached_exp / total).astype(jnp.bfloat16)
    weight_local = (local_exp / total).astype(jnp.bfloat16)
    attended = jnp.einsum(
        "shpc,sche->pshe", weight_cache, stored_values, preferred_element_type=jnp.float32
    )
    attended = attended + jnp.einsum(
        "shpq,sqhe->pshe", weight_local, values_h, preferred_element_type=jnp.float32
    )
    attended = attended.astype(jnp.bfloat16).reshape(draft, local_slots, local_width)
    attn_out = lax.psum_scatter(
        jnp.einsum("psk,kd->psd", attended, w_output, preferred_element_type=jnp.float32).astype(
            jnp.bfloat16
        ),
        "head",
        scatter_dimension=0,
        tiled=True,
    ).astype(jnp.float32)
    head_index = lax.axis_index("head")
    first_position = head_index * quarter
    own = lax.dynamic_slice_in_dim(hidden, first_position, quarter, 1)
    carried = jnp.einsum("spnd,nm->spmd", own, hc_res[0], precision=highest)
    carried = (
        carried + hc_out[0][None, None, :, None] * jnp.transpose(attn_out, (1, 0, 2))[:, :, None, :]
    )
    own_rows = local_slots * quarter
    first = carried.astype(jnp.bfloat16).reshape(own_rows, stream_count, width)
    positions_here = first_position + jnp.arange(quarter, dtype=jnp.int32)
    valid = (positions_here[None, :] < draft_count[:, None]).reshape(-1)
    rows_wide = first.astype(jnp.float32)
    normed_rows = normalize(jnp.einsum("nmd,m->nd", rows_wide, hc_in[1], precision=highest)).astype(
        jnp.bfloat16
    )
    piece = lax.all_gather(normed_rows, "req", axis=0, tiled=True)
    gate = jnp.dot(piece, w_gate, preferred_element_type=jnp.float32)
    upward = jnp.dot(piece, w_up, preferred_element_type=jnp.float32)
    inner = (jax.nn.silu(gate) * upward).astype(jnp.bfloat16)
    mlp_out = lax.psum_scatter(
        jnp.dot(inner, w_down, preferred_element_type=jnp.float32).astype(jnp.bfloat16),
        "req",
        scatter_dimension=0,
        tiled=True,
    ).astype(jnp.float32)
    final_rows = jnp.einsum("nkd,km->nmd", rows_wide, hc_res[1], precision=highest)
    final = jnp.where(
        valid[:, None, None], final_rows + hc_out[1][None, :, None] * mlp_out[:, None, :], 0.0
    ).astype(jnp.bfloat16)
    new_streams = final.reshape(local_slots, quarter, stream_count, width)
    nodes = jnp.arange(draft, dtype=jnp.int32)
    path_row = jnp.sum(
        jnp.where((nodes[None, :] == accepted[:, None])[:, :, None], above, 0.0), axis=1
    )
    take = (
        (depth[:, None, :] == nodes.astype(jnp.float32)[None, :, None])
        & (path_row[:, None, :] > 0.5)
    ).astype(jnp.bfloat16)
    keys_rows = keys.reshape(local_slots, draft, local_width)
    values_rows = values.reshape(local_slots, draft, local_width)
    new_keys = jnp.einsum(
        "stq,sqk->stk", take, keys_rows, preferred_element_type=jnp.float32
    ).astype(jnp.bfloat16)
    new_values = jnp.einsum(
        "stq,sqk->stk", take, values_rows, preferred_element_type=jnp.float32
    ).astype(jnp.bfloat16)
    accepted_kv = jnp.stack([new_keys, new_values], axis=2)
    return (new_streams, accepted_kv)


def solution(mesh):
    placed = (
        P("req", None, None, None),
        P(None, "head"),
        P(None, "head"),
        P(None, "head"),
        P("head", None),
        P(None, "req"),
        P(None, "req"),
        P("req", None),
        P("req", None, "head"),
        P("req", None, "head"),
        P(),
        P(),
        P(),
        P(),
        P(),
        P(),
        P(),
        P(),
    )
    return jax.shard_map(
        body,
        mesh=mesh,
        in_specs=placed,
        out_specs=(P("req", "head", None, None), P("req", None, None, "head")),
        check_vma=False,
    )
```

profile of v0, /device:TPU:0, one launch (start us, length us, event | category | flops | bytes accessed | tf_op | source)
XLA Modules:
  0.0 265.1 jit_solution(14680197965514249326)
XLA Ops:
  9.8 0.9 select_reduce_fusion.1
  13.4 8.5 %fusion.58 = f32[1,4,64,2048]{3,0,2,1:T(1,128)S(1)} fusion(bf16[4,64,4,2048]{3,2,1,0:T(4,128)(2,1)} %param.18, f32[2,4]{1,0:T(2,128)S(1)} %copy-done.11), kind=kOutput, calls=%fused_computation.125 | convolution fusion | flops 25165824 | bytes 6291968 | tf_op jit(solution)/shard_map/spmd,m->spd/dot_general | solution.py:86
  26.3 4.0 %copy.77 = bf16[512,2048]{1,0:T(8,128)(2,1)} copy(bf16[512,2048]{0,1:T(8,128)(2,1)} %bitcast.134) | data formatting | bytes 4194304 | tf_op jit(solution)/shard_map/dot_general | solution.py:90
  30.3 1.0 multiply_cosine_fusion
  31.3 2.3 fusion.65
  33.9 4.0 %copy.78 = bf16[512,2048]{1,0:T(8,128)(2,1)} copy(bf16[512,2048]{0,1:T(8,128)(2,1)} %bitcast.135) | data formatting | bytes 4194304 | tf_op jit(solution)/shard_map/dot_general | solution.py:92
  37.9 2.7 %fusion.66 = f32[256,4,128]{0,2,1:T(8,128)S(1)} fusion(bf16[256,2048,1]{1,0,2:T(8,128)(2,1)} %bitcast.142, bf16[4,128,2048]{2,1,0:T(8,128)(2,1)} %bitcast.137), kind=kOutput, calls=%fused_computation.134 | convolution fusion | flops 536870912 | bytes 3670016 | tf_op jit(solution)/shard_map/dot_general | solution.py:92
  41.5 1.2 fusion.64
  42.8 3.8 %fusion.6 = (f32[4,4,64]{2,1,0:T(4,128)S(1)}, f32[4,4,64,1024]{3,2,1,0:T(8,128)S(1)}) fusion(pred[4,1024]{1,0:T(4,128)(4,1)S(1)} %iota_compare_fusion.3, bf16[4,64,4,128]{3,1,0,2:T(8,128)(2,1)S(1)} %bitcast.139, bf16[4,1024,512]{2,1,0:T(8,128)(2,1)} %param.26), kind=kOutput, calls=%fused_computation.10 | convolution fusion | flops 271580160 | bytes 8658944 | tf_op jit(solution)/shard_map/sphe,sche->shpc/dot_general | solution.py:102
  46.7 1.1 fusion.7
  47.8 1.1 copy-done.7
  48.9 1.7 fusion.20
  50.9 1.7 convolution_convert_fusion.1
  52.7 26.1 %reduce-scatter.3.cloned.1.call-done = bf16[16,4,2048]{2,0,1:T(8,128)(2,1)} async-done(((bf16[64,4,2048]{2,0,1:T(8,128)(2,1)}), bf16[16,4,2048]{2,0,1:T(8,128)(2,1)}) %reduce-scatter.3.cloned.1.call-update) | async-done | bytes 262160 | tf_op jit(solution)/shard_map/reduce_scatter | solution.py:124
  78.8 1.0 convert_bitcast_fusion
  79.8 3.4 %fusion.11 = bf16[4,16,4,2048]{3,2,1,0:T(4,128)(2,1)S(1)} fusion(f32[4,16,2048]{2,1,0:T(8,128)S(1)} %convert_bitcast_fusion, f32[4]{0:T(128)S(1)} %get-tuple-element.22, bf16[4,64,4,2048]{3,2,1,0:T(4,128)(2,1)} %param.18, s32[]{:T(128)S(6)} %select_n.38, f32[2,4,4]{2,1,0:T(4,128)S(1)} %copy-done.10), kind=kOutput, calls=%fused_computation.18 | convolution fusion | flops 26738688 | bytes 2624004 | tf_op jit(solution)/shard_map/spnd,nm->spmd/dot_general | solution.py:135
  83.3 1.8 fusion.57
  86.6 52.8 %all-gather.2.cloned.1.call-done = bf16[2048,2048]{1,0:T(8,128)(2,1)} async-done(((bf16[64,2048]{1,0:T(8,128)(2,1)}), bf16[2048,2048]{1,0:T(8,128)(2,1)}) %all-gather.2.cloned.1.call-update) | async-done | bytes 8388624 | tf_op jit(solution)/shard_map/all_gather | solution.py:147
  139.3 7.1 %fusion.67 = f32[2048,256]{1,0:T(8,128)} fusion(bf16[2048,2048]{1,0:T(8,128)(2,1)} %all-gather.2.cloned.1.call-done, bf16[2048,256]{1,0:T(8,128)(2,1)S(1)} %copy-done.9), kind=kOutput, calls=%fused_computation.135 | convolution fusion | flops 2147483648 | bytes 11534336 | tf_op jit(solution)/shard_map/dot_general | solution.py:148
  146.4 13.8 %convolution_convert_fusion = bf16[2048,2048]{1,0:T(8,128)(2,1)} fusion(bf16[256,2048]{1,0:T(8,128)(2,1)} %param.25, bf16[2048,2048]{1,0:T(8,128)(2,1)} %all-gather.2.cloned.1.call-done, bf16[2048,256]{1,0:T(8,128)(2,1)} %param.24, f32[2048,256]{1,0:T(8,128)} %fusion.67), kind=kOutput, calls=%fused_computation | convolution fusion | flops 4302307328 | bytes 20971520 | tf_op jit(solution)/shard_map/dot_general | solution.py:152
  161.7 1.3 copy.69
  163.1 89.6 %reduce-scatter.5.cloned.1.call-done = bf16[64,2048]{1,0:T(8,128)(2,1)} async-done(((bf16[2048,2048]{1,0:T(8,128)(2,1)}), bf16[64,2048]{1,0:T(8,128)(2,1)}) %reduce-scatter.5.cloned.1.call-update) | async-done | bytes 262160 | tf_op jit(solution)/shard_map/reduce_scatter | solution.py:151
  252.7 1.0 convert_element_type.102
  253.7 4.9 %fusion.13 = bf16[64,4,2048]{2,1,0:T(4,128)(2,1)} fusion(bf16[64,4,2048]{2,1,0:T(4,128)(2,1)} %bitcast.146, f32[64,2048]{1,0:T(8,128)S(1)} %convert_element_type.102, f32[4]{0:T(128)S(1)} %get-tuple-element.21, pred[64]{0:T(512)(128)(4,1)S(1)} %lt.43, f32[2,4,4]{2,1,0:T(4,128)S(1)} %copy-done.10), kind=kOutput, calls=%fused_computation.21 | convolution fusion | flops 27262976 | bytes 2624512 | tf_op jit(solution)/shard_map/nkd,km->nmd/dot_general | solution.py:157
  (86 shorter events, 14.3 us)
Async XLA Ops:
  7.2 43.7 %copy-start = (bf16[512,2048]{1,0:T(8,128)(2,1)S(1)}, bf16[512,2048]{1,0:T(8,128)(2,1)}, u32[]{:S(2)}) copy-start(bf16[512,2048]{1,0:T(8,128)(2,1)} %param.22) | copy-start | bytes 6291460
  7.2 6.3 %copy-start.11 = (f32[2,4]{1,0:T(2,128)S(1)}, f32[2,4]{1,0:T(2,128)}, u32[]{:S(2)}) copy-start(f32[2,4]{1,0:T(2,128)} %param.28) | copy-start | bytes 100
  7.2 71.6 %reduce-scatter.3.cloned.1.call-start = ((), (), s32[]{:S(2)}) async-start(), calls=%async_computation.2 | async-start | bytes 1310720 | tf_op jit(solution)/shard_map/reduce_scatter | solution.py:124
  9.6 3.0 %copy-start.5 = (s32[4]{0:T(128)}, s32[4]{0:T(128)S(1)}, u32[]{:S(2)}) copy-start(s32[4]{0:T(128)S(1)} %get-tuple-element.11) | copy-start | bytes 52
  23.2 1.6 copy-start.8
  24.0 7.3 %copy-start.2 = (bf16[4,64,2048]{2,1,0:T(8,128)(2,1)}, bf16[4,64,2048]{2,1,0:T(8,128)(2,1)S(1)}, u32[]{:S(2)}) copy-start(bf16[4,64,2048]{2,1,0:T(8,128)(2,1)S(1)} %multiply_convert_fusion) | copy-start | bytes 3145732
  46.7 2.2 copy-start.7
  48.9 1.7 copy-start.3
  50.9 1.8 copy-start.4
  50.9 28.9 %copy-start.10 = (f32[2,4,4]{2,1,0:T(4,128)S(1)}, f32[2,4,4]{2,1,0:T(4,128)}, u32[]{:S(2)}) copy-start(f32[2,4,4]{2,1,0:T(4,128)} %param.29) | copy-start | bytes 388
  52.6 86.7 %all-gather.2.cloned.1.call-start = ((), (), s32[]{:S(2)}) async-start(), calls=%async_computation.3 | async-start | bytes 8650752 | tf_op jit(solution)/shard_map/all_gather | solution.py:147
  52.7 30.5 %copy-start.12 = (f32[2,4]{1,0:T(2,128)S(1)}, f32[2,4]{1,0:T(2,128)}, u32[]{:S(2)}) copy-start(f32[2,4]{1,0:T(2,128)} %param.28) | copy-start | bytes 100
  83.2 2.4 copy-start.13
  83.2 56.1 %copy-start.9 = (bf16[2048,256]{1,0:T(8,128)(2,1)S(1)}, bf16[2048,256]{1,0:T(8,128)(2,1)}, u32[]{:S(2)}) copy-start(bf16[2048,256]{1,0:T(8,128)(2,1)} %param.23) | copy-start | bytes 3145732
  86.5 166.1 %reduce-scatter.5.cloned.1.call-start = ((), (), s32[]{:S(2)}) async-start(), calls=%async_computation.4 | async-start | bytes 8650752 | tf_op jit(solution)/shard_map/reduce_scatter | solution.py:151
  160.2 0.6 copy-start.6
  253.7 5.0 %copy-start.1 = (bf16[512,2048]{1,0:T(8,128)(2,1)S(1)}, bf16[512,2048]{1,0:T(8,128)(2,1)}, u32[]{:S(2)}) copy-start(bf16[512,2048]{1,0:T(8,128)(2,1)} %param.22) | copy-start | bytes 6291460
Sparse Core Ops, SparseCore 0:
  52.8 26.0 reduce-scatter.2
  86.6 52.6 all-gather.1
  160.4 92.2 reduce-scatter.4
where the time goes:
time: 266 us; the launch traced here: 265 us
  waiting for transfers between devices  169 us (64%)
  matrix products  56.2 us (21%)
  local copies, waits for them, and re-layouts  14.7 us (6%)
  between operations  14.2 us (5%)
  other arithmetic  11.5 us (4%)
    reduce_scatter x1, waiting for transfers between devices, body(): lax.psum_scatter(jnp.dot(inner, w_down, preferred_element_type=jnp.float3...  89.6 us
    all_gather x1, waiting for transfers between devices, body(): piece = lax.all_gather(normed_rows, 'req', axis=0, tiled=True)  52.8 us
    reduce_scatter x1, waiting for transfers between devices, body(): lax.psum_scatter(jnp.einsum('psk,kd->psd', attended, w_output, preferred_...  26.1 us
    dot_general x1, matrix products, body(): jnp.dot(inner, w_down, preferred_element_type=jnp.float32)  13.8 us
    dot_general x1, matrix products, body(): mixed_in = jnp.einsum('spmd,m->spd', hidden, hc_in[0], precision=highest)  8.45 us
    dot_general x1, matrix products, body(): gate = jnp.dot(piece, w_gate, preferred_element_type=jnp.float32)  7.09 us
  transfers between devices with their start and end apart: 3, of which 3 were waited for; matrix products, arithmetic and copies ran while one was open for 1% of the time, Pallas kernels for 0%

commit v1 on v0

v1 whole, which is shorter than its diff:
```python
import functools

import jax
import jax.numpy as jnp
import numpy as np
from jax import lax
from jax.experimental import pallas as pl
from jax.experimental.pallas import tpu as pltpu
from jax.sharding import PartitionSpec as P

HD = 128
SLOTS = 4
DRAFT = 64
CACHE = 1024
D = 2048
NS = 4
LT = D // 128
Q = 16
SCALE = HD ** (-0.5)
BF = jnp.bfloat16
F32 = jnp.float32
NT = (((1,), (1,)), ((), ()))


def mm(a, b):
    return jnp.dot(a, b, preferred_element_type=F32)


def mm_nt(a, b):
    return lax.dot_general(a, b, NT, preferred_element_type=F32)


def normalize(x):
    center = jnp.sum(x, axis=-1, keepdims=True) * (1.0 / D)
    y = x - center
    spread = jnp.sum(y * y, axis=-1, keepdims=True) * (1.0 / D)
    return y * lax.rsqrt(spread + 1e-05)


def front_kernel(
    place,
    owner,
    dlen,
    clen,
    pick,
    hc_in,
    parents,
    freq,
    st,
    wq,
    wk,
    wv,
    ck,
    cv,
    wo,
    out,
    kv_out,
    raw,
    xbuf,
    normed,
    above_s,
    take_s,
    cos_s,
    sin_s,
    att,
    acc,
    kvs,
):
    i = pl.program_id(0)
    base = place[0] * SLOTS

    @pl.when(i < SLOTS)
    def _():
        s = i
        r = owner[base + s]
        raw[...] = st[...].astype(F32)
        rows = DRAFT
        for j in range(LT):
            x = hc_in[0, 0] * raw[pl.ds(j * NS, rows, stride=LT * NS), :]
            for m in range(1, NS):
                x = x + hc_in[0, m] * raw[pl.ds(j * NS + m, rows, stride=LT * NS), :]
            xbuf[:, j * 128 : (j + 1) * 128] = x
        normed[pl.ds(pl.multiple_of(s * DRAFT, DRAFT), DRAFT), :] = normalize(xbuf[...]).astype(BF)
        par = parents[pl.ds(r, 1), :]
        qi = lax.broadcasted_iota(jnp.int32, (DRAFT, DRAFT), 0)
        pi = lax.broadcasted_iota(jnp.int32, (DRAFT, DRAFT), 1)
        eye = (qi == pi).astype(F32)
        up = jnp.where(par == qi, 1.0, eye)
        for rounds in range(6):
            b = up.astype(BF)
            up = jnp.minimum(mm(b, b), 1.0)
        above = mm_nt(eye.astype(BF), up.astype(BF))
        above_s[s] = above
        depth_row = jnp.sum(up, axis=0, keepdims=True) - 1.0
        depth = jnp.sum(above, axis=1, keepdims=True) - 1.0
        a = jnp.minimum(pick[r], dlen[r] - 1)
        path = above_s[s, pl.ds(a, 1), :]
        take = jnp.where(depth_row == qi.astype(F32), path, 0.0)
        take_s[s] = take.astype(BF)
        angle = (clen[r].astype(F32) + depth) * freq[...]
        lane = lax.broadcasted_iota(jnp.int32, (DRAFT, HD), 1)
        at = pl.ds(pl.multiple_of(s * DRAFT, DRAFT), DRAFT)
        cos_s[at, :] = jnp.cos(angle)
        sine = jnp.sin(angle)
        sin_s[at, :] = jnp.where(lane < HD // 2, -sine, sine)

    @pl.when(i >= SLOTS)
    def _():
        g = i - SLOTS
        x = normed[...]
        q2 = mm(x, wq[...])
        k2 = mm(x, wk[...])
        v2 = mm(x, wv[...]).astype(BF)
        cosine = cos_s[...]
        sine = sin_s[...]
        col = lax.broadcasted_iota(jnp.int32, (DRAFT, CACHE), 1)
        for hh in range(2):
            cols = slice(hh * HD, (hh + 1) * HD)
            qh = q2[:, cols]
            kh = k2[:, cols]
            qh = (qh * cosine + pltpu.roll(qh, HD // 2, 1) * sine).astype(BF)
            kh = (kh * cosine + pltpu.roll(kh, HD // 2, 1) * sine).astype(BF)
            vh = v2[:, cols]
            for s in range(SLOTS):
                at = slice(s * DRAFT, (s + 1) * DRAFT)
                length = clen[owner[base + s]]
                qs, ks, vs = qh[at], kh[at], vh[at]
                sc = mm_nt(qs, ck[s, :, cols]) * SCALE
                sc = jnp.where(col < length, sc, -1e30)
                lo = mm_nt(qs, ks) * SCALE
                lo = jnp.where(above_s[s] > 0.5, lo, -1e30)
                top = jnp.maximum(
                    jnp.max(sc, axis=-1, keepdims=True), jnp.max(lo, axis=-1, keepdims=True)
                )
                e1 = jnp.exp(sc - top)
                e2 = jnp.exp(lo - top)
                total = jnp.sum(e1, axis=-1, keepdims=True) + jnp.sum(e2, axis=-1, keepdims=True)
                inv = 1.0 / total
                w1 = (e1 * inv).astype(BF)
                w2 = (e2 * inv).astype(BF)
                o = mm(w1, cv[s, :, cols]) + mm(w2, vs)
                att[at, cols] = o.astype(BF)
                tk = take_s[s]
                kvs[s, pl.ds((g * 2 + hh) * 2, DRAFT, stride=8), :] = mm(tk, ks)
                kvs[s, pl.ds((g * 2 + hh) * 2 + 1, DRAFT, stride=8), :] = mm(tk, vs)
        part = mm(att[...], wo[...])

        @pl.when(g == 0)
        def _():
            acc[...] = part

        @pl.when(g == 1)
        def _():
            full = (acc[...] + part).astype(BF)
            for s in range(SLOTS):
                for y in range(4):
                    out[y, s * Q : (s + 1) * Q, :] = full[
                        s * DRAFT + y * Q : s * DRAFT + (y + 1) * Q
                    ]
                kv_out[s * 512 : (s + 1) * 512, :] = kvs[s].astype(BF)


def front(place, owner, dlen, clen, pick, hc_in, parents, freq, st, wq, wk, wv, ck, cv, wo):
    smem = pl.BlockSpec(memory_space=pltpu.SMEM)
    head = lambda i, *_: (0, jnp.maximum(i - SLOTS, 0))
    cache = lambda i, *_: (0, 0, jnp.maximum(i - SLOTS, 0))
    return pl.pallas_call(
        front_kernel,
        name="front",
        out_shape=(
            jax.ShapeDtypeStruct((4, SLOTS * Q, D), BF),
            jax.ShapeDtypeStruct((2048, 128), BF),
        ),
        grid_spec=pltpu.PrefetchScalarGridSpec(
            num_scalar_prefetch=5,
            grid=(SLOTS + 2,),
            in_specs=[
                smem,
                pl.BlockSpec((128, DRAFT), lambda i, *_: (0, 0)),
                pl.BlockSpec((1, HD), lambda i, *_: (0, 0)),
                pl.BlockSpec((4096, 128), lambda i, *_: (jnp.minimum(i, SLOTS - 1), 0)),
                pl.BlockSpec((D, 256), head),
                pl.BlockSpec((D, 256), head),
                pl.BlockSpec((D, 256), head),
                pl.BlockSpec((SLOTS, CACHE, 256), cache),
                pl.BlockSpec((SLOTS, CACHE, 256), cache),
                pl.BlockSpec((256, D), lambda i, *_: (jnp.maximum(i - SLOTS, 0), 0)),
            ],
            out_specs=[
                pl.BlockSpec((4, SLOTS * Q, D), lambda i, *_: (0, 0, 0)),
                pl.BlockSpec((2048, 128), lambda i, *_: (0, 0)),
            ],
            scratch_shapes=[
                pltpu.VMEM((4096, 128), F32),
                pltpu.VMEM((DRAFT, D), F32),
                pltpu.VMEM((SLOTS * DRAFT, D), BF),
                pltpu.VMEM((SLOTS, DRAFT, DRAFT), F32),
                pltpu.VMEM((SLOTS, DRAFT, DRAFT), BF),
                pltpu.VMEM((SLOTS * DRAFT, HD), F32),
                pltpu.VMEM((SLOTS * DRAFT, HD), F32),
                pltpu.VMEM((SLOTS * DRAFT, 256), BF),
                pltpu.VMEM((SLOTS * DRAFT, D), F32),
                pltpu.VMEM((SLOTS, 512, 128), F32),
            ],
        ),
        compiler_params=pltpu.CompilerParams(vmem_limit_bytes=56 * 2**20),
    )(place, owner, dlen, clen, pick, hc_in, parents, freq, st, wq, wk, wv, ck, cv, wo)


def mid_kernel(place, hc_in, hc_res, hc_out, parts, st, first, rows_a, rows_b, raw, xbuf):
    i = pl.program_id(0)
    raw[...] = st[...].astype(F32)
    for j in range(LT):
        lanes = slice(j * 128, (j + 1) * 128)
        attn = parts[0, :, lanes].astype(F32)
        for y in range(1, 4):
            attn = attn + parts[y, :, lanes].astype(F32)
        own = [raw[pl.ds(j * NS + n, Q, stride=LT * NS), :] for n in range(NS)]
        x = None
        for m in range(NS):
            c = hc_out[0, m] * attn
            for n in range(NS):
                c = c + hc_res[0, n, m] * own[n]
            c = c.astype(BF)
            first[m, :, lanes] = c
            t = hc_in[1, m] * c.astype(F32)
            x = t if x is None else x + t
        xbuf[:, lanes] = x
    normed = normalize(xbuf[...]).astype(BF)

    @pl.when(i < 2)
    def _():
        rows_a[...] = normed

    @pl.when(i >= 2)
    def _():
        rows_b[...] = normed


def mid(place, hc_in, hc_res, hc_out, parts, st):
    smem = pl.BlockSpec(memory_space=pltpu.SMEM)
    half = SLOTS * Q // 2
    return pl.pallas_call(
        mid_kernel,
        name="mid",
        out_shape=(
            jax.ShapeDtypeStruct((NS, SLOTS * Q, D), BF),
            jax.ShapeDtypeStruct((half, D), BF),
            jax.ShapeDtypeStruct((half, D), BF),
        ),
        grid_spec=pltpu.PrefetchScalarGridSpec(
            num_scalar_prefetch=1,
            grid=(SLOTS,),
            in_specs=[
                smem,
                smem,
                smem,
                pl.BlockSpec((4, Q, D), lambda i, p: (0, i, 0)),
                pl.BlockSpec((1024, 128), lambda i, p: (i * 4 + p[1], 0)),
            ],
            out_specs=[
                pl.BlockSpec((NS, Q, D), lambda i, p: (0, i, 0)),
                pl.BlockSpec((Q, D), lambda i, p: (jnp.minimum(i, 1), 0)),
                pl.BlockSpec((Q, D), lambda i, p: (jnp.maximum(i - 2, 0), 0)),
            ],
            scratch_shapes=[pltpu.VMEM((1024, 128), F32), pltpu.VMEM((Q, D), F32)],
        ),
    )(place, hc_in, hc_res, hc_out, parts, st)


def last_kernel(place, owner, dlen, hc_res, hc_out, first, *refs):
    parts_a, parts_b, out, raw, mlp_s = refs[:4], refs[4:8], refs[8], refs[9], refs[10]
    i = pl.program_id(0)

    @pl.when(i < 2)
    def _():
        t = parts_a[0][...].astype(F32)
        for p in parts_a[1:]:
            t = t + p[...].astype(F32)
        mlp_s[...] = t

    @pl.when(i >= 2)
    def _():
        t = parts_b[0][...].astype(F32)
        for p in parts_b[1:]:
            t = t + p[...].astype(F32)
        mlp_s[...] = t

    count = dlen[owner[place[0] * SLOTS + i]]
    spot = place[1] * Q + lax.broadcasted_iota(jnp.int32, (Q, 128), 0)
    alive = spot < count
    for j in range(LT):
        lanes = slice(j * 128, (j + 1) * 128)
        mlp = mlp_s[:, lanes]
        f = [first[n, :, lanes].astype(F32) for n in range(NS)]
        for m in range(NS):
            c = hc_out[1, m] * mlp
            for n in range(NS):
                c = c + hc_res[1, n, m] * f[n]
            raw[pl.ds(j * NS + m, Q, stride=LT * NS), :] = jnp.where(alive, c, 0.0)
    out[...] = raw[...].astype(BF)


def last(place, owner, dlen, hc_res, hc_out, first, parts_a, parts_b):
    smem = pl.BlockSpec(memory_space=pltpu.SMEM)
    a_spec = pl.BlockSpec((Q, D), lambda i, *_: (jnp.minimum(i, 1), 0))
    b_spec = pl.BlockSpec((Q, D), lambda i, *_: (jnp.maximum(i - 2, 0), 0))
    return pl.pallas_call(
        last_kernel,
        name="last",
        out_shape=jax.ShapeDtypeStruct((SLOTS * 1024, 128), BF),
        grid_spec=pltpu.PrefetchScalarGridSpec(
            num_scalar_prefetch=3,
            grid=(SLOTS,),
            in_specs=[smem, smem, pl.BlockSpec((NS, Q, D), lambda i, *_: (0, i, 0))]
            + [a_spec] * 4
            + [b_spec] * 4,
            out_specs=pl.BlockSpec((1024, 128), lambda i, *_: (i, 0)),
            scratch_shapes=[pltpu.VMEM((1024, 128), F32), pltpu.VMEM((Q, D), F32)],
        ),
    )(place, owner, dlen, hc_res, hc_out, first, *parts_a, *parts_b)


def ffn_kernel(sizes, outs, *refs):
    n = len(sizes)
    xs, (g0, g1, u0, u1, d0, d1) = refs[:n], refs[n : n + 6]
    ys, cat = refs[n + 6 : -1], refs[-1]
    o = 0
    for x, size in zip(xs, sizes):
        cat[o : o + size, :] = x[...]
        o += size
    step = 256
    done = 0
    where = 0
    for c in range(o // step):
        x = cat[c * step : (c + 1) * step, :]
        total = None
        for g, u, d in ((g0, u0, d0), (g1, u1, d1)):
            gate = mm(x, g[...])
            inner = (gate / (1.0 + jnp.exp(-gate)) * mm(x, u[...])).astype(BF)
            t = mm(inner, d[...])
            total = t if total is None else total + t
        total = total.astype(BF)
        pos = 0
        while pos < step:
            size = outs[where]
            ys[where][...] = total[pos : pos + size]
            pos += size
            where += 1


def ffn(xs, weights, outs):
    sizes = tuple(x.shape[0] for x in xs)
    vmem = pl.BlockSpec(memory_space=pltpu.VMEM)
    rows = sum(sizes)
    return pl.pallas_call(
        functools.partial(ffn_kernel, sizes, outs),
        name="ffn",
        out_shape=tuple(jax.ShapeDtypeStruct((o, D), BF) for o in outs),
        in_specs=[vmem] * (len(xs) + 6),
        out_specs=tuple([vmem] * len(outs)),
        scratch_shapes=[pltpu.VMEM((rows, D), BF)],
        cost_estimate=pl.CostEstimate(
            flops=rows * D * 512 * 6, transcendentals=rows * 512, bytes_accessed=rows * D * 4
        ),
        compiler_params=pltpu.CompilerParams(vmem_limit_bytes=56 * 2**20),
    )(*xs, *weights)


def shift_pairs(axis, step):
    pairs = []
    for x in range(4):
        for z in range(4):
            for c in range(2):
                tx = (x + step) % 4 if axis == "x" else x
                tz = (z + step) % 4 if axis == "z" else z
                pairs.append((x * 8 + z * 2 + c, tx * 8 + tz * 2 + c))
    return pairs


def shift(v, axis, step):
    return lax.ppermute(v, "req", shift_pairs(axis, step))


def swap_core(v):
    return lax.ppermute(v, "req", [(i, i ^ 1) for i in range(32)])


def add(a, b):
    return (a.astype(F32) + b.astype(F32)).astype(BF)


def body(
    streams,
    w_query,
    w_key,
    w_value,
    w_output,
    w_gate,
    w_up,
    w_down,
    cache_keys,
    cache_values,
    hc_in,
    hc_res,
    hc_out,
    parents,
    draft_len,
    cache_len,
    accept_pick,
    slot_owner,
):
    place = jnp.stack([lax.axis_index("req"), lax.axis_index("head")]).astype(jnp.int32)
    half = np.arange(64, dtype=np.float64)
    freq = np.power(10000.0, -(half * 2.0 / HD)).astype(np.float32)
    freq = jnp.asarray(np.concatenate([freq, freq])[None, :])
    st = streams.reshape(SLOTS, DRAFT, NS, LT, 128).transpose(0, 1, 3, 2, 4).reshape(-1, 128)
    weights = (w_gate, swap_core(w_gate), w_up, swap_core(w_up), w_down, swap_core(w_down))
    part, kv = front(
        place,
        slot_owner,
        draft_len,
        cache_len,
        accept_pick,
        hc_in,
        parents,
        freq,
        st,
        w_query,
        w_key,
        w_value,
        cache_keys,
        cache_values,
        w_output,
    )
    parts = lax.all_to_all(part, "head", 0, 0, tiled=False)
    first, rows_a, rows_b = mid(place, hc_in, hc_res, hc_out, parts, st)

    order = (("x", "z", rows_a), ("z", "x", rows_b))
    own4 = []
    for one, two, rows in order:
        own4.append(
            jnp.concatenate(
                [rows, shift(rows, one, 1), shift(rows, one, -1), shift(rows, one, 2)], axis=0
            )
        )
    near = []
    for (one, two, _), x in zip(order, own4):
        near.append((shift(x, two, 1), shift(x, two, -1)))
    far = []
    for (one, two, _), (l, r) in zip(order, near):
        far.append((shift(l[:64], two, 1), shift(r[64:], two, -1)))

    own_out = ffn(own4, weights, (128, 128))
    near_out = ffn([near[0][0], near[0][1], near[1][0], near[1][1]], weights, (64,) * 8)
    far_out = ffn([far[0][0], far[0][1], far[1][0], far[1][1]], weights, (64,) * 4)

    back = []
    for k, (one, two, _) in enumerate(order):
        l0, l1, r0, r1 = near_out[4 * k : 4 * k + 4]
        o0, o1 = far_out[2 * k : 2 * k + 2]
        u1 = shift(r1, two, 1)
        u2 = shift(l0, two, -1)
        t1 = shift(o0, two, 1)
        t2 = shift(o1, two, -1)
        v1 = shift(add(r0, t1), two, 1)
        v2 = shift(add(l1, t2), two, -1)
        s = own_out[k].astype(F32)
        upper = s[:64] + v1.astype(F32) + u2.astype(F32)
        lower = s[64:] + u1.astype(F32) + v2.astype(F32)
        back.append((upper.astype(BF), lower.astype(BF)))
    ends = []
    for k, (one, two, _) in enumerate(order):
        upper, lower = back[k]
        ends.append(
            (
                upper[:32],
                shift(upper[32:], one, -1),
                shift(lower[:32], one, 1),
                shift(lower[32:], one, 2),
            )
        )
    final = last(place, slot_owner, draft_len, hc_res, hc_out, first, ends[0], ends[1])
    new_streams = (
        final.reshape(SLOTS, Q, LT, NS, 128).transpose(0, 1, 3, 2, 4).reshape(SLOTS, Q, NS, D)
    )
    accepted_kv = (
        kv.reshape(SLOTS, DRAFT, 4, 2, 128).transpose(0, 1, 3, 2, 4).reshape(SLOTS, DRAFT, 2, 512)
    )
    return (new_streams, accepted_kv)


def solution(mesh):
    placed = (
        P("req", None, None, None),
        P(None, "head"),
        P(None, "head"),
        P(None, "head"),
        P("head", None),
        P(None, "req"),
        P(None, "req"),
        P("req", None),
        P("req", None, "head"),
        P("req", None, "head"),
        P(),
        P(),
        P(),
        P(),
        P(),
        P(),
        P(),
        P(),
    )
    return jax.shard_map(
        body,
        mesh=mesh,
        in_specs=placed,
        out_specs=(P("req", "head", None, None), P("req", None, None, "head")),
        check_vma=False,
    )
```

time: 266 us -> 179 us (0.67)
  waiting for transfers between devices: 169 us -> 50 us
  Pallas kernels: 0 us -> 57.2 us
  matrix products: 56.2 us -> 0 us
  starting transfers between devices: 0.12 us -> 55.3 us
  between operations: 14.2 us -> 1.07 us
  local copies, waits for them, and re-layouts: 14.7 us -> 8.07 us
  other arithmetic: 11.5 us -> 6.4 us
    reduce_scatter x2 -> x0, waiting for transfers between devices: 116 us -> none  [the longest x1 89.6 us: body(): lax.psum_scatter(jnp.dot(inner, w_down, preferred_element_type=jnp.float3...]
    pallas_call x0 -> x6, Pallas kernels: none -> 57.2 us  [the longest x1 26 us: front(): pl.pallas_call(front_kernel, name='front', out_shape=(jax.ShapeDtypeStruc...]
    dot_general x22 -> x0, matrix products: 56.2 us -> none  [the longest x1 13.8 us: body(): jnp.dot(inner, w_down, preferred_element_type=jnp.float32)]
    all_gather x1 -> x0, waiting for transfers between devices: 52.8 us -> none  [body(): piece = lax.all_gather(normed_rows, 'req', axis=0, tiled=True)]
    ppermute x0 -> x35, starting transfers between devices: none -> 50.7 us  [the longest x32 50.1 us: shift(): return lax.ppermute(v, 'req', shift_pairs(axis, step))]
    ppermute x0 -> x35, waiting for transfers between devices: none -> 35.3 us  [the longest x32 35.3 us: shift(): return lax.ppermute(v, 'req', shift_pairs(axis, step))]
    all_to_all x0 -> x1, waiting for transfers between devices: none -> 14.7 us  [body(): parts = lax.all_to_all(part, 'head', 0, 0, tiled=False)]
    dot_general x2 -> x0, local copies, waits for them, and re-layouts: 7.97 us -> none  [the longest x1 3.99 us: body(): jnp.dot(normed, w_key, preferred_element_type=jnp.float32)]
  transfers between devices with their start and end apart: 3 -> 36, of which waited for: 3 -> 15; matrix products, arithmetic and copies ran while one was open for 1% -> 5% of each run, Pallas kernels for 0% -> 11%
where the time goes in v1:
time: 179 us; the launch traced here: 178 us
  Pallas kernels  57.2 us (32%)
  starting transfers between devices  55.3 us (31%)
  waiting for transfers between devices  50 us (28%)
  local copies, waits for them, and re-layouts  8.07 us (5%)
  other arithmetic  6.4 us (4%)
    ppermute x32, starting transfers between devices, shift(): return lax.ppermute(v, 'req', shift_pairs(axis, step))  50.1 us
    ppermute x32, waiting for transfers between devices, shift(): return lax.ppermute(v, 'req', shift_pairs(axis, step))  35.3 us
    pallas_call x1, Pallas kernels, front(): pl.pallas_call(front_kernel, name='front', out_shape=(jax.ShapeDtypeStruc...  26 us
    pallas_call x3, Pallas kernels, ffn(): pl.pallas_call(functools.partial(ffn_kernel, sizes, outs), name='ffn', ou...  20.1 us
    all_to_all x1, waiting for transfers between devices, body(): parts = lax.all_to_all(part, 'head', 0, 0, tiled=False)  14.7 us
    unnamed x57, local copies, waits for them, and re-layouts  6.6 us
    pallas_call x1, Pallas kernels, mid(): pl.pallas_call(mid_kernel, name='mid', out_shape=(jax.ShapeDtypeStruct((N...  5.77 us
    pallas_call x1, Pallas kernels, last(): pl.pallas_call(last_kernel, name='last', out_shape=jax.ShapeDtypeStruct((...  5.3 us
  transfers between devices with their start and end apart: 36, of which 15 were waited for; matrix products, arithmetic and copies ran while one was open for 5% of the time, Pallas kernels for 11%

profile of v1, /device:TPU:0, one launch (start us, length us, event | category | flops | bytes accessed | tf_op | source)
XLA Modules:
  0.0 178.0 jit_solution(1030479577103823371)
XLA Ops:
  2.8 26.0 %front.1 = (bf16[4,64,2048]{2,1,0:T(8,128)(2,1)}, bf16[2048,128]{1,0:T(8,128)(2,1)}) custom-call(s32[2]{0:T(128)} %pad_add_fusion.place, s32[128]{0:T(128)} %owner.3, s32[128]{0:T(128)} %dlen.3, s32[128]{0:T(128)} %clen.1, s32[128]{0:T(128)} %pick.1, f32[2,4]{1,0:T(2,128)} %hc_in.3, s32[128,64]{1,0:T(8,128)} %copy.22.parents, f32[1,128]{1,0:T(1,128)} %constant.11.clone.freq, ...), custom_call_target="tpu_custom_call" | custom-call | tf_op jit(solution)/shard_map/front/pallas_call | solution.py:167
  28.8 4.7 %all-to-all-start = ((bf16[4,64,2048]{2,1,0:T(8,128)(2,1)}), bf16[4,64,2048]{2,1,0:T(8,128)(2,1)}, u32[]{:S(2)}, u32[]{:S(2)}) async-start(bf16[4,64,2048]{2,1,0:T(8,128)(2,1)} %get-tuple-element.21), calls=%async_computation | async-start | bytes 2097152 | tf_op jit(solution)/shard_map/all_to_all | solution.py:436
  34.0 14.7 %all-to-all-done.parts = bf16[4,64,2048]{2,1,0:T(8,128)(2,1)} async-done(((bf16[4,64,2048]{2,1,0:T(8,128)(2,1)}), bf16[4,64,2048]{2,1,0:T(8,128)(2,1)}, u32[]{:S(2)}, u32[]{:S(2)}) %all-to-all-start) | async-done | bytes 1048608 | tf_op jit(solution)/shard_map/all_to_all | solution.py:436
  48.7 5.8 %mid.1 = (bf16[4,64,2048]{2,1,0:T(8,128)(2,1)}, bf16[32,2048]{1,0:T(8,128)(2,1)}, bf16[32,2048]{1,0:T(8,128)(2,1)}) custom-call(s32[2]{0:T(128)} %pad_add_fusion.place, f32[2,4]{1,0:T(2,128)} %hc_in.3, f32[2,4,4]{2,1,0:T(4,128)} %hc_res.3, f32[2,4]{1,0:T(2,128)} %hc_out.3, bf16[4,64,2048]{2,1,0:T(8,128)(2,1)} %all-to-all-done.parts, bf16[16384,128]{1,0:T(8,128)(2,1)} %bitcast.18), custom_call_target="tpu_custom_call" | custom-call | tf_op jit(solution)/shard_map/mid/pallas_call | solution.py:243
  57.4 2.2 %collective-permute-start.4 = (bf16[32,2048]{1,0:T(8,128)(2,1)}, bf16[32,2048]{1,0:T(8,128)(2,1)S(1)}, u32[]{:S(2)}, u32[]{:S(2)}) collective-permute-start(bf16[32,2048]{1,0:T(8,128)(2,1)} %get-tuple-element.24), channel_id=1, source_target_pairs={{0,24},{4,28},{8,0},{12,4},{16,8},{20,12},{24,16},{28,20},{32,56},... | collective-permute-start | bytes 393224 | tf_op jit(solution)/shard_map/ppermute | solution.py:382
  64.9 2.8 %collective-permute-start.1 = (bf16[32,2048]{1,0:T(8,128)(2,1)}, bf16[32,2048]{1,0:T(8,128)(2,1)S(1)}, u32[]{:S(2)}, u32[]{:S(2)}) collective-permute-start(bf16[32,2048]{1,0:T(8,128)(2,1)} %get-tuple-element.23), channel_id=1, source_target_pairs={{0,96},{4,100},{8,104},{12,108},{16,112},{20,116},{24,120},{28,124... | collective-permute-start | bytes 393224 | tf_op jit(solution)/shard_map/ppermute | solution.py:382
  72.4 4.1 %collective-permute-start.12 = (bf16[128,2048]{1,0:T(8,128)(2,1)S(1)}, bf16[128,2048]{1,0:T(8,128)(2,1)S(1)}, u32[]{:S(2)}, u32[]{:S(2)}) collective-permute-start(bf16[128,2048]{1,0:T(8,128)(2,1)S(1)} %constant_dynamic-update-slice_fusion.4.refs_1_), channel_id=1, source_target_pairs={{0,96},{4,100},{8,104},{12,108},{16,112},{20,116},{24,120},{28,124... | collective-permute-start | bytes 1572872 | tf_op jit(solution)/shard_map/ppermute | solution.py:382
  76.6 7.3 %collective-permute-done.11.refs_2_ = bf16[128,2048]{1,0:T(8,128)(2,1)S(1)} collective-permute-done((bf16[128,2048]{1,0:T(8,128)(2,1)S(1)}, bf16[128,2048]{1,0:T(8,128)(2,1)S(1)}, u32[]{:S(2)}, u32[]{:S(2)}) %collective-permute-start.11) | collective-permute-done | bytes 524320 | tf_op jit(solution)/shard_map/ppermute | solution.py:382
  84.2 3.0 %collective-permute-start.10 = (bf16[128,2048]{1,0:T(8,128)(2,1)S(1)}, bf16[128,2048]{1,0:T(8,128)(2,1)S(1)}, u32[]{:S(2)}, u32[]{:S(2)}) collective-permute-start(bf16[128,2048]{1,0:T(8,128)(2,1)S(1)} %constant_dynamic-update-slice_fusion.refs_0_), channel_id=1, source_target_pairs={{0,24},{4,28},{8,0},{12,4},{16,8},{20,12},{24,16},{28,20},{32,56},... | collective-permute-start | bytes 1572872 | tf_op jit(solution)/shard_map/ppermute | solution.py:382
  87.2 8.6 %collective-permute-done.9.refs_0_ = bf16[128,2048]{1,0:T(8,128)(2,1)S(1)} collective-permute-done((bf16[128,2048]{1,0:T(8,128)(2,1)S(1)}, bf16[128,2048]{1,0:T(8,128)(2,1)S(1)}, u32[]{:S(2)}, u32[]{:S(2)}) %collective-permute-start.9) | collective-permute-done | bytes 524320 | tf_op jit(solution)/shard_map/ppermute | solution.py:382
  96.8 2.5 %collective-permute-start.16 = (bf16[64,2048]{1,0:T(8,128)(2,1)S(1)}, bf16[64,2048]{1,0:T(8,128)(2,1)S(1)}, u32[]{:S(2)}, u32[]{:S(2)}) collective-permute-start(bf16[64,2048]{1,0:T(8,128)(2,1)S(1)} %slice.68), channel_id=1, source_target_pairs={{0,96},{4,100},{8,104},{12,108},{16,112},{20,116},{24,120},{28,124... | collective-permute-start | bytes 786440 | tf_op jit(solution)/shard_map/ppermute | solution.py:382
  99.4 3.2 %collective-permute-start.14 = (bf16[64,2048]{1,0:T(8,128)(2,1)S(1)}, bf16[64,2048]{1,0:T(8,128)(2,1)S(1)}, u32[]{:S(2)}, u32[]{:S(2)}) collective-permute-start(bf16[64,2048]{1,0:T(8,128)(2,1)S(1)} %slice.66), channel_id=1, source_target_pairs={{0,24},{4,28},{8,0},{12,4},{16,8},{20,12},{24,16},{28,20},{32,56},... | collective-permute-start | bytes 786440 | tf_op jit(solution)/shard_map/ppermute | solution.py:382
  103.6 6.0 %ffn.3 = (bf16[128,2048]{1,0:T(8,128)(2,1)}, bf16[128,2048]{1,0:T(8,128)(2,1)}) custom-call(bf16[128,2048]{1,0:T(8,128)(2,1)} %copy-done.4, bf16[128,2048]{1,0:T(8,128)(2,1)} %copy-done.5, bf16[2048,256]{1,0:T(8,128)(2,1)} %refs_4_.5, bf16[2048,256]{1,0:T(8,128)(2,1)} %collective-permute-done.6.refs_3_.refs_5_, bf16[2048,256]{1,0:T(8,128)(2,1)} %refs_6_.5, ...), custom_call_target="tpu_custom_call" | custom-call | flops 1610612736 | bytes 2097152 | tf_op jit(solution)/shard_map/ffn/pallas_call | solution.py:356
  113.5 6.0 %ffn.5 = (bf16[64,2048]{1,0:T(8,128)(2,1)}, bf16[64,2048]{1,0:T(8,128)(2,1)}, bf16[64,2048]{1,0:T(8,128)(2,1)}, bf16[64,2048]{1,0:T(8,128)(2,1)}) custom-call(bf16[64,2048]{1,0:T(8,128)(2,1)} %copy-done.9, bf16[64,2048]{1,0:T(8,128)(2,1)} %copy-done.10, bf16[64,2048]{1,0:T(8,128)(2,1)} %copy-done.7, bf16[64,2048]{1,0:T(8,128)(2,1)} %copy-done.8, ...), custom_call_target="tpu_custom_call" | custom-call | flops 1610612736 | bytes 2097152 | tf_op jit(solution)/shard_map/ffn/pallas_call | solution.py:356
  119.6 8.1 %ffn.4 = (bf16[64,2048]{1,0:T(8,128)(2,1)}, bf16[64,2048]{1,0:T(8,128)(2,1)}, bf16[64,2048]{1,0:T(8,128)(2,1)}, bf16[64,2048]{1,0:T(8,128)(2,1)}, bf16[64,2048]{...) custom-call(bf16[128,2048]{1,0:T(8,128)(2,1)} %copy-done.19, ...), custom_call_target="tpu_custom_call" | custom-call | flops 3221225472 | bytes 4194304 | tf_op jit(solution)/shard_map/ffn/pallas_call | solution.py:356
  127.7 3.2 %collective-permute-start.28 = (bf16[64,2048]{1,0:T(8,128)(2,1)}, bf16[64,2048]{1,0:T(8,128)(2,1)S(1)}, u32[]{:S(2)}, u32[]{:S(2)}) collective-permute-start(bf16[64,2048]{1,0:T(8,128)(2,1)} %get-tuple-element.35), channel_id=1, source_target_pairs={{0,96},{4,100},{8,104},{12,108},{16,112},{20,116},{24,120},{28,124... | collective-permute-start | bytes 786440 | tf_op jit(solution)/shard_map/ppermute | solution.py:382
  131.5 3.2 %collective-permute-start.31 = (bf16[64,2048]{1,0:T(8,128)(2,1)S(1)}, bf16[64,2048]{1,0:T(8,128)(2,1)S(1)}, u32[]{:S(2)}, u32[]{:S(2)}) collective-permute-start(bf16[64,2048]{1,0:T(8,128)(2,1)S(1)} %copy-done.24), channel_id=1, source_target_pairs={{0,96},{4,100},{8,104},{12,108},{16,112},{20,116},{24,120},{28,124... | collective-permute-start | bytes 786440 | tf_op jit(solution)/shard_map/ppermute | solution.py:382
  140.1 2.2 %collective-permute-done.17 = bf16[64,2048]{1,0:T(8,128)(2,1)S(1)} collective-permute-done((bf16[64,2048]{1,0:T(8,128)(2,1)S(1)}, bf16[64,2048]{1,0:T(8,128)(2,1)S(1)}, u32[]{:S(2)}, u32[]{:S(2)}) %collective-permute-start.17) | collective-permute-done | bytes 262176 | tf_op jit(solution)/shard_map/ppermute | solution.py:382
  145.0 6.1 %collective-permute-start.32 = (bf16[64,2048]{1,0:T(8,128)(2,1)S(1)}, bf16[64,2048]{1,0:T(8,128)(2,1)S(1)}, u32[]{:S(2)}, u32[]{:S(2)}) collective-permute-start(bf16[64,2048]{1,0:T(8,128)(2,1)S(1)} %add_convert_fusion), channel_id=1, source_target_pairs={{0,96},{4,100},{8,104},{12,108},{16,112},{20,116},{24,120},{28,124... | collective-permute-start | bytes 786440 | tf_op jit(solution)/shard_map/ppermute | solution.py:382
  152.1 3.1 %collective-permute-start.23 = (bf16[64,2048]{1,0:T(8,128)(2,1)S(1)}, bf16[64,2048]{1,0:T(8,128)(2,1)S(1)}, u32[]{:S(2)}, u32[]{:S(2)}) collective-permute-start(bf16[64,2048]{1,0:T(8,128)(2,1)S(1)} %add_convert_fusion.2), channel_id=1, source_target_pairs={{0,24},{4,28},{8,0},{12,4},{16,8},{20,12},{24,16},{28,20},{32,56},... | collective-permute-start | bytes 786440 | tf_op jit(solution)/shard_map/ppermute | solution.py:382
  159.3 2.8 %collective-permute-done.18 = bf16[64,2048]{1,0:T(8,128)(2,1)S(1)} collective-permute-done((bf16[64,2048]{1,0:T(8,128)(2,1)S(1)}, bf16[64,2048]{1,0:T(8,128)(2,1)S(1)}, u32[]{:S(2)}, u32[]{:S(2)}) %collective-permute-start.18) | collective-permute-done | bytes 262176 | tf_op jit(solution)/shard_map/ppermute | solution.py:382
  165.9 2.0 %collective-permute-done.20.refs_1_ = bf16[32,2048]{1,0:T(8,128)(2,1)S(1)} collective-permute-done((bf16[32,2048]{1,0:T(8,128)(2,1)S(1)}, bf16[32,2048]{1,0:T(8,128)(2,1)S(1)}, u32[]{:S(2)}, u32[]{:S(2)}) %collective-permute-start.20) | collective-permute-done | bytes 131104 | tf_op jit(solution)/shard_map/ppermute | solution.py:382
  167.9 4.1 %collective-permute-done.24.refs_2_ = bf16[32,2048]{1,0:T(8,128)(2,1)S(1)} collective-permute-done((bf16[32,2048]{1,0:T(8,128)(2,1)S(1)}, bf16[32,2048]{1,0:T(8,128)(2,1)S(1)}, u32[]{:S(2)}, u32[]{:S(2)}) %collective-permute-start.24) | collective-permute-done | bytes 131104 | tf_op jit(solution)/shard_map/ppermute | solution.py:382
  172.7 5.3 %last.1 = bf16[4096,128]{1,0:T(8,128)(2,1)} custom-call(s32[2]{0:T(128)} %pad_add_fusion.place, s32[128]{0:T(128)} %owner.3, s32[128]{0:T(128)} %dlen.3, f32[2,4,4]{2,1,0:T(4,128)} %hc_res.3, f32[2,4]{1,0:T(2,128)} %hc_out.3, bf16[4,64,2048]{2,1,0:T(8,128)(2,1)} %get-tuple-element.22.first, bf16[32,2048]{1,0:T(8,128)(2,1)} %get-tuple-element.51.refs_0_, ...), custom_call_target="tpu_custom_call" | custom-call | tf_op jit(solution)/shard_map/last/pallas_call | solution.py:308
  (130 shorter events, 40.0 us)
Async XLA Ops:
  28.8 19.9 %all-to-all-start = ((bf16[4,64,2048]{2,1,0:T(8,128)(2,1)}), bf16[4,64,2048]{2,1,0:T(8,128)(2,1)}, u32[]{:S(2)}, u32[]{:S(2)}) async-start(bf16[4,64,2048]{2,1,0:T(8,128)(2,1)} %get-tuple-element.21), calls=%async_computation | async-start | bytes 2097152 | tf_op jit(solution)/shard_map/all_to_all | solution.py:436
  33.5 65.8 %collective-permute-start.6 = (bf16[2048,256]{1,0:T(8,128)(2,1)S(1)}, bf16[2048,256]{1,0:T(8,128)(2,1)}, u32[]{:S(2)}, u32[]{:S(2)}) collective-permute-start(bf16[2048,256]{1,0:T(8,128)(2,1)S(1)} %copy-done), channel_id=1, source_target_pairs={{0,4},{4,0},{8,12},{12,8},{16,20},{20,16},{24,28},{28,24},{32,36},... | collective-permute-start | bytes 3145736 | tf_op jit(solution)/shard_map/ppermute | solution.py:386
  33.5 65.9 %collective-permute-start.7 = (bf16[2048,256]{1,0:T(8,128)(2,1)S(1)}, bf16[2048,256]{1,0:T(8,128)(2,1)}, u32[]{:S(2)}, u32[]{:S(2)}) collective-permute-start(bf16[2048,256]{1,0:T(8,128)(2,1)S(1)} %copy-done.1), channel_id=1, source_target_pairs={{0,4},{4,0},{8,12},{12,8},{16,20},{20,16},{24,28},{28,24},{32,36},... | collective-permute-start | bytes 3145736 | tf_op jit(solution)/shard_map/ppermute | solution.py:386
  59.6 8.1 %collective-permute-start.5 = (bf16[32,2048]{1,0:T(8,128)(2,1)}, bf16[32,2048]{1,0:T(8,128)(2,1)S(1)}, u32[]{:S(2)}, u32[]{:S(2)}) collective-permute-start(bf16[32,2048]{1,0:T(8,128)(2,1)} %get-tuple-element.24), channel_id=1, source_target_pairs={{0,16},{4,20},{8,24},{12,28},{16,0},{20,4},{24,8},{28,12},{32,48},... | collective-permute-start | bytes 393224 | tf_op jit(solution)/shard_map/ppermute | solution.py:382
  67.7 8.8 %collective-permute-start.2 = (bf16[32,2048]{1,0:T(8,128)(2,1)}, bf16[32,2048]{1,0:T(8,128)(2,1)S(1)}, u32[]{:S(2)}, u32[]{:S(2)}) collective-permute-start(bf16[32,2048]{1,0:T(8,128)(2,1)} %get-tuple-element.23), channel_id=1, source_target_pairs={{0,64},{4,68},{8,72},{12,76},{16,80},{20,84},{24,88},{28,92},{32,9... | collective-permute-start | bytes 393224 | tf_op jit(solution)/shard_map/ppermute | solution.py:382
  71.0 12.9 %collective-permute-start.11 = (bf16[128,2048]{1,0:T(8,128)(2,1)S(1)}, bf16[128,2048]{1,0:T(8,128)(2,1)S(1)}, u32[]{:S(2)}, u32[]{:S(2)}) collective-permute-start(bf16[128,2048]{1,0:T(8,128)(2,1)S(1)} %constant_dynamic-update-slice_fusion.4.refs_1_), channel_id=1, source_target_pairs={{0,32},{4,36},{8,40},{12,44},{16,48},{20,52},{24,56},{28,60},{32,6... | collective-permute-start | bytes 1572872 | tf_op jit(solution)/shard_map/ppermute | solution.py:382
  72.4 11.8 %collective-permute-start.12 = (bf16[128,2048]{1,0:T(8,128)(2,1)S(1)}, bf16[128,2048]{1,0:T(8,128)(2,1)S(1)}, u32[]{:S(2)}, u32[]{:S(2)}) collective-permute-start(bf16[128,2048]{1,0:T(8,128)(2,1)S(1)} %constant_dynamic-update-slice_fusion.4.refs_1_), channel_id=1, source_target_pairs={{0,96},{4,100},{8,104},{12,108},{16,112},{20,116},{24,120},{28,124... | collective-permute-start | bytes 1572872 | tf_op jit(solution)/shard_map/ppermute | solution.py:382
  76.5 26.2 %collective-permute-start.8 = (bf16[256,2048]{1,0:T(8,128)(2,1)S(1)}, bf16[256,2048]{1,0:T(8,128)(2,1)S(1)}, u32[]{:S(2)}, u32[]{:S(2)}) collective-permute-start(bf16[256,2048]{1,0:T(8,128)(2,1)S(1)} %copy-done.2), channel_id=1, source_target_pairs={{0,4},{4,0},{8,12},{12,8},{16,20},{20,16},{24,28},{28,24},{32,36},... | collective-permute-start | bytes 3145736 | tf_op jit(solution)/shard_map/ppermute | solution.py:386
  83.9 11.9 %collective-permute-start.9 = (bf16[128,2048]{1,0:T(8,128)(2,1)S(1)}, bf16[128,2048]{1,0:T(8,128)(2,1)S(1)}, u32[]{:S(2)}, u32[]{:S(2)}) collective-permute-start(bf16[128,2048]{1,0:T(8,128)(2,1)S(1)} %constant_dynamic-update-slice_fusion.refs_0_), channel_id=1, source_target_pairs={{0,8},{4,12},{8,16},{12,20},{16,24},{20,28},{24,0},{28,4},{32,40},... | collective-permute-start | bytes 1572872 | tf_op jit(solution)/shard_map/ppermute | solution.py:382
  84.2 12.6 %collective-permute-start.10 = (bf16[128,2048]{1,0:T(8,128)(2,1)S(1)}, bf16[128,2048]{1,0:T(8,128)(2,1)S(1)}, u32[]{:S(2)}, u32[]{:S(2)}) collective-permute-start(bf16[128,2048]{1,0:T(8,128)(2,1)S(1)} %constant_dynamic-update-slice_fusion.refs_0_), channel_id=1, source_target_pairs={{0,24},{4,28},{8,0},{12,4},{16,8},{20,12},{24,16},{28,20},{32,56},... | collective-permute-start | bytes 1572872 | tf_op jit(solution)/shard_map/ppermute | solution.py:382
  95.8 16.2 %collective-permute-start.15 = (bf16[64,2048]{1,0:T(8,128)(2,1)S(1)}, bf16[64,2048]{1,0:T(8,128)(2,1)S(1)}, u32[]{:S(2)}, u32[]{:S(2)}) collective-permute-start(bf16[64,2048]{1,0:T(8,128)(2,1)S(1)} %slice.67), channel_id=1, source_target_pairs={{0,32},{4,36},{8,40},{12,44},{16,48},{20,52},{24,56},{28,60},{32,6... | collective-permute-start | bytes 786440 | tf_op jit(solution)/shard_map/ppermute | solution.py:382
  96.8 15.2 %collective-permute-start.16 = (bf16[64,2048]{1,0:T(8,128)(2,1)S(1)}, bf16[64,2048]{1,0:T(8,128)(2,1)S(1)}, u32[]{:S(2)}, u32[]{:S(2)}) collective-permute-start(bf16[64,2048]{1,0:T(8,128)(2,1)S(1)} %slice.68), channel_id=1, source_target_pairs={{0,96},{4,100},{8,104},{12,108},{16,112},{20,116},{24,120},{28,124... | collective-permute-start | bytes 786440 | tf_op jit(solution)/shard_map/ppermute | solution.py:382
  99.3 12.6 %collective-permute-start.13 = (bf16[64,2048]{1,0:T(8,128)(2,1)S(1)}, bf16[64,2048]{1,0:T(8,128)(2,1)S(1)}, u32[]{:S(2)}, u32[]{:S(2)}) collective-permute-start(bf16[64,2048]{1,0:T(8,128)(2,1)S(1)} %slice.65), channel_id=1, source_target_pairs={{0,8},{4,12},{8,16},{12,20},{16,24},{20,28},{24,0},{28,4},{32,40},... | collective-permute-start | bytes 786440 | tf_op jit(solution)/shard_map/ppermute | solution.py:382
  99.4 12.6 %collective-permute-start.14 = (bf16[64,2048]{1,0:T(8,128)(2,1)S(1)}, bf16[64,2048]{1,0:T(8,128)(2,1)S(1)}, u32[]{:S(2)}, u32[]{:S(2)}) collective-permute-start(bf16[64,2048]{1,0:T(8,128)(2,1)S(1)} %slice.66), channel_id=1, source_target_pairs={{0,24},{4,28},{8,0},{12,4},{16,8},{20,12},{24,16},{28,20},{32,56},... | collective-permute-start | bytes 786440 | tf_op jit(solution)/shard_map/ppermute | solution.py:382
  119.5 15.2 %collective-permute-start.26 = (bf16[64,2048]{1,0:T(8,128)(2,1)}, bf16[64,2048]{1,0:T(8,128)(2,1)S(1)}, u32[]{:S(2)}, u32[]{:S(2)}) collective-permute-start(bf16[64,2048]{1,0:T(8,128)(2,1)} %get-tuple-element.34), channel_id=1, source_target_pairs={{0,32},{4,36},{8,40},{12,44},{16,48},{20,52},{24,56},{28,60},{32,6... | collective-permute-start | bytes 786440 | tf_op jit(solution)/shard_map/ppermute | solution.py:382
  127.7 23.4 %collective-permute-start.28 = (bf16[64,2048]{1,0:T(8,128)(2,1)}, bf16[64,2048]{1,0:T(8,128)(2,1)S(1)}, u32[]{:S(2)}, u32[]{:S(2)}) collective-permute-start(bf16[64,2048]{1,0:T(8,128)(2,1)} %get-tuple-element.35), channel_id=1, source_target_pairs={{0,96},{4,100},{8,104},{12,108},{16,112},{20,116},{24,120},{28,124... | collective-permute-start | bytes 786440 | tf_op jit(solution)/shard_map/ppermute | solution.py:382
  131.0 21.0 %collective-permute-start.30 = (bf16[64,2048]{1,0:T(8,128)(2,1)}, bf16[64,2048]{1,0:T(8,128)(2,1)S(1)}, u32[]{:S(2)}, u32[]{:S(2)}) collective-permute-start(bf16[64,2048]{1,0:T(8,128)(2,1)} %get-tuple-element.36), channel_id=1, source_target_pairs={{0,32},{4,36},{8,40},{12,44},{16,48},{20,52},{24,56},{28,60},{32,6... | collective-permute-start | bytes 786440 | tf_op jit(solution)/shard_map/ppermute | solution.py:382
  131.0 26.5 %collective-permute-start.19 = (bf16[64,2048]{1,0:T(8,128)(2,1)}, bf16[64,2048]{1,0:T(8,128)(2,1)S(1)}, u32[]{:S(2)}, u32[]{:S(2)}) collective-permute-start(bf16[64,2048]{1,0:T(8,128)(2,1)} %get-tuple-element.28), channel_id=1, source_target_pairs={{0,24},{4,28},{8,0},{12,4},{16,8},{20,12},{24,16},{28,20},{32,56},... | collective-permute-start | bytes 786440 | tf_op jit(solution)/shard_map/ppermute | solution.py:382
  142.4 9.7 %collective-permute-start.27 = (bf16[64,2048]{1,0:T(8,128)(2,1)S(1)}, bf16[64,2048]{1,0:T(8,128)(2,1)S(1)}, u32[]{:S(2)}, u32[]{:S(2)}) collective-permute-start(bf16[64,2048]{1,0:T(8,128)(2,1)S(1)} %add_convert_fusion.1), channel_id=1, source_target_pairs={{0,32},{4,36},{8,40},{12,44},{16,48},{20,52},{24,56},{28,60},{32,6... | collective-permute-start | bytes 786440 | tf_op jit(solution)/shard_map/ppermute | solution.py:382
  145.0 11.0 %collective-permute-start.32 = (bf16[64,2048]{1,0:T(8,128)(2,1)S(1)}, bf16[64,2048]{1,0:T(8,128)(2,1)S(1)}, u32[]{:S(2)}, u32[]{:S(2)}) collective-permute-start(bf16[64,2048]{1,0:T(8,128)(2,1)S(1)} %add_convert_fusion), channel_id=1, source_target_pairs={{0,96},{4,100},{8,104},{12,108},{16,112},{20,116},{24,120},{28,124... | collective-permute-start | bytes 786440 | tf_op jit(solution)/shard_map/ppermute | solution.py:382
  152.0 10.1 %collective-permute-start.18 = (bf16[64,2048]{1,0:T(8,128)(2,1)S(1)}, bf16[64,2048]{1,0:T(8,128)(2,1)S(1)}, u32[]{:S(2)}, u32[]{:S(2)}) collective-permute-start(bf16[64,2048]{1,0:T(8,128)(2,1)S(1)} %add_convert_fusion.3), channel_id=1, source_target_pairs={{0,8},{4,12},{8,16},{12,20},{16,24},{20,28},{24,0},{28,4},{32,40},... | collective-permute-start | bytes 786440 | tf_op jit(solution)/shard_map/ppermute | solution.py:382
  152.1 10.0 %collective-permute-start.23 = (bf16[64,2048]{1,0:T(8,128)(2,1)S(1)}, bf16[64,2048]{1,0:T(8,128)(2,1)S(1)}, u32[]{:S(2)}, u32[]{:S(2)}) collective-permute-start(bf16[64,2048]{1,0:T(8,128)(2,1)S(1)} %add_convert_fusion.2), channel_id=1, source_target_pairs={{0,24},{4,28},{8,0},{12,4},{16,8},{20,12},{24,16},{28,20},{32,56},... | collective-permute-start | bytes 786440 | tf_op jit(solution)/shard_map/ppermute | solution.py:382
  156.9 8.2 %collective-permute-start.29 = (bf16[32,2048]{1,0:T(8,128)(2,1)S(1)}, bf16[32,2048]{1,0:T(8,128)(2,1)S(1)}, u32[]{:S(2)}, u32[]{:S(2)}) collective-permute-start(bf16[32,2048]{1,0:T(8,128)(2,1)S(1)} %get-tuple-element.46), channel_id=1, source_target_pairs={{0,24},{4,28},{8,0},{12,4},{16,8},{20,12},{24,16},{28,20},{32,56},... | collective-permute-start | bytes 393224 | tf_op jit(solution)/shard_map/ppermute | solution.py:382
  157.4 8.5 %collective-permute-start.33 = (bf16[32,2048]{1,0:T(8,128)(2,1)S(1)}, bf16[32,2048]{1,0:T(8,128)(2,1)S(1)}, u32[]{:S(2)}, u32[]{:S(2)}) collective-permute-start(bf16[32,2048]{1,0:T(8,128)(2,1)S(1)} %get-tuple-element.45), channel_id=1, source_target_pairs={{0,8},{4,12},{8,16},{12,20},{16,24},{20,28},{24,0},{28,4},{32,40},... | collective-permute-start | bytes 393224 | tf_op jit(solution)/shard_map/ppermute | solution.py:382
  (37 other events, 363.7 us)

commit v2 on v1

--- a/solution.py
+++ b/solution.py
@@ -19,6 +19,11 @@
 SCALE = HD ** (-0.5)
 BF = jnp.bfloat16
 F32 = jnp.float32
+BLOCKS = 8
+PACKED = 3072
+OFFSETS = ((1, 1), (-1, -1), (1, -1), (-1, 1), (2, 0), (0, 2), (2, 2))
+MEMBERS = len(OFFSETS) + 1
+FIRST = 4
 NT = (((1,), (1,)), ((), ()))
 
 
@@ -207,8 +212,7 @@
     )(place, owner, dlen, clen, pick, hc_in, parents, freq, st, wq, wk, wv, ck, cv, wo)
 
 
-def mid_kernel(place, hc_in, hc_res, hc_out, parts, st, first, rows_a, rows_b, raw, xbuf):
-    i = pl.program_id(0)
+def mid_kernel(place, hc_in, hc_res, hc_out, parts, st, first, rows, raw, xbuf):
     raw[...] = st[...].astype(F32)
     for j in range(LT):
         lanes = slice(j * 128, (j + 1) * 128)
@@ -226,27 +230,17 @@
             t = hc_in[1, m] * c.astype(F32)
             x = t if x is None else x + t
         xbuf[:, lanes] = x
-    normed = normalize(xbuf[...]).astype(BF)
-
-    @pl.when(i < 2)
-    def _():
-        rows_a[...] = normed
-
-    @pl.when(i >= 2)
-    def _():
-        rows_b[...] = normed
+    rows[...] = normalize(xbuf[...]).astype(BF)
 
 
 def mid(place, hc_in, hc_res, hc_out, parts, st):
     smem = pl.BlockSpec(memory_space=pltpu.SMEM)
-    half = SLOTS * Q // 2
     return pl.pallas_call(
         mid_kernel,
         name="mid",
         out_shape=(
             jax.ShapeDtypeStruct((NS, SLOTS * Q, D), BF),
-            jax.ShapeDtypeStruct((half, D), BF),
-            jax.ShapeDtypeStruct((half, D), BF),
+            jax.ShapeDtypeStruct((SLOTS * Q, D), BF),
         ),
         grid_spec=pltpu.PrefetchScalarGridSpec(
             num_scalar_prefetch=1,
@@ -260,8 +254,7 @@
             ],
             out_specs=[
                 pl.BlockSpec((NS, Q, D), lambda i, p: (0, i, 0)),
-                pl.BlockSpec((Q, D), lambda i, p: (jnp.minimum(i, 1), 0)),
-                pl.BlockSpec((Q, D), lambda i, p: (jnp.maximum(i - 2, 0), 0)),
+                pl.BlockSpec((Q, D), lambda i, p: (i, 0)),
             ],
             scratch_shapes=[pltpu.VMEM((1024, 128), F32), pltpu.VMEM((Q, D), F32)],
         ),
@@ -269,29 +262,16 @@
 
 
 def last_kernel(place, owner, dlen, hc_res, hc_out, first, *refs):
-    parts_a, parts_b, out, raw, mlp_s = refs[:4], refs[4:8], refs[8], refs[9], refs[10]
+    parts, out, raw = refs[:MEMBERS], refs[MEMBERS], refs[MEMBERS + 1]
     i = pl.program_id(0)
-
-    @pl.when(i < 2)
-    def _():
-        t = parts_a[0][...].astype(F32)
-        for p in parts_a[1:]:
-            t = t + p[...].astype(F32)
-        mlp_s[...] = t
-
-    @pl.when(i >= 2)
-    def _():
-        t = parts_b[0][...].astype(F32)
-        for p in parts_b[1:]:
-            t = t + p[...].astype(F32)
-        mlp_s[...] = t
-
     count = dlen[owner[place[0] * SLOTS + i]]
     spot = place[1] * Q + lax.broadcasted_iota(jnp.int32, (Q, 128), 0)
     alive = spot < count
     for j in range(LT):
         lanes = slice(j * 128, (j + 1) * 128)
-        mlp = mlp_s[:, lanes]
+        mlp = parts[0][:, lanes].astype(F32)
+        for p in parts[1:]:
+            mlp = mlp + p[:, lanes].astype(F32)
         f = [first[n, :, lanes].astype(F32) for n in range(NS)]
         for m in range(NS):
             c = hc_out[1, m] * mlp
@@ -301,10 +281,8 @@
     out[...] = raw[...].astype(BF)
 
 
-def last(place, owner, dlen, hc_res, hc_out, first, parts_a, parts_b):
+def last(place, owner, dlen, hc_res, hc_out, first, parts):
     smem = pl.BlockSpec(memory_space=pltpu.SMEM)
-    a_spec = pl.BlockSpec((Q, D), lambda i, *_: (jnp.minimum(i, 1), 0))
-    b_spec = pl.BlockSpec((Q, D), lambda i, *_: (jnp.maximum(i - 2, 0), 0))
     return pl.pallas_call(
         last_kernel,
         name="last",
@@ -313,81 +291,110 @@
             num_scalar_prefetch=3,
             grid=(SLOTS,),
             in_specs=[smem, smem, pl.BlockSpec((NS, Q, D), lambda i, *_: (0, i, 0))]
-            + [a_spec] * 4
-            + [b_spec] * 4,
+            + [pl.BlockSpec((Q, D), lambda i, *_: (i, 0))] * MEMBERS,
             out_specs=pl.BlockSpec((1024, 128), lambda i, *_: (i, 0)),
-            scratch_shapes=[pltpu.VMEM((1024, 128), F32), pltpu.VMEM((Q, D), F32)],
-        ),
-    )(place, owner, dlen, hc_res, hc_out, first, *parts_a, *parts_b)
-
-
-def ffn_kernel(sizes, outs, *refs):
-    n = len(sizes)
-    xs, (g0, g1, u0, u1, d0, d1) = refs[:n], refs[n : n + 6]
-    ys, cat = refs[n + 6 : -1], refs[-1]
-    o = 0
-    for x, size in zip(xs, sizes):
-        cat[o : o + size, :] = x[...]
-        o += size
-    step = 256
-    done = 0
-    where = 0
-    for c in range(o // step):
-        x = cat[c * step : (c + 1) * step, :]
-        total = None
-        for g, u, d in ((g0, u0, d0), (g1, u1, d1)):
-            gate = mm(x, g[...])
-            inner = (gate / (1.0 + jnp.exp(-gate)) * mm(x, u[...])).astype(BF)
-            t = mm(inner, d[...])
-            total = t if total is None else total + t
-        total = total.astype(BF)
-        pos = 0
-        while pos < step:
-            size = outs[where]
-            ys[where][...] = total[pos : pos + size]
-            pos += size
-            where += 1
-
-
-def ffn(xs, weights, outs):
-    sizes = tuple(x.shape[0] for x in xs)
+            scratch_shapes=[pltpu.VMEM((1024, 128), F32)],
+        ),
+    )(place, owner, dlen, hc_res, hc_out, first, *parts)
+
+
+def pack_kernel(g, u, d, one, two):
+    for k, w in enumerate((one, two)):
+        lanes = slice(k * 128, (k + 1) * 128)
+        w[0:512, 0:128] = g[:, lanes]
+        w[0:512, 128:256] = u[:, lanes]
+        w[512:640, :] = d[lanes, 0:256]
+        w[640:768, :] = d[lanes, 256:512]
+
+
+def pack(g, u, d):
+    tall = pl.BlockSpec((512, 256), lambda j: (j, 0))
+    packed = pl.BlockSpec((768, 256), lambda j: (j, 0))
+    return pl.pallas_call(
+        pack_kernel,
+        name="pack",
+        grid=(4,),
+        out_shape=(jax.ShapeDtypeStruct((PACKED, 256), BF),) * 2,
+        in_specs=[tall, tall, pl.BlockSpec((256, 512), lambda j: (0, j))],
+        out_specs=(packed, packed),
+    )(g, u, d)
+
+
+def ffn_kernel(n, *refs):
+    xs, ws, ys = refs[:n], refs[n : n + BLOCKS], refs[n + BLOCKS : 2 * n + BLOCKS]
+    cat, wbuf, inner, sems = refs[2 * n + BLOCKS :]
+    rows = SLOTS * Q
+    arrive = [
+        pltpu.make_async_copy(x, cat.at[pl.ds(k * rows, rows), :], sems.at[BLOCKS + k])
+        for k, x in enumerate(xs)
+    ]
+    copies = [pltpu.make_async_copy(w, wbuf.at[k], sems.at[k]) for k, w in enumerate(ws)]
+    for c in arrive + copies:
+        c.start()
+    for c in arrive:
+        c.wait()
+    for k in range(BLOCKS):
+        copies[k].wait()
+        both = None
+        for j in range(4):
+            t = mm(cat[:, 512 * j : 512 * (j + 1)], wbuf[k, 768 * j : 768 * j + 512, :])
+            both = t if both is None else both + t
+        gate = both[:, :128]
+        inner[:, k * 128 : (k + 1) * 128] = (gate / (1.0 + jnp.exp(-gate)) * both[:, 128:]).astype(
+            BF
+        )
+    h = inner[...]
+    for c in range(8):
+        at = 768 * (c // 2) + 512 + 128 * (c % 2)
+        down = jnp.concatenate([wbuf[k, at : at + 128, :] for k in range(BLOCKS)], axis=0)
+        t = mm(h, down).astype(BF)
+        for k in range(n):
+            ys[k][:, 256 * c : 256 * (c + 1)] = t[k * rows : (k + 1) * rows]
+
+
+def ffn(xs, weights):
+    n = len(xs)
     vmem = pl.BlockSpec(memory_space=pltpu.VMEM)
-    rows = sum(sizes)
+    rows = n * SLOTS * Q
     return pl.pallas_call(
-        functools.partial(ffn_kernel, sizes, outs),
+        functools.partial(ffn_kernel, n),
         name="ffn",
-        out_shape=tuple(jax.ShapeDtypeStruct((o, D), BF) for o in outs),
-        in_specs=[vmem] * (len(xs) + 6),
-        out_specs=tuple([vmem] * len(outs)),
-        scratch_shapes=[pltpu.VMEM((rows, D), BF)],
+        out_shape=tuple(jax.ShapeDtypeStruct((SLOTS * Q, D), BF) for _ in xs),
+        in_specs=[pl.BlockSpec(memory_space=pl.ANY)] * (n + BLOCKS),
+        out_specs=tuple([vmem] * n),
+        scratch_shapes=[
+            pltpu.VMEM((rows, D), BF),
+            pltpu.VMEM((BLOCKS, PACKED, 256), BF),
+            pltpu.VMEM((rows, 128 * BLOCKS), BF),
+            pltpu.SemaphoreType.DMA((BLOCKS + n,)),
+        ],
         cost_estimate=pl.CostEstimate(
-            flops=rows * D * 512 * 6, transcendentals=rows * 512, bytes_accessed=rows * D * 4
+            flops=rows * D * 1024 * 6, transcendentals=rows * 1024, bytes_accessed=rows * D * 4
         ),
         compiler_params=pltpu.CompilerParams(vmem_limit_bytes=56 * 2**20),
     )(*xs, *weights)
 
 
-def shift_pairs(axis, step):
-    pairs = []
+def pairs(move):
+    out = []
     for x in range(4):
         for z in range(4):
             for c in range(2):
-                tx = (x + step) % 4 if axis == "x" else x
-                tz = (z + step) % 4 if axis == "z" else z
-                pairs.append((x * 8 + z * 2 + c, tx * 8 + tz * 2 + c))
-    return pairs
-
-
-def shift(v, axis, step):
-    return lax.ppermute(v, "req", shift_pairs(axis, step))
-
-
-def swap_core(v):
-    return lax.ppermute(v, "req", [(i, i ^ 1) for i in range(32)])
-
-
-def add(a, b):
-    return (a.astype(F32) + b.astype(F32)).astype(BF)
+                tx, tz, tc = move(x, z, c)
+                out.append((x * 8 + z * 2 + c, (tx % 4) * 8 + (tz % 4) * 2 + tc))
+    return out
+
+
+def send(v, move):
+    return lax.ppermute(v, "req", pairs(move))
+
+
+def shift(v, dx, dz):
+    return send(v, lambda x, z, c: (x + dx, z + dz, c))
+
+
+def other_core(v):
+    return send(v, lambda x, z, c: (x, z, 1 - c))
 
 
 def body(
@@ -415,7 +422,10 @@
     freq = np.power(10000.0, -(half * 2.0 / HD)).astype(np.float32)
     freq = jnp.asarray(np.concatenate([freq, freq])[None, :])
     st = streams.reshape(SLOTS, DRAFT, NS, LT, 128).transpose(0, 1, 3, 2, 4).reshape(-1, 128)
-    weights = (w_gate, swap_core(w_gate), w_up, swap_core(w_up), w_down, swap_core(w_down))
+    one, two = pack(w_gate, w_up, w_down)
+    one_z = send(one, lambda x, z, c: (x, z ^ 1, c))
+    two_x = send(two, lambda x, z, c: (x ^ 1, z, c))
+    weights = (one, two, other_core(one), other_core(two))
     part, kv = front(
         place,
         slot_owner,
@@ -433,54 +443,15 @@
         cache_values,
         w_output,
     )
+    part, one_z, two_x = lax.optimization_barrier((part, one_z, two_x))
     parts = lax.all_to_all(part, "head", 0, 0, tiled=False)
-    first, rows_a, rows_b = mid(place, hc_in, hc_res, hc_out, parts, st)
-
-    order = (("x", "z", rows_a), ("z", "x", rows_b))
-    own4 = []
-    for one, two, rows in order:
-        own4.append(
-            jnp.concatenate(
-                [rows, shift(rows, one, 1), shift(rows, one, -1), shift(rows, one, 2)], axis=0
-            )
-        )
-    near = []
-    for (one, two, _), x in zip(order, own4):
-        near.append((shift(x, two, 1), shift(x, two, -1)))
-    far = []
-    for (one, two, _), (l, r) in zip(order, near):
-        far.append((shift(l[:64], two, 1), shift(r[64:], two, -1)))
-
-    own_out = ffn(own4, weights, (128, 128))
-    near_out = ffn([near[0][0], near[0][1], near[1][0], near[1][1]], weights, (64,) * 8)
-    far_out = ffn([far[0][0], far[0][1], far[1][0], far[1][1]], weights, (64,) * 4)
-
-    back = []
-    for k, (one, two, _) in enumerate(order):
-        l0, l1, r0, r1 = near_out[4 * k : 4 * k + 4]
-        o0, o1 = far_out[2 * k : 2 * k + 2]
-        u1 = shift(r1, two, 1)
-        u2 = shift(l0, two, -1)
-        t1 = shift(o0, two, 1)
-        t2 = shift(o1, two, -1)
-        v1 = shift(add(r0, t1), two, 1)
-        v2 = shift(add(l1, t2), two, -1)
-        s = own_out[k].astype(F32)
-        upper = s[:64] + v1.astype(F32) + u2.astype(F32)
-        lower = s[64:] + u1.astype(F32) + v2.astype(F32)
-        back.append((upper.astype(BF), lower.astype(BF)))
-    ends = []
-    for k, (one, two, _) in enumerate(order):
-        upper, lower = back[k]
-        ends.append(
-            (
-                upper[:32],
-                shift(upper[32:], one, -1),
-                shift(lower[:32], one, 1),
-                shift(lower[32:], one, 2),
-            )
-        )
-    final = last(place, slot_owner, draft_len, hc_res, hc_out, first, ends[0], ends[1])
+    weights = weights + (one_z, two_x, other_core(one_z), other_core(two_x))
+    parts, weights = lax.optimization_barrier((parts, weights))
+    first, rows = mid(place, hc_in, hc_res, hc_out, parts, st)
+    pieces = [rows] + [shift(rows, dx, dz) for dx, dz in OFFSETS]
+    sums = ffn(pieces[:FIRST], weights) + ffn(pieces[FIRST:], weights)
+    back = [sums[0]] + [shift(t, -dx, -dz) for t, (dx, dz) in zip(sums[1:], OFFSETS)]
+    final = last(place, slot_owner, draft_len, hc_res, hc_out, first, back)
     new_streams = (
         final.reshape(SLOTS, Q, LT, NS, 128).transpose(0, 1, 3, 2, 4).reshape(SLOTS, Q, NS, D)
     )

time: 179 us -> 147 us (0.82)
  starting transfers between devices: 55.3 us -> 39.9 us
  waiting for transfers between devices: 50 us -> 41.8 us
  other arithmetic: 6.4 us -> 0.67 us
  local copies, waits for them, and re-layouts: 8.07 us -> 2.82 us
  Pallas kernels: 57.2 us -> 60.8 us
    ppermute x35 -> x20, starting transfers between devices: 50.7 us -> 35.4 us  [send(): return lax.ppermute(v, 'req', pairs(move))]
    ppermute x35 -> x20, waiting for transfers between devices: 35.3 us -> 26.4 us  [send(): return lax.ppermute(v, 'req', pairs(move))]
    convert_element_type x8 -> x0, other arithmetic: 5.76 us -> none  [the longest x4 3.1 us: add(): return (a.astype(F32) + b.astype(F32)).astype(BF)]
    unnamed x57 -> x35, local copies, waits for them, and re-layouts: 6.6 us -> 2.82 us
    pallas_call x3, Pallas kernels: 20.1 us -> 23.3 us  [the longest x2 19 us: ffn(): pl.pallas_call(functools.partial(ffn_kernel, n), name='ffn', out_shape=tu...]
  transfers between devices with their start and end apart: 36 -> 21, of which waited for: 15 -> 9; matrix products, arithmetic and copies ran while one was open for 5% -> 1% of each run, Pallas kernels for 11% -> 31%
where the time goes in v2:
time: 147 us
  Pallas kernels  60.8 us (41%)
  waiting for transfers between devices  41.8 us (28%)
  starting transfers between devices  39.9 us (27%)
  local copies, waits for them, and re-layouts  2.82 us (2%)
    ppermute x20, starting transfers between devices, send(): return lax.ppermute(v, 'req', pairs(move))  35.4 us
    ppermute x20, waiting for transfers between devices, send(): return lax.ppermute(v, 'req', pairs(move))  26.4 us
    pallas_call x1, Pallas kernels, front(): pl.pallas_call(front_kernel, name='front', out_shape=(jax.ShapeDtypeStruc...  26 us
    pallas_call x2, Pallas kernels, ffn(): pl.pallas_call(functools.partial(ffn_kernel, n), name='ffn', out_shape=tu...  19 us
    all_to_all x1, waiting for transfers between devices, body(): parts = lax.all_to_all(part, 'head', 0, 0, tiled=False)  15.4 us
    pallas_call x1, Pallas kernels, mid(): pl.pallas_call(mid_kernel, name='mid', out_shape=(jax.ShapeDtypeStruct((N...  5.72 us
    pallas_call x1, Pallas kernels, last(): pl.pallas_call(last_kernel, name='last', out_shape=jax.ShapeDtypeStruct((...  5.7 us
    all_to_all x1, starting transfers between devices, body(): parts = lax.all_to_all(part, 'head', 0, 0, tiled=False)  4.46 us
  transfers between devices with their start and end apart: 21, of which 9 were waited for; matrix products, arithmetic and copies ran while one was open for 1% of the time, Pallas kernels for 31%

profile of v2, /device:TPU:0, one launch (start us, length us, event | category | flops | bytes accessed | tf_op | source)
XLA Modules:
  0.0 146.7 jit_solution(3458494444147536350)
XLA Ops:
  0.6 4.3 %pack.1 = (bf16[3072,256]{1,0:T(8,128)(2,1)}, bf16[3072,256]{1,0:T(8,128)(2,1)}) custom-call(bf16[2048,256]{1,0:T(8,128)(2,1)} %g.1, bf16[2048,256]{1,0:T(8,128)(2,1)} %u.1, bf16[256,2048]{1,0:T(8,128)(2,1)} %d.1), custom_call_target="tpu_custom_call" | custom-call | tf_op jit(solution)/shard_map/pack/pallas_call | solution.py:313
  4.9 2.0 %collective-permute-start = (bf16[3072,256]{1,0:T(8,128)(2,1)}, bf16[3072,256]{1,0:T(8,128)(2,1)S(1)}, u32[]{:S(2)}, u32[]{:S(2)}) collective-permute-start(bf16[3072,256]{1,0:T(8,128)(2,1)} %get-tuple-element.37.refs_4_), channel_id=1, source_target_pairs={{0,8},{4,12},{8,0},{12,4},{16,24},{20,28},{24,16},{28,20},{32,40},... | collective-permute-start | bytes 4718600 | tf_op jit(solution)/shard_map/ppermute | solution.py:389
  10.3 26.0 %front.1 = (bf16[4,64,2048]{2,1,0:T(8,128)(2,1)}, bf16[2048,128]{1,0:T(8,128)(2,1)}) custom-call(s32[2]{0:T(128)} %pad_add_fusion.place, s32[128]{0:T(128)} %owner.3, s32[128]{0:T(128)} %dlen.3, s32[128]{0:T(128)} %clen.1, s32[128]{0:T(128)} %pick.1, f32[2,4]{1,0:T(2,128)} %hc_in.3, s32[128,64]{1,0:T(8,128)} %copy.22.parents, f32[1,128]{1,0:T(1,128)} %constant.11.clone.freq, ...), custom_call_target="tpu_custom_call" | custom-call | tf_op jit(solution)/shard_map/front/pallas_call | solution.py:172
  36.3 5.2 %collective-permute-done.refs_8_ = bf16[3072,256]{1,0:T(8,128)(2,1)S(1)} collective-permute-done((bf16[3072,256]{1,0:T(8,128)(2,1)}, bf16[3072,256]{1,0:T(8,128)(2,1)S(1)}, u32[]{:S(2)}, u32[]{:S(2)}) %collective-permute-start) | collective-permute-done | bytes 1572896 | tf_op jit(solution)/shard_map/ppermute | solution.py:389
  43.5 4.5 %all-to-all-start = ((bf16[4,64,2048]{2,1,0:T(8,128)(2,1)}), bf16[4,64,2048]{2,1,0:T(8,128)(2,1)}, u32[]{:S(2)}, u32[]{:S(2)}) async-start(bf16[4,64,2048]{2,1,0:T(8,128)(2,1)} %get-tuple-element.31), calls=%async_computation | async-start | bytes 2097152 | tf_op jit(solution)/shard_map/all_to_all | solution.py:447
  48.0 15.4 %all-to-all-done.parts = bf16[4,64,2048]{2,1,0:T(8,128)(2,1)} async-done(((bf16[4,64,2048]{2,1,0:T(8,128)(2,1)}), bf16[4,64,2048]{2,1,0:T(8,128)(2,1)}, u32[]{:S(2)}, u32[]{:S(2)}) %all-to-all-start) | async-done | bytes 1048608 | tf_op jit(solution)/shard_map/all_to_all | solution.py:447
  63.4 5.7 %mid.1 = (bf16[4,64,2048]{2,1,0:T(8,128)(2,1)}, bf16[64,2048]{1,0:T(8,128)(2,1)}) custom-call(s32[2]{0:T(128)} %pad_add_fusion.place, f32[2,4]{1,0:T(2,128)} %hc_in.3, f32[2,4,4]{2,1,0:T(4,128)} %hc_res.3, f32[2,4]{1,0:T(2,128)} %hc_out.3, bf16[4,64,2048]{2,1,0:T(8,128)(2,1)} %all-to-all-done.parts, bf16[16384,128]{1,0:T(8,128)(2,1)} %bitcast.18), custom_call_target="tpu_custom_call" | custom-call | tf_op jit(solution)/shard_map/mid/pallas_call | solution.py:238
  69.1 6.1 %collective-permute-start.15 = (bf16[64,2048]{1,0:T(8,128)(2,1)}, bf16[64,2048]{1,0:T(8,128)(2,1)S(1)}, u32[]{:S(2)}, u32[]{:S(2)}) collective-permute-start(bf16[64,2048]{1,0:T(8,128)(2,1)} %get-tuple-element.36.refs_0_), channel_id=1, source_target_pairs={{0,80},{4,84},{8,88},{12,92},{16,64},{20,68},{24,72},{28,76},{32,1... | collective-permute-start | bytes 786440 | tf_op jit(solution)/shard_map/ppermute | solution.py:389
  75.9 2.4 %collective-permute-start.12 = (bf16[64,2048]{1,0:T(8,128)(2,1)}, bf16[64,2048]{1,0:T(8,128)(2,1)S(1)}, u32[]{:S(2)}, u32[]{:S(2)}) collective-permute-start(bf16[64,2048]{1,0:T(8,128)(2,1)} %get-tuple-element.36.refs_0_), channel_id=1, source_target_pairs={{0,104},{4,108},{8,112},{12,116},{16,120},{20,124},{24,96},{28,100... | collective-permute-start | bytes 786440 | tf_op jit(solution)/shard_map/ppermute | solution.py:389
  78.3 1.7 %collective-permute-start.8 = (bf16[64,2048]{1,0:T(8,128)(2,1)}, bf16[64,2048]{1,0:T(8,128)(2,1)S(1)}, u32[]{:S(2)}, u32[]{:S(2)}) collective-permute-start(bf16[64,2048]{1,0:T(8,128)(2,1)} %get-tuple-element.36.refs_0_), channel_id=1, source_target_pairs={{0,56},{4,60},{8,32},{12,36},{16,40},{20,44},{24,48},{28,52},{32,8... | collective-permute-start | bytes 786440 | tf_op jit(solution)/shard_map/ppermute | solution.py:389
  80.0 2.4 %collective-permute-done.15.refs_3_ = bf16[64,2048]{1,0:T(8,128)(2,1)S(1)} collective-permute-done((bf16[64,2048]{1,0:T(8,128)(2,1)}, bf16[64,2048]{1,0:T(8,128)(2,1)S(1)}, u32[]{:S(2)}, u32[]{:S(2)}) %collective-permute-start.15) | collective-permute-done | bytes 262176 | tf_op jit(solution)/shard_map/ppermute | solution.py:389
  82.4 5.1 %collective-permute-start.7 = (bf16[64,2048]{1,0:T(8,128)(2,1)}, bf16[64,2048]{1,0:T(8,128)(2,1)S(1)}, u32[]{:S(2)}, u32[]{:S(2)}) collective-permute-start(bf16[64,2048]{1,0:T(8,128)(2,1)} %get-tuple-element.36.refs_0_), channel_id=1, source_target_pairs={{0,120},{4,124},{8,96},{12,100},{16,104},{20,108},{24,112},{28,116... | collective-permute-start | bytes 786440 | tf_op jit(solution)/shard_map/ppermute | solution.py:389
  87.5 3.2 %collective-permute-done.14.refs_2_ = bf16[64,2048]{1,0:T(8,128)(2,1)S(1)} collective-permute-done((bf16[64,2048]{1,0:T(8,128)(2,1)}, bf16[64,2048]{1,0:T(8,128)(2,1)S(1)}, u32[]{:S(2)}, u32[]{:S(2)}) %collective-permute-start.14) | collective-permute-done | bytes 262176 | tf_op jit(solution)/shard_map/ppermute | solution.py:389
  90.7 2.9 %collective-permute-done.12.refs_0_ = bf16[64,2048]{1,0:T(8,128)(2,1)S(1)} collective-permute-done((bf16[64,2048]{1,0:T(8,128)(2,1)}, bf16[64,2048]{1,0:T(8,128)(2,1)S(1)}, u32[]{:S(2)}, u32[]{:S(2)}) %collective-permute-start.12) | collective-permute-done | bytes 262176 | tf_op jit(solution)/shard_map/ppermute | solution.py:389
  94.3 9.5 %ffn.3 = (bf16[64,2048]{1,0:T(8,128)(2,1)}, bf16[64,2048]{1,0:T(8,128)(2,1)}, bf16[64,2048]{1,0:T(8,128)(2,1)}, bf16[64,2048]{1,0:T(8,128)(2,1)}) custom-call(bf16[64,2048]{1,0:T(8,128)(2,1)} %copy-done.15, bf16[64,2048]{1,0:T(8,128)(2,1)} %copy-done.14, bf16[64,2048]{1,0:T(8,128)(2,1)} %copy-done.13, bf16[64,2048]{1,0:T(8,128)(2,1)} %copy-done.12, ...), custom_call_target="tpu_custom_call" | custom-call | flops 3221225472 | bytes 2097152 | tf_op jit(solution)/shard_map/ffn/pallas_call | solution.py:359
  103.8 3.0 %collective-permute-start.16 = (bf16[64,2048]{1,0:T(8,128)(2,1)}, bf16[64,2048]{1,0:T(8,128)(2,1)S(1)}, u32[]{:S(2)}, u32[]{:S(2)}) collective-permute-start(bf16[64,2048]{1,0:T(8,128)(2,1)} %get-tuple-element.49), channel_id=1, source_target_pairs={{0,56},{4,60},{8,32},{12,36},{16,40},{20,44},{24,48},{28,52},{32,8... | collective-permute-start | bytes 786440 | tf_op jit(solution)/shard_map/ppermute | solution.py:389
  109.9 3.5 %collective-permute-start.19 = (bf16[64,2048]{1,0:T(8,128)(2,1)}, bf16[64,2048]{1,0:T(8,128)(2,1)S(1)}, u32[]{:S(2)}, u32[]{:S(2)}) collective-permute-start(bf16[64,2048]{1,0:T(8,128)(2,1)} %get-tuple-element.52), channel_id=1, source_target_pairs={{0,80},{4,84},{8,88},{12,92},{16,64},{20,68},{24,72},{28,76},{32,1... | collective-permute-start | bytes 786440 | tf_op jit(solution)/shard_map/ppermute | solution.py:389
  114.1 9.5 %ffn.2 = (bf16[64,2048]{1,0:T(8,128)(2,1)}, bf16[64,2048]{1,0:T(8,128)(2,1)}, bf16[64,2048]{1,0:T(8,128)(2,1)}, bf16[64,2048]{1,0:T(8,128)(2,1)}) custom-call(bf16[64,2048]{1,0:T(8,128)(2,1)} %get-tuple-element.36.refs_0_, bf16[64,2048]{1,0:T(8,128)(2,1)} %copy-done.11, bf16[64,2048]{1,0:T(8,128)(2,1)} %copy-done.10, bf16[64,2048]{1,0:T(8,128)(2,1)} %copy-done.9, ...), custom_call_target="tpu_custom_call" | custom-call | flops 3221225472 | bytes 2097152 | tf_op jit(solution)/shard_map/ffn/pallas_call | solution.py:359
  123.6 2.9 %collective-permute-start.9 = (bf16[64,2048]{1,0:T(8,128)(2,1)}, bf16[64,2048]{1,0:T(8,128)(2,1)S(1)}, u32[]{:S(2)}, u32[]{:S(2)}) collective-permute-start(bf16[64,2048]{1,0:T(8,128)(2,1)} %get-tuple-element.46), channel_id=1, source_target_pairs={{0,120},{4,124},{8,96},{12,100},{16,104},{20,108},{24,112},{28,116... | collective-permute-start | bytes 786440 | tf_op jit(solution)/shard_map/ppermute | solution.py:389
  126.6 2.4 %collective-permute-start.11 = (bf16[64,2048]{1,0:T(8,128)(2,1)}, bf16[64,2048]{1,0:T(8,128)(2,1)S(1)}, u32[]{:S(2)}, u32[]{:S(2)}) collective-permute-start(bf16[64,2048]{1,0:T(8,128)(2,1)} %get-tuple-element.48), channel_id=1, source_target_pairs={{0,104},{4,108},{8,112},{12,116},{16,120},{20,124},{24,96},{28,100... | collective-permute-start | bytes 786440 | tf_op jit(solution)/shard_map/ppermute | solution.py:389
  129.0 5.4 %collective-permute-done.9.refs_1_ = bf16[64,2048]{1,0:T(8,128)(2,1)S(1)} collective-permute-done((bf16[64,2048]{1,0:T(8,128)(2,1)}, bf16[64,2048]{1,0:T(8,128)(2,1)S(1)}, u32[]{:S(2)}, u32[]{:S(2)}) %collective-permute-start.9) | collective-permute-done | bytes 262176 | tf_op jit(solution)/shard_map/ppermute | solution.py:389
  134.4 4.0 %collective-permute-done.10.refs_2_ = bf16[64,2048]{1,0:T(8,128)(2,1)S(1)} collective-permute-done((bf16[64,2048]{1,0:T(8,128)(2,1)}, bf16[64,2048]{1,0:T(8,128)(2,1)S(1)}, u32[]{:S(2)}, u32[]{:S(2)}) %collective-permute-start.10) | collective-permute-done | bytes 262176 | tf_op jit(solution)/shard_map/ppermute | solution.py:389
  138.4 1.9 %collective-permute-done.11.refs_3_ = bf16[64,2048]{1,0:T(8,128)(2,1)S(1)} collective-permute-done((bf16[64,2048]{1,0:T(8,128)(2,1)}, bf16[64,2048]{1,0:T(8,128)(2,1)S(1)}, u32[]{:S(2)}, u32[]{:S(2)}) %collective-permute-start.11) | collective-permute-done | bytes 262176 | tf_op jit(solution)/shard_map/ppermute | solution.py:389
  141.0 5.7 %last.1 = bf16[4096,128]{1,0:T(8,128)(2,1)} custom-call(s32[2]{0:T(128)} %pad_add_fusion.place, s32[128]{0:T(128)} %owner.3, s32[128]{0:T(128)} %dlen.3, f32[2,4,4]{2,1,0:T(4,128)} %hc_res.3, f32[2,4]{1,0:T(2,128)} %hc_out.3, bf16[4,64,2048]{2,1,0:T(8,128)(2,1)} %get-tuple-element.35.first, bf16[64,2048]{1,0:T(8,128)(2,1)} %get-tuple-element.45.refs_0_, ...), custom_call_target="tpu_custom_call" | custom-call | tf_op jit(solution)/shard_map/last/pallas_call | solution.py:286
  (60 shorter events, 11.3 us)
Async XLA Ops:
  4.9 36.6 %collective-permute-start = (bf16[3072,256]{1,0:T(8,128)(2,1)}, bf16[3072,256]{1,0:T(8,128)(2,1)S(1)}, u32[]{:S(2)}, u32[]{:S(2)}) collective-permute-start(bf16[3072,256]{1,0:T(8,128)(2,1)} %get-tuple-element.37.refs_4_), channel_id=1, source_target_pairs={{0,8},{4,12},{8,0},{12,4},{16,24},{20,28},{24,16},{28,20},{32,40},... | collective-permute-start | bytes 4718600 | tf_op jit(solution)/shard_map/ppermute | solution.py:389
  6.9 36.1 %collective-permute-start.1 = (bf16[3072,256]{1,0:T(8,128)(2,1)}, bf16[3072,256]{1,0:T(8,128)(2,1)S(1)}, u32[]{:S(2)}, u32[]{:S(2)}) collective-permute-start(bf16[3072,256]{1,0:T(8,128)(2,1)} %get-tuple-element.38.refs_5_), channel_id=1, source_target_pairs={{0,32},{4,36},{8,40},{12,44},{16,48},{20,52},{24,56},{28,60},{32,0... | collective-permute-start | bytes 4718600 | tf_op jit(solution)/shard_map/ppermute | solution.py:389
  8.4 39.6 %collective-permute-start.2 = (bf16[3072,256]{1,0:T(8,128)(2,1)}, bf16[3072,256]{1,0:T(8,128)(2,1)}, u32[]{:S(2)}, u32[]{:S(2)}) collective-permute-start(bf16[3072,256]{1,0:T(8,128)(2,1)} %get-tuple-element.37.refs_4_), channel_id=1, source_target_pairs={{0,4},{4,0},{8,12},{12,8},{16,20},{20,16},{24,28},{28,24},{32,36},... | collective-permute-start | bytes 4718600 | tf_op jit(solution)/shard_map/ppermute | solution.py:389
  8.4 39.6 %collective-permute-start.3 = (bf16[3072,256]{1,0:T(8,128)(2,1)}, bf16[3072,256]{1,0:T(8,128)(2,1)}, u32[]{:S(2)}, u32[]{:S(2)}) collective-permute-start(bf16[3072,256]{1,0:T(8,128)(2,1)} %get-tuple-element.38.refs_5_), channel_id=1, source_target_pairs={{0,4},{4,0},{8,12},{12,8},{16,20},{20,16},{24,28},{28,24},{32,36},... | collective-permute-start | bytes 4718600 | tf_op jit(solution)/shard_map/ppermute | solution.py:389
  41.5 27.6 %copy-start = (bf16[3072,256]{1,0:T(8,128)(2,1)}, bf16[3072,256]{1,0:T(8,128)(2,1)S(1)}, u32[]{:S(2)}) copy-start(bf16[3072,256]{1,0:T(8,128)(2,1)S(1)} %collective-permute-done.refs_8_) | copy-start | bytes 4718596
  43.0 26.1 %copy-start.1 = (bf16[3072,256]{1,0:T(8,128)(2,1)}, bf16[3072,256]{1,0:T(8,128)(2,1)S(1)}, u32[]{:S(2)}) copy-start(bf16[3072,256]{1,0:T(8,128)(2,1)S(1)} %collective-permute-done.1.refs_9_) | copy-start | bytes 4718596
  43.0 20.4 %collective-permute-start.4 = (bf16[3072,256]{1,0:T(8,128)(2,1)S(1)}, bf16[3072,256]{1,0:T(8,128)(2,1)}, u32[]{:S(2)}, u32[]{:S(2)}) collective-permute-start(bf16[3072,256]{1,0:T(8,128)(2,1)S(1)} %collective-permute-done.refs_8_), channel_id=1, source_target_pairs={{0,4},{4,0},{8,12},{12,8},{16,20},{20,16},{24,28},{28,24},{32,36},... | collective-permute-start | bytes 4718600 | tf_op jit(solution)/shard_map/ppermute | solution.py:389
  43.0 20.4 %collective-permute-start.5 = (bf16[3072,256]{1,0:T(8,128)(2,1)S(1)}, bf16[3072,256]{1,0:T(8,128)(2,1)}, u32[]{:S(2)}, u32[]{:S(2)}) collective-permute-start(bf16[3072,256]{1,0:T(8,128)(2,1)S(1)} %collective-permute-done.1.refs_9_), channel_id=1, source_target_pairs={{0,4},{4,0},{8,12},{12,8},{16,20},{20,16},{24,28},{28,24},{32,36},... | collective-permute-start | bytes 4718600 | tf_op jit(solution)/shard_map/ppermute | solution.py:389
  43.5 19.9 %all-to-all-start = ((bf16[4,64,2048]{2,1,0:T(8,128)(2,1)}), bf16[4,64,2048]{2,1,0:T(8,128)(2,1)}, u32[]{:S(2)}, u32[]{:S(2)}) async-start(bf16[4,64,2048]{2,1,0:T(8,128)(2,1)} %get-tuple-element.31), calls=%async_computation | async-start | bytes 2097152 | tf_op jit(solution)/shard_map/all_to_all | solution.py:447
  69.1 13.3 %collective-permute-start.15 = (bf16[64,2048]{1,0:T(8,128)(2,1)}, bf16[64,2048]{1,0:T(8,128)(2,1)S(1)}, u32[]{:S(2)}, u32[]{:S(2)}) collective-permute-start(bf16[64,2048]{1,0:T(8,128)(2,1)} %get-tuple-element.36.refs_0_), channel_id=1, source_target_pairs={{0,80},{4,84},{8,88},{12,92},{16,64},{20,68},{24,72},{28,76},{32,1... | collective-permute-start | bytes 786440 | tf_op jit(solution)/shard_map/ppermute | solution.py:389
  75.2 15.4 %collective-permute-start.14 = (bf16[64,2048]{1,0:T(8,128)(2,1)}, bf16[64,2048]{1,0:T(8,128)(2,1)S(1)}, u32[]{:S(2)}, u32[]{:S(2)}) collective-permute-start(bf16[64,2048]{1,0:T(8,128)(2,1)} %get-tuple-element.36.refs_0_), channel_id=1, source_target_pairs={{0,16},{4,20},{8,24},{12,28},{16,0},{20,4},{24,8},{28,12},{32,48},... | collective-permute-start | bytes 786440 | tf_op jit(solution)/shard_map/ppermute | solution.py:389
  75.2 15.4 %collective-permute-start.13 = (bf16[64,2048]{1,0:T(8,128)(2,1)}, bf16[64,2048]{1,0:T(8,128)(2,1)S(1)}, u32[]{:S(2)}, u32[]{:S(2)}) collective-permute-start(bf16[64,2048]{1,0:T(8,128)(2,1)} %get-tuple-element.36.refs_0_), channel_id=1, source_target_pairs={{0,64},{4,68},{8,72},{12,76},{16,80},{20,84},{24,88},{28,92},{32,9... | collective-permute-start | bytes 786440 | tf_op jit(solution)/shard_map/ppermute | solution.py:389
  75.9 17.7 %collective-permute-start.12 = (bf16[64,2048]{1,0:T(8,128)(2,1)}, bf16[64,2048]{1,0:T(8,128)(2,1)S(1)}, u32[]{:S(2)}, u32[]{:S(2)}) collective-permute-start(bf16[64,2048]{1,0:T(8,128)(2,1)} %get-tuple-element.36.refs_0_), channel_id=1, source_target_pairs={{0,104},{4,108},{8,112},{12,116},{16,120},{20,124},{24,96},{28,100... | collective-permute-start | bytes 786440 | tf_op jit(solution)/shard_map/ppermute | solution.py:389
  78.3 30.2 %collective-permute-start.8 = (bf16[64,2048]{1,0:T(8,128)(2,1)}, bf16[64,2048]{1,0:T(8,128)(2,1)S(1)}, u32[]{:S(2)}, u32[]{:S(2)}) collective-permute-start(bf16[64,2048]{1,0:T(8,128)(2,1)} %get-tuple-element.36.refs_0_), channel_id=1, source_target_pairs={{0,56},{4,60},{8,32},{12,36},{16,40},{20,44},{24,48},{28,52},{32,8... | collective-permute-start | bytes 786440 | tf_op jit(solution)/shard_map/ppermute | solution.py:389
  82.4 27.5 %collective-permute-start.7 = (bf16[64,2048]{1,0:T(8,128)(2,1)}, bf16[64,2048]{1,0:T(8,128)(2,1)S(1)}, u32[]{:S(2)}, u32[]{:S(2)}) collective-permute-start(bf16[64,2048]{1,0:T(8,128)(2,1)} %get-tuple-element.36.refs_0_), channel_id=1, source_target_pairs={{0,120},{4,124},{8,96},{12,100},{16,104},{20,108},{24,112},{28,116... | collective-permute-start | bytes 786440 | tf_op jit(solution)/shard_map/ppermute | solution.py:389
  90.7 22.7 %collective-permute-start.6 = (bf16[64,2048]{1,0:T(8,128)(2,1)}, bf16[64,2048]{1,0:T(8,128)(2,1)S(1)}, u32[]{:S(2)}, u32[]{:S(2)}) collective-permute-start(bf16[64,2048]{1,0:T(8,128)(2,1)} %get-tuple-element.36.refs_0_), channel_id=1, source_target_pairs={{0,40},{4,44},{8,48},{12,52},{16,56},{20,60},{24,32},{28,36},{32,7... | collective-permute-start | bytes 786440 | tf_op jit(solution)/shard_map/ppermute | solution.py:389
  103.8 22.7 %collective-permute-start.16 = (bf16[64,2048]{1,0:T(8,128)(2,1)}, bf16[64,2048]{1,0:T(8,128)(2,1)S(1)}, u32[]{:S(2)}, u32[]{:S(2)}) collective-permute-start(bf16[64,2048]{1,0:T(8,128)(2,1)} %get-tuple-element.49), channel_id=1, source_target_pairs={{0,56},{4,60},{8,32},{12,36},{16,40},{20,44},{24,48},{28,52},{32,8... | collective-permute-start | bytes 786440 | tf_op jit(solution)/shard_map/ppermute | solution.py:389
  106.9 19.8 %collective-permute-start.17 = (bf16[64,2048]{1,0:T(8,128)(2,1)}, bf16[64,2048]{1,0:T(8,128)(2,1)S(1)}, u32[]{:S(2)}, u32[]{:S(2)}) collective-permute-start(bf16[64,2048]{1,0:T(8,128)(2,1)} %get-tuple-element.50), channel_id=1, source_target_pairs={{0,64},{4,68},{8,72},{12,76},{16,80},{20,84},{24,88},{28,92},{32,9... | collective-permute-start | bytes 786440 | tf_op jit(solution)/shard_map/ppermute | solution.py:389
  108.5 20.5 %collective-permute-start.18 = (bf16[64,2048]{1,0:T(8,128)(2,1)}, bf16[64,2048]{1,0:T(8,128)(2,1)S(1)}, u32[]{:S(2)}, u32[]{:S(2)}) collective-permute-start(bf16[64,2048]{1,0:T(8,128)(2,1)} %get-tuple-element.51), channel_id=1, source_target_pairs={{0,16},{4,20},{8,24},{12,28},{16,0},{20,4},{24,8},{28,12},{32,48},... | collective-permute-start | bytes 786440 | tf_op jit(solution)/shard_map/ppermute | solution.py:389
  109.9 19.1 %collective-permute-start.19 = (bf16[64,2048]{1,0:T(8,128)(2,1)}, bf16[64,2048]{1,0:T(8,128)(2,1)S(1)}, u32[]{:S(2)}, u32[]{:S(2)}) collective-permute-start(bf16[64,2048]{1,0:T(8,128)(2,1)} %get-tuple-element.52), channel_id=1, source_target_pairs={{0,80},{4,84},{8,88},{12,92},{16,64},{20,68},{24,72},{28,76},{32,1... | collective-permute-start | bytes 786440 | tf_op jit(solution)/shard_map/ppermute | solution.py:389
  123.6 10.8 %collective-permute-start.9 = (bf16[64,2048]{1,0:T(8,128)(2,1)}, bf16[64,2048]{1,0:T(8,128)(2,1)S(1)}, u32[]{:S(2)}, u32[]{:S(2)}) collective-permute-start(bf16[64,2048]{1,0:T(8,128)(2,1)} %get-tuple-element.46), channel_id=1, source_target_pairs={{0,120},{4,124},{8,96},{12,100},{16,104},{20,108},{24,112},{28,116... | collective-permute-start | bytes 786440 | tf_op jit(solution)/shard_map/ppermute | solution.py:389
  126.5 13.8 %copy-start.2 = (bf16[64,2048]{1,0:T(8,128)(2,1)}, bf16[64,2048]{1,0:T(8,128)(2,1)S(1)}, u32[]{:S(2)}) copy-start(bf16[64,2048]{1,0:T(8,128)(2,1)S(1)} %collective-permute-done.16.refs_4_) | copy-start | bytes 786436
  126.5 11.9 %collective-permute-start.10 = (bf16[64,2048]{1,0:T(8,128)(2,1)}, bf16[64,2048]{1,0:T(8,128)(2,1)S(1)}, u32[]{:S(2)}, u32[]{:S(2)}) collective-permute-start(bf16[64,2048]{1,0:T(8,128)(2,1)} %get-tuple-element.47), channel_id=1, source_target_pairs={{0,40},{4,44},{8,48},{12,52},{16,56},{20,60},{24,32},{28,36},{32,7... | collective-permute-start | bytes 786440 | tf_op jit(solution)/shard_map/ppermute | solution.py:389
  126.6 13.7 %collective-permute-start.11 = (bf16[64,2048]{1,0:T(8,128)(2,1)}, bf16[64,2048]{1,0:T(8,128)(2,1)S(1)}, u32[]{:S(2)}, u32[]{:S(2)}) collective-permute-start(bf16[64,2048]{1,0:T(8,128)(2,1)} %get-tuple-element.48), channel_id=1, source_target_pairs={{0,104},{4,108},{8,112},{12,116},{16,120},{20,124},{24,96},{28,100... | collective-permute-start | bytes 786440 | tf_op jit(solution)/shard_map/ppermute | solution.py:389
  (14 other events, 80.0 us)

commit v3 on v2

v3 whole, which is shorter than its diff:
```python
import functools

import jax
import jax.numpy as jnp
import numpy as np
from jax import lax
from jax.experimental import pallas as pl
from jax.experimental.pallas import tpu as pltpu
from jax.sharding import PartitionSpec as P

HD = 128
SLOTS = 4
DRAFT = 64
CACHE = 1024
D = 2048
NS = 4
LT = D // 128
Q = 16
SCALE = HD ** (-0.5)
BF = jnp.bfloat16
F32 = jnp.float32
BLOCKS = 8
PITCH = 72
PACKED = 3072
OFFSETS = ((1, 1), (-1, -1), (1, -1), (-1, 1), (2, 0), (0, 2), (2, 2))
MEMBERS = len(OFFSETS) + 1
FIRST = 4
CH = 4
NT = (((1,), (1,)), ((), ()))


def near(x):
    return pltpu.with_memory_space_constraint(x, pltpu.VMEM)


def mm(a, b):
    return jnp.dot(a, b, preferred_element_type=F32)


def mm_nt(a, b):
    return lax.dot_general(a, b, NT, preferred_element_type=F32)


def normalize(x):
    center = jnp.sum(x, axis=-1, keepdims=True) * (1.0 / D)
    y = x - center
    spread = jnp.sum(y * y, axis=-1, keepdims=True) * (1.0 / D)
    return y * lax.rsqrt(spread + 1e-05)


def front_kernel(
    place,
    owner,
    dlen,
    clen,
    pick,
    hc_in,
    parents,
    freq,
    st,
    wq_h,
    wk_h,
    wv_h,
    wo_h,
    ck_h,
    cv_h,
    out0,
    out1,
    out2,
    out3,
    own,
    kv_out,
    raw,
    xbuf,
    normed,
    above_s,
    take_s,
    cos_s,
    sin_s,
    att,
    acc,
    kvs,
    wq,
    wk,
    wv,
    wo,
    ck,
    cv,
    sems,
):
    i = pl.program_id(0)
    base = place[0] * SLOTS

    def loads(g):
        cols = pl.ds(g * 256, 256)
        return (
            pltpu.make_async_copy(wq_h.at[:, cols], wq.at[g], sems.at[g, 0]),
            pltpu.make_async_copy(wk_h.at[:, cols], wk.at[g], sems.at[g, 1]),
            pltpu.make_async_copy(wv_h.at[:, cols], wv.at[g], sems.at[g, 2]),
            pltpu.make_async_copy(ck_h.at[:, :, cols], ck.at[g], sems.at[g, 3]),
            pltpu.make_async_copy(cv_h.at[:, :, cols], cv.at[g], sems.at[g, 4]),
            pltpu.make_async_copy(wo_h.at[cols, :], wo.at[g], sems.at[g, 5]),
        )

    @pl.when(i == 0)
    def _():
        for c in loads(0):
            c.start()

    @pl.when(i == 1)
    def _():
        for c in loads(1):
            c.start()

    @pl.when(i == 0)
    def _():
        pi = lax.broadcasted_iota(jnp.int32, (DRAFT, DRAFT), 0)
        qi = lax.broadcasted_iota(jnp.int32, (DRAFT, DRAFT), 1)
        eye = (qi == pi).astype(F32)
        who = lax.broadcasted_iota(jnp.int32, (DRAFT, 128), 1)
        lane = lax.broadcasted_iota(jnp.int32, (DRAFT, HD), 1)
        ones = jnp.ones((8, DRAFT), BF)
        ups = []
        for s in range(SLOTS):
            r = owner[base + s]
            par = jnp.sum(jnp.where(who == r, parents[...], 0), axis=1, keepdims=True)
            ups.append(jnp.where(par == qi, 1.0, eye))
        for rounds in range(6):
            nxt = []
            for up in ups:
                b = up.astype(BF)
                nxt.append(jnp.minimum(mm(b, b), 1.0))
            ups = nxt
        for s in range(SLOTS):
            r = owner[base + s]
            above = ups[s]
            above_s[s] = above
            depth_row = mm_nt(ones, above.astype(BF))[0:1] - 1.0
            depth = jnp.sum(above, axis=1, keepdims=True) - 1.0
            a = jnp.minimum(pick[r], dlen[r] - 1)
            path = above_s[s, pl.ds(a, 1), :]
            take = jnp.where(depth_row == pi.astype(F32), path, 0.0)
            take_s[s] = take.astype(BF)
            angle = (clen[r].astype(F32) + depth) * freq[...]
            at = slice(s * DRAFT, (s + 1) * DRAFT)
            cos_s[at, :] = jnp.cos(angle)
            sine = jnp.sin(angle)
            sin_s[at, :] = jnp.where(lane < HD // 2, -sine, sine)

    @pl.when(i < SLOTS)
    def _():
        s = i
        for p in range(DRAFT):
            raw[p * PITCH : p * PITCH + 64, :] = st[p * 64 : (p + 1) * 64, :].astype(F32)
        total = None
        for j in range(LT):
            x = hc_in[0, 0] * raw[pl.ds(j * NS, DRAFT, stride=PITCH), :]
            for m in range(1, NS):
                x = x + hc_in[0, m] * raw[pl.ds(j * NS + m, DRAFT, stride=PITCH), :]
            xbuf[:, j * 128 : (j + 1) * 128] = x
            total = x if total is None else total + x
        for j in range(LT):
            for n in range(NS):
                own[n, pl.ds(pl.multiple_of(s * Q, Q), Q), j * 128 : (j + 1) * 128] = raw[
                    pl.ds(place[1] * (Q * PITCH) + j * NS + n, Q, stride=PITCH), :
                ].astype(BF)
        center = jnp.sum(total, axis=-1, keepdims=True) * (1.0 / D)
        y = xbuf[...] - center
        spread = jnp.sum(y * y, axis=-1, keepdims=True) * (1.0 / D)
        normed[pl.ds(pl.multiple_of(s * DRAFT, DRAFT), DRAFT), :] = (
            y * lax.rsqrt(spread + 1e-05)
        ).astype(BF)

    def heads(g):
        arrive = loads(g)
        for c in arrive[:3]:
            c.wait()
        x = normed[...]
        q2 = mm(x, wq[g])
        k2 = mm(x, wk[g])
        v2 = mm(x, wv[g]).astype(BF)
        cosine = cos_s[...]
        sine = sin_s[...]
        col = lax.broadcasted_iota(jnp.int32, (DRAFT, CACHE), 1)
        for c in arrive[3:]:
            c.wait()
        for hh in range(2):
            cols = slice(hh * HD, (hh + 1) * HD)
            qh = q2[:, cols]
            kh = k2[:, cols]
            qh = (qh * cosine + pltpu.roll(qh, HD // 2, 1) * sine).astype(BF)
            kh = (kh * cosine + pltpu.roll(kh, HD // 2, 1) * sine).astype(BF)
            vh = v2[:, cols]
            for s in range(SLOTS):
                at = slice(s * DRAFT, (s + 1) * DRAFT)
                length = clen[owner[base + s]]
                qs, ks, vs = qh[at], kh[at], vh[at]
                sc = mm_nt(qs, ck[g, s, :, cols]) * SCALE
                sc = jnp.where(col < length, sc, -1e30)
                lo = mm_nt(qs, ks) * SCALE
                lo = jnp.where(above_s[s] > 0.5, lo, -1e30)
                top = jnp.maximum(
                    jnp.max(sc, axis=-1, keepdims=True), jnp.max(lo, axis=-1, keepdims=True)
                )
                e1 = jnp.exp(sc - top)
                e2 = jnp.exp(lo - top)
                total = jnp.sum(e1, axis=-1, keepdims=True) + jnp.sum(e2, axis=-1, keepdims=True)
                inv = 1.0 / total
                w1 = (e1 * inv).astype(BF)
                w2 = (e2 * inv).astype(BF)
                o = mm(w1, cv[g, s, :, cols]) + mm(w2, vs)
                att[at, cols] = o.astype(BF)
                tk = take_s[s]
                h = g * 2 + hh
                kvs[s, pl.ds(h * 2, DRAFT, stride=8), :] = mm(tk, ks)
                kvs[s, pl.ds(h * 2 + 1, DRAFT, stride=8), :] = mm(tk, vs)
        part = mm(att[...], wo[g])
        if g == 0:
            acc[...] = part
        else:
            acc[...] = acc[...] + part
            for s in range(SLOTS):
                for k, out in enumerate((out0, out1, out2, out3)):
                    from_row = s * DRAFT + lax.rem(place[1] + k, 4) * Q
                    out[s * Q : (s + 1) * Q, :] = acc[
                        pl.ds(pl.multiple_of(from_row, Q), Q), :
                    ].astype(BF)
                kv_out[s * 512 : (s + 1) * 512, :] = kvs[s].astype(BF)

    @pl.when(i == SLOTS - 1)
    def _():
        heads(0)
        heads(1)


def front(place, owner, dlen, clen, pick, hc_in, parents, freq, st, wq, wk, wv, ck, cv, wo):
    smem = pl.BlockSpec(memory_space=pltpu.SMEM)
    vmem = pl.BlockSpec(memory_space=pltpu.VMEM)
    return pl.pallas_call(
        front_kernel,
        name="front",
        out_shape=(pltpu.VMEM((SLOTS * Q, D), BF),) * 4
        + (
            pltpu.VMEM((NS, SLOTS * Q, D), BF),
            jax.ShapeDtypeStruct((2048, 128), BF),
        ),
        grid_spec=pltpu.PrefetchScalarGridSpec(
            num_scalar_prefetch=5,
            grid=(SLOTS,),
            in_specs=[
                smem,
                pl.BlockSpec((DRAFT, 128), lambda i, *_: (0, 0)),
                pl.BlockSpec((1, HD), lambda i, *_: (0, 0)),
                pl.BlockSpec((4096, 128), lambda i, *_: (i, 0)),
            ]
            + [pl.BlockSpec(memory_space=pltpu.HBM)] * 6,
            out_specs=[vmem] * 5 + [pl.BlockSpec((2048, 128), lambda i, *_: (0, 0))],
            scratch_shapes=[
                pltpu.VMEM((DRAFT * PITCH, 128), F32),
                pltpu.VMEM((DRAFT, D), F32),
                pltpu.VMEM((SLOTS * DRAFT, D), BF),
                pltpu.VMEM((SLOTS, DRAFT, DRAFT), F32),
                pltpu.VMEM((SLOTS, DRAFT, DRAFT), BF),
                pltpu.VMEM((SLOTS * DRAFT, HD), F32),
                pltpu.VMEM((SLOTS * DRAFT, HD), F32),
                pltpu.VMEM((SLOTS * DRAFT, 256), BF),
                pltpu.VMEM((SLOTS * DRAFT, D), F32),
                pltpu.VMEM((SLOTS, 512, 128), F32),
                pltpu.VMEM((2, D, 256), BF),
                pltpu.VMEM((2, D, 256), BF),
                pltpu.VMEM((2, D, 256), BF),
                pltpu.VMEM((2, 256, D), BF),
                pltpu.VMEM((2, SLOTS, CACHE, 256), BF),
                pltpu.VMEM((2, SLOTS, CACHE, 256), BF),
                pltpu.SemaphoreType.DMA((2, 6)),
            ],
        ),
        compiler_params=pltpu.CompilerParams(vmem_limit_bytes=36 * 2**20),
    )(
        place,
        owner,
        dlen,
        clen,
        pick,
        hc_in,
        parents,
        freq,
        pltpu.with_memory_space_constraint(st, pltpu.HBM),
        *[pltpu.with_memory_space_constraint(x, pltpu.HBM) for x in (wq, wk, wv, wo, ck, cv)],
    )


def mid_kernel(hc_in, hc_res, hc_out, p0, p1, p2, p3, own, first, rows, xbuf):
    for s in range(SLOTS):
        at = slice(s * Q, (s + 1) * Q)
        total = None
        for j in range(LT):
            lanes = slice(j * 128, (j + 1) * 128)
            attn = p0[at, lanes].astype(F32)
            for p in (p1, p2, p3):
                attn = attn + p[at, lanes].astype(F32)
            mine = [own[n, at, lanes].astype(F32) for n in range(NS)]
            x = None
            for m in range(NS):
                c = hc_out[0, m] * attn
                for n in range(NS):
                    c = c + hc_res[0, n, m] * mine[n]
                c = c.astype(BF)
                first[m, at, lanes] = c
                t = hc_in[1, m] * c.astype(F32)
                x = t if x is None else x + t
            xbuf[at, lanes] = x
            total = x if total is None else total + x
        center = jnp.sum(total, axis=-1, keepdims=True) * (1.0 / D)
        y = xbuf[at, :] - center
        spread = jnp.sum(y * y, axis=-1, keepdims=True) * (1.0 / D)
        rows[at, :] = (y * lax.rsqrt(spread + 1e-05)).astype(BF)


def mid(hc_in, hc_res, hc_out, parts, own):
    smem = pl.BlockSpec(memory_space=pltpu.SMEM)
    vmem = pl.BlockSpec(memory_space=pltpu.VMEM)
    return pl.pallas_call(
        mid_kernel,
        name="mid",
        out_shape=(pltpu.VMEM((NS, SLOTS * Q, D), BF), pltpu.VMEM((SLOTS * Q, D), BF)),
        in_specs=[smem] * 3 + [vmem] * 5,
        out_specs=(vmem, vmem),
        scratch_shapes=[pltpu.VMEM((SLOTS * Q, D), F32)],
        compiler_params=pltpu.CompilerParams(vmem_limit_bytes=8 * 2**20),
    )(hc_in, hc_res, hc_out, *[near(p) for p in parts], near(own))


def last_kernel(place, owner, dlen, hc_res, hc_out, first, *refs):
    parts, out, raw = refs[:MEMBERS], refs[MEMBERS], refs[MEMBERS + 1]
    spot = place[1] * Q + lax.broadcasted_iota(jnp.int32, (Q, 128), 0)
    for s in range(SLOTS):
        at = slice(s * Q, (s + 1) * Q)
        alive = spot < dlen[owner[place[0] * SLOTS + s]]
        for j in range(LT):
            lanes = slice(j * 128, (j + 1) * 128)
            mlp = parts[0][at, lanes].astype(F32)
            for p in parts[1:]:
                mlp = mlp + p[at, lanes].astype(F32)
            f = [first[n, at, lanes].astype(F32) for n in range(NS)]
            for m in range(NS):
                c = hc_out[1, m] * mlp
                for n in range(NS):
                    c = c + hc_res[1, n, m] * f[n]
                raw[pl.ds(j * NS + m, Q, stride=PITCH), :] = jnp.where(alive, c, 0.0)
        for p in range(Q):
            out[(s * Q + p) * 64 : (s * Q + p + 1) * 64, :] = raw[
                p * PITCH : p * PITCH + 64, :
            ].astype(BF)


def last(place, owner, dlen, hc_res, hc_out, first, parts):
    smem = pl.BlockSpec(memory_space=pltpu.SMEM)
    vmem = pl.BlockSpec(memory_space=pltpu.VMEM)
    return pl.pallas_call(
        last_kernel,
        name="last",
        out_shape=jax.ShapeDtypeStruct((SLOTS * 1024, 128), BF),
        in_specs=[smem] * 5 + [vmem] * (1 + MEMBERS),
        out_specs=vmem,
        scratch_shapes=[pltpu.VMEM((Q * PITCH, 128), F32)],
        compiler_params=pltpu.CompilerParams(vmem_limit_bytes=8 * 2**20),
    )(place, owner, dlen, hc_res, hc_out, near(first), *[near(p) for p in parts])


def pack_kernel(g, u, d, one, two, buf, sems):
    ins, outs = [], []
    for k, w in enumerate((one, two)):
        part = pl.ds(k * 128, 128)
        here = buf.at[k]
        ins.append(
            [
                pltpu.make_async_copy(
                    g.at[:, part], here.at[pl.ds(0, D), pl.ds(0, 128)], sems.at[k, 0]
                ),
                pltpu.make_async_copy(
                    u.at[:, part], here.at[pl.ds(0, D), pl.ds(128, 128)], sems.at[k, 1]
                ),
            ]
            + [
                pltpu.make_async_copy(
                    d.at[part, pl.ds(256 * c, 256)],
                    here.at[pl.ds(D + 128 * c, 128), :],
                    sems.at[k, 2 + c],
                )
                for c in range(8)
            ]
        )
        outs.append(pltpu.make_async_copy(here, w, sems.at[k, 10]))
    for k in range(2):
        for c in ins[k]:
            c.start()
    for k in range(2):
        for c in ins[k]:
            c.wait()
        outs[k].start()
    for k in range(2):
        outs[k].wait()


def pack(g, u, d):
    hbm = pl.BlockSpec(memory_space=pltpu.HBM)
    return pl.pallas_call(
        pack_kernel,
        name="pack",
        out_shape=(jax.ShapeDtypeStruct((PACKED, 256), BF),) * 2,
        in_specs=[hbm] * 3,
        out_specs=(hbm, hbm),
        scratch_shapes=[pltpu.VMEM((2, PACKED, 256), BF), pltpu.SemaphoreType.DMA((2, 11))],
    )(*[pltpu.with_memory_space_constraint(x, pltpu.HBM) for x in (g, u, d)])


def ffn_kernel(n, *refs):
    xs, ws, ys = refs[:n], refs[n : n + BLOCKS], refs[n + BLOCKS : 2 * n + BLOCKS]
    cat, inner = refs[2 * n + BLOCKS :]
    rows = SLOTS * Q
    for k, x in enumerate(xs):
        cat[k * rows : (k + 1) * rows, :] = x[...]
    step = CH * rows
    spans = [(o, min(o + step, n * rows)) for o in range(0, n * rows, step)]
    for lo, hi in spans:
        for k, w in enumerate(ws):
            both = mm(cat[lo:hi, :], w[:D, :])
            gate = both[:, :128]
            inner[lo:hi, k * 128 : (k + 1) * 128] = (
                gate / (1.0 + jnp.exp(-gate)) * both[:, 128:]
            ).astype(BF)
        for c in range(8):
            at = D + 128 * c
            down = jnp.concatenate([w[at : at + 128, :] for w in ws], axis=0)
            t = mm(inner[lo:hi, :], down).astype(BF)
            for k in range(lo // rows, hi // rows):
                ys[k][:, 256 * c : 256 * (c + 1)] = t[k * rows - lo : (k + 1) * rows - lo]


def ffn(xs, weights):
    n = len(xs)
    vmem = pl.BlockSpec(memory_space=pltpu.VMEM)
    rows = n * SLOTS * Q
    return pl.pallas_call(
        functools.partial(ffn_kernel, n),
        name="ffn",
        out_shape=tuple(pltpu.VMEM((SLOTS * Q, D), BF) for _ in xs),
        in_specs=[vmem] * (n + BLOCKS),
        out_specs=tuple([vmem] * n),
        scratch_shapes=[
            pltpu.VMEM((rows, D), BF),
            pltpu.VMEM((rows, 128 * BLOCKS), BF),
        ],
        cost_estimate=pl.CostEstimate(
            flops=rows * D * 1024 * 6, transcendentals=rows * 1024, bytes_accessed=rows * D * 4
        ),
        compiler_params=pltpu.CompilerParams(vmem_limit_bytes=24 * 2**20),
    )(*[near(x) for x in xs], *[near(w) for w in weights])


def pairs(move):
    out = []
    for x in range(4):
        for z in range(4):
            for c in range(2):
                tx, tz, tc = move(x, z, c)
                out.append((x * 8 + z * 2 + c, (tx % 4) * 8 + (tz % 4) * 2 + tc))
    return out


def send(v, move):
    return lax.ppermute(v, "req", pairs(move))


def shift(v, dx, dz):
    return send(v, lambda x, z, c: (x + dx, z + dz, c))


def other_core(v):
    return send(v, lambda x, z, c: (x, z, 1 - c))


def body(
    streams,
    w_query,
    w_key,
    w_value,
    w_output,
    w_gate,
    w_up,
    w_down,
    cache_keys,
    cache_values,
    hc_in,
    hc_res,
    hc_out,
    parents,
    draft_len,
    cache_len,
    accept_pick,
    slot_owner,
):
    place = jnp.stack([lax.axis_index("req"), lax.axis_index("head")]).astype(jnp.int32)
    half = np.arange(64, dtype=np.float64)
    freq = np.power(10000.0, -(half * 2.0 / HD)).astype(np.float32)
    freq = jnp.asarray(np.concatenate([freq, freq])[None, :])
    st = streams.reshape(SLOTS, DRAFT, NS, LT, 128).transpose(0, 1, 3, 2, 4).reshape(-1, 128)
    one, two = pack(w_gate, w_up, w_down)
    one_z = send(one, lambda x, z, c: (x, z ^ 1, c))
    two_x = send(two, lambda x, z, c: (x ^ 1, z, c))
    weights = (one, two, other_core(one), other_core(two))
    *out, own, kv = front(
        place,
        slot_owner,
        draft_len,
        cache_len,
        accept_pick,
        hc_in,
        parents.T,
        freq,
        st,
        w_query,
        w_key,
        w_value,
        cache_keys,
        cache_values,
        w_output,
    )
    parts = [out[0]] + [
        lax.ppermute(out[k], "head", [(y, (y + k) % 4) for y in range(4)]) for k in (1, 3, 2)
    ]
    parts, one_z, two_x = lax.optimization_barrier((parts, one_z, two_x))
    weights = weights + (one_z, two_x, other_core(one_z), other_core(two_x))
    first, rows = mid(hc_in, hc_res, hc_out, [parts[0], parts[1], parts[3], parts[2]], own)
    rows, weights = lax.optimization_barrier((rows, weights))
    pieces = [rows] + [shift(rows, dx, dz) for dx, dz in OFFSETS]
    sums = ffn(pieces[:FIRST], weights) + ffn(pieces[FIRST:], weights)
    back = [sums[0]] + [shift(t, -dx, -dz) for t, (dx, dz) in zip(sums[1:], OFFSETS)]
    final = last(place, slot_owner, draft_len, hc_res, hc_out, first, back)
    new_streams = (
        final.reshape(SLOTS, Q, LT, NS, 128).transpose(0, 1, 3, 2, 4).reshape(SLOTS, Q, NS, D)
    )
    accepted_kv = (
        kv.reshape(SLOTS, DRAFT, 4, 2, 128).transpose(0, 1, 3, 2, 4).reshape(SLOTS, DRAFT, 2, 512)
    )
    return (new_streams, accepted_kv)


def solution(mesh):
    placed = (
        P("req", None, None, None),
        P(None, "head"),
        P(None, "head"),
        P(None, "head"),
        P("head", None),
        P(None, "req"),
        P(None, "req"),
        P("req", None),
        P("req", None, "head"),
        P("req", None, "head"),
        P(),
        P(),
        P(),
        P(),
        P(),
        P(),
        P(),
        P(),
    )
    return jax.shard_map(
        body,
        mesh=mesh,
        in_specs=placed,
        out_specs=(P("req", "head", None, None), P("req", None, None, "head")),
        check_vma=False,
    )
```

time: 147 us -> 125 us (0.85); the launches traced: 147 us -> 123 us
  Pallas kernels: 60.8 us -> 36.7 us
  waiting for transfers between devices: 41.8 us -> 45.3 us
  local copies, waits for them, and re-layouts: 2.82 us -> 0.05 us
    all_to_all x1 -> x0, waiting for transfers between devices: 15.4 us -> none  [body(): parts = lax.all_to_all(part, 'head', 0, 0, tiled=False)]
    pallas_call x2, Pallas kernels: 19 us -> 6.87 us  [ffn(): pl.pallas_call(functools.partial(ffn_kernel, n), name='ffn', out_shape=tu...]
    ppermute x0 -> x3, waiting for transfers between devices: none -> 10.3 us  [body(): lax.ppermute(out[k], 'head', [(y, (y + k) % 4) for y in range(4)])]
    pallas_call x3, Pallas kernels: 36 us -> 27 us  [the longest x1 21.8 us: front(): pl.pallas_call(front_kernel, name='front', out_shape=(pltpu.VMEM((SLOTS *...]
    ppermute x20, waiting for transfers between devices: 26.4 us -> 34.9 us  [send(): return lax.ppermute(v, 'req', pairs(move))]
    ppermute x0 -> x3, starting transfers between devices: none -> 5.29 us  [body(): lax.ppermute(out[k], 'head', [(y, (y + k) % 4) for y in range(4)])]
    all_to_all x1 -> x0, starting transfers between devices: 4.46 us -> none  [body(): parts = lax.all_to_all(part, 'head', 0, 0, tiled=False)]
    pallas_call x1, Pallas kernels: 5.7 us -> 2.88 us  [last(): pl.pallas_call(last_kernel, name='last', out_shape=jax.ShapeDtypeStruct((...]
  transfers between devices with their start and end apart: 21 -> 23, of which waited for: 9 -> 11; matrix products, arithmetic and copies ran while one was open for 1% -> 0% of each run, Pallas kernels for 31% -> 25%
where the time goes in v3:
time: 125 us; the launch traced here: 123 us
  waiting for transfers between devices  45.3 us (36%)
  starting transfers between devices  40.2 us (32%)
  Pallas kernels  36.7 us (29%)
    ppermute x20, waiting for transfers between devices, send(): return lax.ppermute(v, 'req', pairs(move))  34.9 us
    ppermute x20, starting transfers between devices, send(): return lax.ppermute(v, 'req', pairs(move))  34.9 us
    pallas_call x1, Pallas kernels, front(): pl.pallas_call(front_kernel, name='front', out_shape=(pltpu.VMEM((SLOTS *...  21.8 us
    ppermute x3, waiting for transfers between devices, body(): lax.ppermute(out[k], 'head', [(y, (y + k) % 4) for y in range(4)])  10.3 us
    pallas_call x2, Pallas kernels, ffn(): pl.pallas_call(functools.partial(ffn_kernel, n), name='ffn', out_shape=tu...  6.87 us
    ppermute x3, starting transfers between devices, body(): lax.ppermute(out[k], 'head', [(y, (y + k) % 4) for y in range(4)])  5.29 us
    pallas_call x1, Pallas kernels, pack(): pl.pallas_call(pack_kernel, name='pack', out_shape=(jax.ShapeDtypeStruct(...  3.17 us
    pallas_call x1, Pallas kernels, last(): pl.pallas_call(last_kernel, name='last', out_shape=jax.ShapeDtypeStruct((...  2.88 us
  transfers between devices with their start and end apart: 23, of which 11 were waited for; matrix products, arithmetic and copies ran while one was open for 0% of the time, Pallas kernels for 25%

profile of v3, /device:TPU:0, one launch (start us, length us, event | category | flops | bytes accessed | tf_op | source)
XLA Modules:
  0.0 123.2 jit_solution(4172046929406359832)
XLA Ops:
  0.7 3.2 %pack.1 = (bf16[3072,256]{1,0:T(8,128)(2,1)}, bf16[3072,256]{1,0:T(8,128)(2,1)}) custom-call(bf16[2048,256]{1,0:T(8,128)(2,1)} %g.1, bf16[2048,256]{1,0:T(8,128)(2,1)} %u.1, bf16[256,2048]{1,0:T(8,128)(2,1)} %d.1), custom_call_target="tpu_custom_call" | custom-call | tf_op jit(solution)/shard_map/pack/pallas_call | solution.py:408
  3.9 2.1 %collective-permute-start.3 = (bf16[3072,256]{1,0:T(8,128)(2,1)}, bf16[3072,256]{1,0:T(8,128)(2,1)S(1)}, u32[]{:S(2)}, u32[]{:S(2)}) collective-permute-start(bf16[3072,256]{1,0:T(8,128)(2,1)} %get-tuple-element.51.refs_4_), channel_id=1, source_target_pairs={{0,8},{4,12},{8,0},{12,4},{16,24},{20,28},{24,16},{28,20},{32,40},... | collective-permute-start | bytes 4718600 | tf_op jit(solution)/shard_map/ppermute | solution.py:473
  7.6 21.8 %front.1 = (bf16[64,2048]{1,0:T(8,128)(2,1)S(1)}, bf16[64,2048]{1,0:T(8,128)(2,1)S(1)}, bf16[64,2048]{1,0:T(8,128)(2,1)S(1)}, bf16[64,2048]{1,0:T(8,128)(2,1)S(1...) custom-call(s32[2]{0:T(128)S(1)} %pad_add_fusion.place, s32[128]{0:T(128)S(1)} %copy-done.6, ...), custom_call_target="tpu_custom_call" | custom-call | tf_op jit(solution)/shard_map/front/pallas_call | solution.py:239
  32.7 2.0 %collective-permute-start.2 = (bf16[64,2048]{1,0:T(8,128)(2,1)S(1)}, bf16[64,2048]{1,0:T(8,128)(2,1)S(1)}, u32[]{:S(2)}, u32[]{:S(2)}) collective-permute-start(bf16[64,2048]{1,0:T(8,128)(2,1)S(1)} %get-tuple-element.38), channel_id=1, source_target_pairs={{0,2},{1,3},{2,0},{3,1},{4,6},{5,7},{6,4},{7,5},{8,10},{9,11},{10,... | collective-permute-start | bytes 786440 | tf_op jit(solution)/shard_map/ppermute | solution.py:531
  34.7 4.1 %collective-permute-done.p1 = bf16[64,2048]{1,0:T(8,128)(2,1)S(1)} collective-permute-done((bf16[64,2048]{1,0:T(8,128)(2,1)S(1)}, bf16[64,2048]{1,0:T(8,128)(2,1)S(1)}, u32[]{:S(2)}, u32[]{:S(2)}) %collective-permute-start) | collective-permute-done | bytes 262176 | tf_op jit(solution)/shard_map/ppermute | solution.py:531
  38.9 4.4 %collective-permute-done.1.p3 = bf16[64,2048]{1,0:T(8,128)(2,1)S(1)} collective-permute-done((bf16[64,2048]{1,0:T(8,128)(2,1)S(1)}, bf16[64,2048]{1,0:T(8,128)(2,1)S(1)}, u32[]{:S(2)}, u32[]{:S(2)}) %collective-permute-start.1) | collective-permute-done | bytes 262176 | tf_op jit(solution)/shard_map/ppermute | solution.py:531
  45.6 2.0 %mid.1 = (bf16[4,64,2048]{2,1,0:T(8,128)(2,1)S(1)}, bf16[64,2048]{1,0:T(8,128)(2,1)S(1)}) custom-call(f32[2,4]{1,0:T(2,128)S(1)} %copy-done.4, f32[2,4,4]{2,1,0:T(4,128)S(1)} %copy-done.3, f32[2,4]{1,0:T(2,128)S(1)} %copy-done.5, bf16[64,2048]{1,0:T(8,128)(2,1)S(1)} %get-tuple-element.41.p0, bf16[64,2048]{1,0:T(8,128)(2,1)S(1)} %collective-permute-done.p1, ...), custom_call_target="tpu_custom_call" | custom-call | tf_op jit(solution)/shard_map/mid/pallas_call | solution.py:323
  48.9 2.2 %collective-permute-done.8.refs_11_ = bf16[3072,256]{1,0:T(8,128)(2,1)S(1)} collective-permute-done((bf16[3072,256]{1,0:T(8,128)(2,1)S(1)}, bf16[3072,256]{1,0:T(8,128)(2,1)S(1)}, u32[]{:S(2)}, u32[]{:S(2)}) %collective-permute-start.8) | collective-permute-done | bytes 1572896 | tf_op jit(solution)/shard_map/ppermute | solution.py:473
  51.2 5.8 %collective-permute-start.18 = (bf16[64,2048]{1,0:T(8,128)(2,1)S(1)}, bf16[64,2048]{1,0:T(8,128)(2,1)S(1)}, u32[]{:S(2)}, u32[]{:S(2)}) collective-permute-start(bf16[64,2048]{1,0:T(8,128)(2,1)S(1)} %get-tuple-element.50.refs_0_), channel_id=1, source_target_pairs={{0,80},{4,84},{8,88},{12,92},{16,64},{20,68},{24,72},{28,76},{32,1... | collective-permute-start | bytes 786440 | tf_op jit(solution)/shard_map/ppermute | solution.py:473
  57.7 1.8 %collective-permute-start.15 = (bf16[64,2048]{1,0:T(8,128)(2,1)S(1)}, bf16[64,2048]{1,0:T(8,128)(2,1)S(1)}, u32[]{:S(2)}, u32[]{:S(2)}) collective-permute-start(bf16[64,2048]{1,0:T(8,128)(2,1)S(1)} %get-tuple-element.50.refs_0_), channel_id=1, source_target_pairs={{0,104},{4,108},{8,112},{12,116},{16,120},{20,124},{24,96},{28,100... | collective-permute-start | bytes 786440 | tf_op jit(solution)/shard_map/ppermute | solution.py:473
  59.6 2.3 %collective-permute-start.11 = (bf16[64,2048]{1,0:T(8,128)(2,1)S(1)}, bf16[64,2048]{1,0:T(8,128)(2,1)S(1)}, u32[]{:S(2)}, u32[]{:S(2)}) collective-permute-start(bf16[64,2048]{1,0:T(8,128)(2,1)S(1)} %get-tuple-element.50.refs_0_), channel_id=1, source_target_pairs={{0,56},{4,60},{8,32},{12,36},{16,40},{20,44},{24,48},{28,52},{32,8... | collective-permute-start | bytes 786440 | tf_op jit(solution)/shard_map/ppermute | solution.py:473
  61.9 1.8 %collective-permute-done.18.refs_3_ = bf16[64,2048]{1,0:T(8,128)(2,1)S(1)} collective-permute-done((bf16[64,2048]{1,0:T(8,128)(2,1)S(1)}, bf16[64,2048]{1,0:T(8,128)(2,1)S(1)}, u32[]{:S(2)}, u32[]{:S(2)}) %collective-permute-start.18) | collective-permute-done | bytes 262176 | tf_op jit(solution)/shard_map/ppermute | solution.py:473
  63.7 4.7 %collective-permute-start.10 = (bf16[64,2048]{1,0:T(8,128)(2,1)S(1)}, bf16[64,2048]{1,0:T(8,128)(2,1)S(1)}, u32[]{:S(2)}, u32[]{:S(2)}) collective-permute-start(bf16[64,2048]{1,0:T(8,128)(2,1)S(1)} %get-tuple-element.50.refs_0_), channel_id=1, source_target_pairs={{0,120},{4,124},{8,96},{12,100},{16,104},{20,108},{24,112},{28,116... | collective-permute-start | bytes 786440 | tf_op jit(solution)/shard_map/ppermute | solution.py:473
  68.4 6.1 %collective-permute-done.17.refs_2_ = bf16[64,2048]{1,0:T(8,128)(2,1)S(1)} collective-permute-done((bf16[64,2048]{1,0:T(8,128)(2,1)S(1)}, bf16[64,2048]{1,0:T(8,128)(2,1)S(1)}, u32[]{:S(2)}, u32[]{:S(2)}) %collective-permute-start.17) | collective-permute-done | bytes 262176 | tf_op jit(solution)/shard_map/ppermute | solution.py:473
  75.0 3.4 %ffn.3 = (bf16[64,2048]{1,0:T(8,128)(2,1)S(1)}, bf16[64,2048]{1,0:T(8,128)(2,1)S(1)}, bf16[64,2048]{1,0:T(8,128)(2,1)S(1)}, bf16[64,2048]{1,0:T(8,128)(2,1)S(1)}) custom-call(bf16[64,2048]{1,0:T(8,128)(2,1)S(1)} %collective-permute-done.15.refs_0_, bf16[64,2048]{1,0:T(8,128)(2,1)S(1)} %collective-permute-done.16.refs_1_, ...), custom_call_target="tpu_custom_call" | custom-call | flops 3221225472 | bytes 2097152 | tf_op jit(solution)/shard_map/ffn/pallas_call | solution.py:445
  78.5 4.5 %collective-permute-start.19 = (bf16[64,2048]{1,0:T(8,128)(2,1)S(1)}, bf16[64,2048]{1,0:T(8,128)(2,1)S(1)}, u32[]{:S(2)}, u32[]{:S(2)}) collective-permute-start(bf16[64,2048]{1,0:T(8,128)(2,1)S(1)} %get-tuple-element.63), channel_id=1, source_target_pairs={{0,56},{4,60},{8,32},{12,36},{16,40},{20,44},{24,48},{28,52},{32,8... | collective-permute-start | bytes 786440 | tf_op jit(solution)/shard_map/ppermute | solution.py:473
  83.0 1.8 %collective-permute-start.20 = (bf16[64,2048]{1,0:T(8,128)(2,1)S(1)}, bf16[64,2048]{1,0:T(8,128)(2,1)S(1)}, u32[]{:S(2)}, u32[]{:S(2)}) collective-permute-start(bf16[64,2048]{1,0:T(8,128)(2,1)S(1)} %get-tuple-element.64), channel_id=1, source_target_pairs={{0,64},{4,68},{8,72},{12,76},{16,80},{20,84},{24,88},{28,92},{32,9... | collective-permute-start | bytes 786440 | tf_op jit(solution)/shard_map/ppermute | solution.py:473
  84.8 2.1 %collective-permute-start.21 = (bf16[64,2048]{1,0:T(8,128)(2,1)S(1)}, bf16[64,2048]{1,0:T(8,128)(2,1)S(1)}, u32[]{:S(2)}, u32[]{:S(2)}) collective-permute-start(bf16[64,2048]{1,0:T(8,128)(2,1)S(1)} %get-tuple-element.65), channel_id=1, source_target_pairs={{0,16},{4,20},{8,24},{12,28},{16,0},{20,4},{24,8},{28,12},{32,48},... | collective-permute-start | bytes 786440 | tf_op jit(solution)/shard_map/ppermute | solution.py:473
  87.0 2.6 %collective-permute-start.22 = (bf16[64,2048]{1,0:T(8,128)(2,1)S(1)}, bf16[64,2048]{1,0:T(8,128)(2,1)S(1)}, u32[]{:S(2)}, u32[]{:S(2)}) collective-permute-start(bf16[64,2048]{1,0:T(8,128)(2,1)S(1)} %get-tuple-element.66), channel_id=1, source_target_pairs={{0,80},{4,84},{8,88},{12,92},{16,64},{20,68},{24,72},{28,76},{32,1... | collective-permute-start | bytes 786440 | tf_op jit(solution)/shard_map/ppermute | solution.py:473
  89.5 3.4 %ffn.2 = (bf16[64,2048]{1,0:T(8,128)(2,1)S(1)}, bf16[64,2048]{1,0:T(8,128)(2,1)S(1)}, bf16[64,2048]{1,0:T(8,128)(2,1)S(1)}, bf16[64,2048]{1,0:T(8,128)(2,1)S(1)}) custom-call(bf16[64,2048]{1,0:T(8,128)(2,1)S(1)} %get-tuple-element.50.refs_0_, bf16[64,2048]{1,0:T(8,128)(2,1)S(1)} %collective-permute-done.9.refs_1_, ...), custom_call_target="tpu_custom_call" | custom-call | flops 3221225472 | bytes 2097152 | tf_op jit(solution)/shard_map/ffn/pallas_call | solution.py:445
  94.6 12.8 %collective-permute-done.19.refs_4_ = bf16[64,2048]{1,0:T(8,128)(2,1)S(1)} collective-permute-done((bf16[64,2048]{1,0:T(8,128)(2,1)S(1)}, bf16[64,2048]{1,0:T(8,128)(2,1)S(1)}, u32[]{:S(2)}, u32[]{:S(2)}) %collective-permute-start.19) | collective-permute-done | bytes 262176 | tf_op jit(solution)/shard_map/ppermute | solution.py:473
  107.4 2.7 %collective-permute-start.14 = (bf16[64,2048]{1,0:T(8,128)(2,1)S(1)}, bf16[64,2048]{1,0:T(8,128)(2,1)S(1)}, u32[]{:S(2)}, u32[]{:S(2)}) collective-permute-start(bf16[64,2048]{1,0:T(8,128)(2,1)S(1)} %get-tuple-element.62), channel_id=1, source_target_pairs={{0,104},{4,108},{8,112},{12,116},{16,120},{20,124},{24,96},{28,100... | collective-permute-start | bytes 786440 | tf_op jit(solution)/shard_map/ppermute | solution.py:473
  110.1 9.7 %collective-permute-done.13.refs_2_ = bf16[64,2048]{1,0:T(8,128)(2,1)S(1)} collective-permute-done((bf16[64,2048]{1,0:T(8,128)(2,1)S(1)}, bf16[64,2048]{1,0:T(8,128)(2,1)S(1)}, u32[]{:S(2)}, u32[]{:S(2)}) %collective-permute-start.13) | collective-permute-done | bytes 262176 | tf_op jit(solution)/shard_map/ppermute | solution.py:473
  120.3 2.9 %last.1 = bf16[4096,128]{1,0:T(8,128)(2,1)} custom-call(s32[2]{0:T(128)S(1)} %pad_add_fusion.place, s32[128]{0:T(128)S(1)} %copy-done.6, s32[128]{0:T(128)S(1)} %copy-done.7, f32[2,4,4]{2,1,0:T(4,128)S(1)} %copy-done.3, f32[2,4]{1,0:T(2,128)S(1)} %copy-done.5, bf16[4,64,2048]{2,1,0:T(8,128)(2,1)S(1)} %get-tuple-element.46.first, ...), custom_call_target="tpu_custom_call" | custom-call | tf_op jit(solution)/shard_map/last/pallas_call | solution.py:360
  (51 shorter events, 12.0 us)
Async XLA Ops:
  3.9 41.2 %collective-permute-start.3 = (bf16[3072,256]{1,0:T(8,128)(2,1)}, bf16[3072,256]{1,0:T(8,128)(2,1)S(1)}, u32[]{:S(2)}, u32[]{:S(2)}) collective-permute-start(bf16[3072,256]{1,0:T(8,128)(2,1)} %get-tuple-element.51.refs_4_), channel_id=1, source_target_pairs={{0,8},{4,12},{8,0},{12,4},{16,24},{20,28},{24,16},{28,20},{32,40},... | collective-permute-start | bytes 4718600 | tf_op jit(solution)/shard_map/ppermute | solution.py:473
  6.0 39.1 %collective-permute-start.4 = (bf16[3072,256]{1,0:T(8,128)(2,1)}, bf16[3072,256]{1,0:T(8,128)(2,1)S(1)}, u32[]{:S(2)}, u32[]{:S(2)}) collective-permute-start(bf16[3072,256]{1,0:T(8,128)(2,1)} %get-tuple-element.52.refs_5_), channel_id=1, source_target_pairs={{0,32},{4,36},{8,40},{12,44},{16,48},{20,52},{24,56},{28,60},{32,0... | collective-permute-start | bytes 4718600 | tf_op jit(solution)/shard_map/ppermute | solution.py:473
  7.6 38.0 %copy-start.3 = (f32[2,4,4]{2,1,0:T(4,128)S(1)}, f32[2,4,4]{2,1,0:T(4,128)}, u32[]{:S(2)}) copy-start(f32[2,4,4]{2,1,0:T(4,128)} %hc_res.3) | copy-start | bytes 388
  29.4 9.4 %collective-permute-start = (bf16[64,2048]{1,0:T(8,128)(2,1)S(1)}, bf16[64,2048]{1,0:T(8,128)(2,1)S(1)}, u32[]{:S(2)}, u32[]{:S(2)}) collective-permute-start(bf16[64,2048]{1,0:T(8,128)(2,1)S(1)} %get-tuple-element.36), channel_id=1, source_target_pairs={{0,1},{1,2},{2,3},{3,0},{4,5},{5,6},{6,7},{7,4},{8,9},{9,10},{10,1... | collective-permute-start | bytes 786440 | tf_op jit(solution)/shard_map/ppermute | solution.py:531
  31.1 12.2 %collective-permute-start.1 = (bf16[64,2048]{1,0:T(8,128)(2,1)S(1)}, bf16[64,2048]{1,0:T(8,128)(2,1)S(1)}, u32[]{:S(2)}, u32[]{:S(2)}) collective-permute-start(bf16[64,2048]{1,0:T(8,128)(2,1)S(1)} %get-tuple-element.37), channel_id=1, source_target_pairs={{0,3},{1,0},{2,1},{3,2},{4,7},{5,4},{6,5},{7,6},{8,11},{9,8},{10,9... | collective-permute-start | bytes 786440 | tf_op jit(solution)/shard_map/ppermute | solution.py:531
  32.7 12.3 %collective-permute-start.2 = (bf16[64,2048]{1,0:T(8,128)(2,1)S(1)}, bf16[64,2048]{1,0:T(8,128)(2,1)S(1)}, u32[]{:S(2)}, u32[]{:S(2)}) collective-permute-start(bf16[64,2048]{1,0:T(8,128)(2,1)S(1)} %get-tuple-element.38), channel_id=1, source_target_pairs={{0,2},{1,3},{2,0},{3,1},{4,6},{5,7},{6,4},{7,5},{8,10},{9,11},{10,... | collective-permute-start | bytes 786440 | tf_op jit(solution)/shard_map/ppermute | solution.py:531
  38.9 8.7 %collective-permute-start.5 = (bf16[3072,256]{1,0:T(8,128)(2,1)S(1)}, bf16[3072,256]{1,0:T(8,128)(2,1)S(1)}, u32[]{:S(2)}, u32[]{:S(2)}) collective-permute-start(bf16[3072,256]{1,0:T(8,128)(2,1)S(1)} %copy-done), channel_id=1, source_target_pairs={{0,4},{4,0},{8,12},{12,8},{16,20},{20,16},{24,28},{28,24},{32,36},... | collective-permute-start | bytes 4718600 | tf_op jit(solution)/shard_map/ppermute | solution.py:473
  43.3 4.3 %collective-permute-start.6 = (bf16[3072,256]{1,0:T(8,128)(2,1)S(1)}, bf16[3072,256]{1,0:T(8,128)(2,1)S(1)}, u32[]{:S(2)}, u32[]{:S(2)}) collective-permute-start(bf16[3072,256]{1,0:T(8,128)(2,1)S(1)} %copy-done.1), channel_id=1, source_target_pairs={{0,4},{4,0},{8,12},{12,8},{16,20},{20,16},{24,28},{28,24},{32,36},... | collective-permute-start | bytes 4718600 | tf_op jit(solution)/shard_map/ppermute | solution.py:473
  45.1 3.9 %collective-permute-start.7 = (bf16[3072,256]{1,0:T(8,128)(2,1)S(1)}, bf16[3072,256]{1,0:T(8,128)(2,1)S(1)}, u32[]{:S(2)}, u32[]{:S(2)}) collective-permute-start(bf16[3072,256]{1,0:T(8,128)(2,1)S(1)} %collective-permute-done.3.refs_8_), channel_id=1, source_target_pairs={{0,4},{4,0},{8,12},{12,8},{16,20},{20,16},{24,28},{28,24},{32,36},... | collective-permute-start | bytes 4718600 | tf_op jit(solution)/shard_map/ppermute | solution.py:473
  45.1 6.1 %collective-permute-start.8 = (bf16[3072,256]{1,0:T(8,128)(2,1)S(1)}, bf16[3072,256]{1,0:T(8,128)(2,1)S(1)}, u32[]{:S(2)}, u32[]{:S(2)}) collective-permute-start(bf16[3072,256]{1,0:T(8,128)(2,1)S(1)} %collective-permute-done.4.refs_9_), channel_id=1, source_target_pairs={{0,4},{4,0},{8,12},{12,8},{16,20},{20,16},{24,28},{28,24},{32,36},... | collective-permute-start | bytes 4718600 | tf_op jit(solution)/shard_map/ppermute | solution.py:473
  51.2 12.5 %collective-permute-start.18 = (bf16[64,2048]{1,0:T(8,128)(2,1)S(1)}, bf16[64,2048]{1,0:T(8,128)(2,1)S(1)}, u32[]{:S(2)}, u32[]{:S(2)}) collective-permute-start(bf16[64,2048]{1,0:T(8,128)(2,1)S(1)} %get-tuple-element.50.refs_0_), channel_id=1, source_target_pairs={{0,80},{4,84},{8,88},{12,92},{16,64},{20,68},{24,72},{28,76},{32,1... | collective-permute-start | bytes 786440 | tf_op jit(solution)/shard_map/ppermute | solution.py:473
  56.9 17.6 %collective-permute-start.17 = (bf16[64,2048]{1,0:T(8,128)(2,1)S(1)}, bf16[64,2048]{1,0:T(8,128)(2,1)S(1)}, u32[]{:S(2)}, u32[]{:S(2)}) collective-permute-start(bf16[64,2048]{1,0:T(8,128)(2,1)S(1)} %get-tuple-element.50.refs_0_), channel_id=1, source_target_pairs={{0,16},{4,20},{8,24},{12,28},{16,0},{20,4},{24,8},{28,12},{32,48},... | collective-permute-start | bytes 786440 | tf_op jit(solution)/shard_map/ppermute | solution.py:473
  56.9 17.6 %collective-permute-start.16 = (bf16[64,2048]{1,0:T(8,128)(2,1)S(1)}, bf16[64,2048]{1,0:T(8,128)(2,1)S(1)}, u32[]{:S(2)}, u32[]{:S(2)}) collective-permute-start(bf16[64,2048]{1,0:T(8,128)(2,1)S(1)} %get-tuple-element.50.refs_0_), channel_id=1, source_target_pairs={{0,64},{4,68},{8,72},{12,76},{16,80},{20,84},{24,88},{28,92},{32,9... | collective-permute-start | bytes 786440 | tf_op jit(solution)/shard_map/ppermute | solution.py:473
  57.7 17.3 %collective-permute-start.15 = (bf16[64,2048]{1,0:T(8,128)(2,1)S(1)}, bf16[64,2048]{1,0:T(8,128)(2,1)S(1)}, u32[]{:S(2)}, u32[]{:S(2)}) collective-permute-start(bf16[64,2048]{1,0:T(8,128)(2,1)S(1)} %get-tuple-element.50.refs_0_), channel_id=1, source_target_pairs={{0,104},{4,108},{8,112},{12,116},{16,120},{20,124},{24,96},{28,100... | collective-permute-start | bytes 786440 | tf_op jit(solution)/shard_map/ppermute | solution.py:473
  59.6 25.3 %collective-permute-start.11 = (bf16[64,2048]{1,0:T(8,128)(2,1)S(1)}, bf16[64,2048]{1,0:T(8,128)(2,1)S(1)}, u32[]{:S(2)}, u32[]{:S(2)}) collective-permute-start(bf16[64,2048]{1,0:T(8,128)(2,1)S(1)} %get-tuple-element.50.refs_0_), channel_id=1, source_target_pairs={{0,56},{4,60},{8,32},{12,36},{16,40},{20,44},{24,48},{28,52},{32,8... | collective-permute-start | bytes 786440 | tf_op jit(solution)/shard_map/ppermute | solution.py:473
  63.7 23.3 %collective-permute-start.10 = (bf16[64,2048]{1,0:T(8,128)(2,1)S(1)}, bf16[64,2048]{1,0:T(8,128)(2,1)S(1)}, u32[]{:S(2)}, u32[]{:S(2)}) collective-permute-start(bf16[64,2048]{1,0:T(8,128)(2,1)S(1)} %get-tuple-element.50.refs_0_), channel_id=1, source_target_pairs={{0,120},{4,124},{8,96},{12,100},{16,104},{20,108},{24,112},{28,116... | collective-permute-start | bytes 786440 | tf_op jit(solution)/shard_map/ppermute | solution.py:473
  74.5 15.0 %collective-permute-start.9 = (bf16[64,2048]{1,0:T(8,128)(2,1)S(1)}, bf16[64,2048]{1,0:T(8,128)(2,1)S(1)}, u32[]{:S(2)}, u32[]{:S(2)}) collective-permute-start(bf16[64,2048]{1,0:T(8,128)(2,1)S(1)} %get-tuple-element.50.refs_0_), channel_id=1, source_target_pairs={{0,40},{4,44},{8,48},{12,52},{16,56},{20,60},{24,32},{28,36},{32,7... | collective-permute-start | bytes 786440 | tf_op jit(solution)/shard_map/ppermute | solution.py:473
  78.5 28.9 %collective-permute-start.19 = (bf16[64,2048]{1,0:T(8,128)(2,1)S(1)}, bf16[64,2048]{1,0:T(8,128)(2,1)S(1)}, u32[]{:S(2)}, u32[]{:S(2)}) collective-permute-start(bf16[64,2048]{1,0:T(8,128)(2,1)S(1)} %get-tuple-element.63), channel_id=1, source_target_pairs={{0,56},{4,60},{8,32},{12,36},{16,40},{20,44},{24,48},{28,52},{32,8... | collective-permute-start | bytes 786440 | tf_op jit(solution)/shard_map/ppermute | solution.py:473
  83.0 24.4 %collective-permute-start.20 = (bf16[64,2048]{1,0:T(8,128)(2,1)S(1)}, bf16[64,2048]{1,0:T(8,128)(2,1)S(1)}, u32[]{:S(2)}, u32[]{:S(2)}) collective-permute-start(bf16[64,2048]{1,0:T(8,128)(2,1)S(1)} %get-tuple-element.64), channel_id=1, source_target_pairs={{0,64},{4,68},{8,72},{12,76},{16,80},{20,84},{24,88},{28,92},{32,9... | collective-permute-start | bytes 786440 | tf_op jit(solution)/shard_map/ppermute | solution.py:473
  84.8 25.3 %collective-permute-start.21 = (bf16[64,2048]{1,0:T(8,128)(2,1)S(1)}, bf16[64,2048]{1,0:T(8,128)(2,1)S(1)}, u32[]{:S(2)}, u32[]{:S(2)}) collective-permute-start(bf16[64,2048]{1,0:T(8,128)(2,1)S(1)} %get-tuple-element.65), channel_id=1, source_target_pairs={{0,16},{4,20},{8,24},{12,28},{16,0},{20,4},{24,8},{28,12},{32,48},... | collective-permute-start | bytes 786440 | tf_op jit(solution)/shard_map/ppermute | solution.py:473
  87.0 23.2 %collective-permute-start.22 = (bf16[64,2048]{1,0:T(8,128)(2,1)S(1)}, bf16[64,2048]{1,0:T(8,128)(2,1)S(1)}, u32[]{:S(2)}, u32[]{:S(2)}) collective-permute-start(bf16[64,2048]{1,0:T(8,128)(2,1)S(1)} %get-tuple-element.66), channel_id=1, source_target_pairs={{0,80},{4,84},{8,88},{12,92},{16,64},{20,68},{24,72},{28,76},{32,1... | collective-permute-start | bytes 786440 | tf_op jit(solution)/shard_map/ppermute | solution.py:473
  93.0 17.2 %collective-permute-start.12 = (bf16[64,2048]{1,0:T(8,128)(2,1)S(1)}, bf16[64,2048]{1,0:T(8,128)(2,1)S(1)}, u32[]{:S(2)}, u32[]{:S(2)}) collective-permute-start(bf16[64,2048]{1,0:T(8,128)(2,1)S(1)} %get-tuple-element.60), channel_id=1, source_target_pairs={{0,120},{4,124},{8,96},{12,100},{16,104},{20,108},{24,112},{28,116... | collective-permute-start | bytes 786440 | tf_op jit(solution)/shard_map/ppermute | solution.py:473
  107.4 12.4 %collective-permute-start.13 = (bf16[64,2048]{1,0:T(8,128)(2,1)S(1)}, bf16[64,2048]{1,0:T(8,128)(2,1)S(1)}, u32[]{:S(2)}, u32[]{:S(2)}) collective-permute-start(bf16[64,2048]{1,0:T(8,128)(2,1)S(1)} %get-tuple-element.61), channel_id=1, source_target_pairs={{0,40},{4,44},{8,48},{12,52},{16,56},{20,60},{24,32},{28,36},{32,7... | collective-permute-start | bytes 786440 | tf_op jit(solution)/shard_map/ppermute | solution.py:473
  107.4 12.9 %collective-permute-start.14 = (bf16[64,2048]{1,0:T(8,128)(2,1)S(1)}, bf16[64,2048]{1,0:T(8,128)(2,1)S(1)}, u32[]{:S(2)}, u32[]{:S(2)}) collective-permute-start(bf16[64,2048]{1,0:T(8,128)(2,1)S(1)} %get-tuple-element.62), channel_id=1, source_target_pairs={{0,104},{4,108},{8,112},{12,116},{16,120},{20,124},{24,96},{28,100... | collective-permute-start | bytes 786440 | tf_op jit(solution)/shard_map/ppermute | solution.py:473
  (10 other events, 153.1 us)

commit v4 on v3

--- a/solution.py
+++ b/solution.py
@@ -86,6 +86,10 @@
     wo,
     ck,
     cv,
+    sc_s,
+    lo_s,
+    w1_s,
+    w2_s,
     sems,
 ):
     i = pl.program_id(0)
@@ -107,7 +111,7 @@
         for c in loads(0):
             c.start()
 
-    @pl.when(i == 1)
+    @pl.when(i == SLOTS - 1)
     def _():
         for c in loads(1):
             c.start()
@@ -184,36 +188,47 @@
         col = lax.broadcasted_iota(jnp.int32, (DRAFT, CACHE), 1)
         for c in arrive[3:]:
             c.wait()
+        kept = []
         for hh in range(2):
             cols = slice(hh * HD, (hh + 1) * HD)
             qh = q2[:, cols]
             kh = k2[:, cols]
             qh = (qh * cosine + pltpu.roll(qh, HD // 2, 1) * sine).astype(BF)
             kh = (kh * cosine + pltpu.roll(kh, HD // 2, 1) * sine).astype(BF)
-            vh = v2[:, cols]
-            for s in range(SLOTS):
-                at = slice(s * DRAFT, (s + 1) * DRAFT)
-                length = clen[owner[base + s]]
-                qs, ks, vs = qh[at], kh[at], vh[at]
-                sc = mm_nt(qs, ck[g, s, :, cols]) * SCALE
-                sc = jnp.where(col < length, sc, -1e30)
-                lo = mm_nt(qs, ks) * SCALE
-                lo = jnp.where(above_s[s] > 0.5, lo, -1e30)
-                top = jnp.maximum(
-                    jnp.max(sc, axis=-1, keepdims=True), jnp.max(lo, axis=-1, keepdims=True)
-                )
-                e1 = jnp.exp(sc - top)
-                e2 = jnp.exp(lo - top)
-                total = jnp.sum(e1, axis=-1, keepdims=True) + jnp.sum(e2, axis=-1, keepdims=True)
-                inv = 1.0 / total
-                w1 = (e1 * inv).astype(BF)
-                w2 = (e2 * inv).astype(BF)
-                o = mm(w1, cv[g, s, :, cols]) + mm(w2, vs)
-                att[at, cols] = o.astype(BF)
-                tk = take_s[s]
-                h = g * 2 + hh
-                kvs[s, pl.ds(h * 2, DRAFT, stride=8), :] = mm(tk, ks)
-                kvs[s, pl.ds(h * 2 + 1, DRAFT, stride=8), :] = mm(tk, vs)
+            kept.append((cols, qh, kh, v2[:, cols]))
+        todo = [(hh, s) for hh in range(2) for s in range(SLOTS)]
+        for n, (hh, s) in enumerate(todo):
+            cols, qh, kh, vh = kept[hh]
+            at = slice(s * DRAFT, (s + 1) * DRAFT)
+            to = slice(n * DRAFT, (n + 1) * DRAFT)
+            length = clen[owner[base + s]]
+            sc = mm_nt(qh[at], ck[g, s, :, cols]) * SCALE
+            sc_s[to, :] = jnp.where(col < length, sc, -1e30)
+            lo = mm_nt(qh[at], kh[at]) * SCALE
+            lo_s[to, :] = jnp.where(above_s[s] > 0.5, lo, -1e30)
+        for hh in range(2):
+            to = slice(hh * 256, (hh + 1) * 256)
+            sc = sc_s[to, :]
+            lo = lo_s[to, :]
+            top = jnp.maximum(
+                jnp.max(sc, axis=-1, keepdims=True), jnp.max(lo, axis=-1, keepdims=True)
+            )
+            e1 = jnp.exp(sc - top)
+            e2 = jnp.exp(lo - top)
+            total = jnp.sum(e1, axis=-1, keepdims=True) + jnp.sum(e2, axis=-1, keepdims=True)
+            inv = 1.0 / total
+            w1_s[to, :] = (e1 * inv).astype(BF)
+            w2_s[to, :] = (e2 * inv).astype(BF)
+        for n, (hh, s) in enumerate(todo):
+            cols, qh, kh, vh = kept[hh]
+            at = slice(s * DRAFT, (s + 1) * DRAFT)
+            to = slice(n * DRAFT, (n + 1) * DRAFT)
+            o = mm(w1_s[to, :], cv[g, s, :, cols]) + mm(w2_s[to, :], vh[at])
+            att[at, cols] = o.astype(BF)
+            tk = take_s[s]
+            h = g * 2 + hh
+            kvs[s, pl.ds(h * 2, DRAFT, stride=8), :] = mm(tk, kh[at])
+            kvs[s, pl.ds(h * 2 + 1, DRAFT, stride=8), :] = mm(tk, vh[at])
         part = mm(att[...], wo[g])
         if g == 0:
             acc[...] = part
@@ -272,10 +287,14 @@
                 pltpu.VMEM((2, 256, D), BF),
                 pltpu.VMEM((2, SLOTS, CACHE, 256), BF),
                 pltpu.VMEM((2, SLOTS, CACHE, 256), BF),
+                pltpu.VMEM((512, CACHE), F32),
+                pltpu.VMEM((512, DRAFT), F32),
+                pltpu.VMEM((512, CACHE), BF),
+                pltpu.VMEM((512, DRAFT), BF),
                 pltpu.SemaphoreType.DMA((2, 6)),
             ],
         ),
-        compiler_params=pltpu.CompilerParams(vmem_limit_bytes=36 * 2**20),
+        compiler_params=pltpu.CompilerParams(vmem_limit_bytes=40 * 2**20),
     )(
         place,
         owner,
@@ -368,50 +387,41 @@
     )(place, owner, dlen, hc_res, hc_out, near(first), *[near(p) for p in parts])
 
 
-def pack_kernel(g, u, d, one, two, buf, sems):
-    ins, outs = [], []
+def pack_kernel(g, u, d, one, two, sems):
+    ins = []
     for k, w in enumerate((one, two)):
         part = pl.ds(k * 128, 128)
-        here = buf.at[k]
         ins.append(
-            [
-                pltpu.make_async_copy(
-                    g.at[:, part], here.at[pl.ds(0, D), pl.ds(0, 128)], sems.at[k, 0]
-                ),
-                pltpu.make_async_copy(
-                    u.at[:, part], here.at[pl.ds(0, D), pl.ds(128, 128)], sems.at[k, 1]
-                ),
-            ]
-            + [
+            pltpu.make_async_copy(g.at[:, part], w.at[pl.ds(0, D), pl.ds(0, 128)], sems.at[k, 0])
+        )
+        ins.append(
+            pltpu.make_async_copy(u.at[:, part], w.at[pl.ds(0, D), pl.ds(128, 128)], sems.at[k, 1])
+        )
+        for c in range(8):
+            ins.append(
                 pltpu.make_async_copy(
                     d.at[part, pl.ds(256 * c, 256)],
-                    here.at[pl.ds(D + 128 * c, 128), :],
+                    w.at[pl.ds(D + 128 * c, 128), :],
                     sems.at[k, 2 + c],
                 )
-                for c in range(8)
-            ]
-        )
-        outs.append(pltpu.make_async_copy(here, w, sems.at[k, 10]))
-    for k in range(2):
-        for c in ins[k]:
-            c.start()
-    for k in range(2):
-        for c in ins[k]:
-            c.wait()
-        outs[k].start()
-    for k in range(2):
-        outs[k].wait()
+            )
+    for c in ins:
+        c.start()
+    for c in ins:
+        c.wait()
 
 
 def pack(g, u, d):
     hbm = pl.BlockSpec(memory_space=pltpu.HBM)
+    vmem = pl.BlockSpec(memory_space=pltpu.VMEM)
     return pl.pallas_call(
         pack_kernel,
         name="pack",
-        out_shape=(jax.ShapeDtypeStruct((PACKED, 256), BF),) * 2,
+        out_shape=(pltpu.VMEM((PACKED, 256), BF),) * 2,
         in_specs=[hbm] * 3,
-        out_specs=(hbm, hbm),
-        scratch_shapes=[pltpu.VMEM((2, PACKED, 256), BF), pltpu.SemaphoreType.DMA((2, 11))],
+        out_specs=(vmem, vmem),
+        scratch_shapes=[pltpu.SemaphoreType.DMA((2, 10))],
+        compiler_params=pltpu.CompilerParams(vmem_limit_bytes=8 * 2**20),
     )(*[pltpu.with_memory_space_constraint(x, pltpu.HBM) for x in (g, u, d)])
 
 
@@ -509,7 +519,7 @@
     one, two = pack(w_gate, w_up, w_down)
     one_z = send(one, lambda x, z, c: (x, z ^ 1, c))
     two_x = send(two, lambda x, z, c: (x ^ 1, z, c))
-    weights = (one, two, other_core(one), other_core(two))
+    one_c, two_c = other_core(one), other_core(two)
     *out, own, kv = front(
         place,
         slot_owner,
@@ -527,15 +537,17 @@
         cache_values,
         w_output,
     )
-    parts = [out[0]] + [
-        lax.ppermute(out[k], "head", [(y, (y + k) % 4) for y in range(4)]) for k in (1, 3, 2)
-    ]
-    parts, one_z, two_x = lax.optimization_barrier((parts, one_z, two_x))
-    weights = weights + (one_z, two_x, other_core(one_z), other_core(two_x))
-    first, rows = mid(hc_in, hc_res, hc_out, [parts[0], parts[1], parts[3], parts[2]], own)
+    turn = lambda v, k: lax.ppermute(v, "head", [(y, (y + k) % 4) for y in range(4)])
+    out, one_c, two_c = lax.optimization_barrier((out, one_c, two_c))
+    p1 = turn(out[1], 1)
+    p3 = turn(out[3], 3)
+    p2 = turn(out[2], 2)
+    p1, p2, p3, one_z, two_x = lax.optimization_barrier((p1, p2, p3, one_z, two_x))
+    weights = (one, two, one_c, two_c, one_z, two_x, other_core(one_z), other_core(two_x))
+    first, rows = mid(hc_in, hc_res, hc_out, [out[0], p1, p2, p3], own)
     rows, weights = lax.optimization_barrier((rows, weights))
     pieces = [rows] + [shift(rows, dx, dz) for dx, dz in OFFSETS]
-    sums = ffn(pieces[:FIRST], weights) + ffn(pieces[FIRST:], weights)
+    sums = ffn(pieces, weights)
     back = [sums[0]] + [shift(t, -dx, -dz) for t, (dx, dz) in zip(sums[1:], OFFSETS)]
     final = last(place, slot_owner, draft_len, hc_res, hc_out, first, back)
     new_streams = (

time: 125 us -> 123 us (0.984); the launches traced: 123 us -> 123 us
  waiting for transfers between devices: 45.3 us -> 54.8 us
  Pallas kernels: 36.7 us -> 31.5 us
  starting transfers between devices: 40.2 us -> 35.5 us
    ppermute x20, waiting for transfers between devices: 34.9 us -> 54.8 us  [send(): return lax.ppermute(v, 'req', pairs(move))]
    ppermute x3, waiting for transfers between devices: 10.3 us -> 0.01 us  [body(): lax.ppermute(v, 'head', [(y, (y + k) % 4) for y in range(4)])]
    pallas_call x1, Pallas kernels: 21.8 us -> 15 us  [front(): pl.pallas_call(front_kernel, name='front', out_shape=(pltpu.VMEM((SLOTS *...]
    ppermute x20, starting transfers between devices: 34.9 us -> 29.6 us  [send(): return lax.ppermute(v, 'req', pairs(move))]
    pallas_call x2 -> x1, Pallas kernels: 6.87 us -> 9.59 us  [ffn(): pl.pallas_call(functools.partial(ffn_kernel, n), name='ffn', out_shape=tu...]
  transfers between devices with their start and end apart: 23 -> 23, of which waited for: 11 -> 14; matrix products, arithmetic and copies ran while one was open for 0% -> 0% of each run, Pallas kernels for 25% -> 14%
where the time goes in v4:
time: 123 us
  waiting for transfers between devices  54.8 us (45%)
  starting transfers between devices  35.5 us (29%)
  Pallas kernels  31.5 us (26%)
    ppermute x20, waiting for transfers between devices, send(): return lax.ppermute(v, 'req', pairs(move))  54.8 us
    ppermute x20, starting transfers between devices, send(): return lax.ppermute(v, 'req', pairs(move))  29.6 us
    pallas_call x1, Pallas kernels, front(): pl.pallas_call(front_kernel, name='front', out_shape=(pltpu.VMEM((SLOTS *...  15 us
    pallas_call x1, Pallas kernels, ffn(): pl.pallas_call(functools.partial(ffn_kernel, n), name='ffn', out_shape=tu...  9.59 us
    ppermute x3, starting transfers between devices, body(): lax.ppermute(v, 'head', [(y, (y + k) % 4) for y in range(4)])  5.9 us
    pallas_call x1, Pallas kernels, last(): pl.pallas_call(last_kernel, name='last', out_shape=jax.ShapeDtypeStruct((...  2.88 us
  transfers between devices with their start and end apart: 23, of which 14 were waited for; matrix products, arithmetic and copies ran while one was open for 0% of the time, Pallas kernels for 14%

profile of v4, /device:TPU:0, one launch (start us, length us, event | category | flops | bytes accessed | tf_op | source)
XLA Modules:
  0.0 122.8 jit_solution(3308785354523426115)
XLA Ops:
  0.7 2.0 %pack.1 = (bf16[3072,256]{1,0:T(8,128)(2,1)S(1)}, bf16[3072,256]{1,0:T(8,128)(2,1)S(1)}) custom-call(bf16[2048,256]{1,0:T(8,128)(2,1)} %g.1, bf16[2048,256]{1,0:T(8,128)(2,1)} %u.1, bf16[256,2048]{1,0:T(8,128)(2,1)} %d.1), custom_call_target="tpu_custom_call" | custom-call | tf_op jit(solution)/shard_map/pack/pallas_call | solution.py:417
  3.3 2.0 %collective-permute-start.5 = (bf16[3072,256]{1,0:T(8,128)(2,1)S(1)}, bf16[3072,256]{1,0:T(8,128)(2,1)}, u32[]{:S(2)}, u32[]{:S(2)}) collective-permute-start(bf16[3072,256]{1,0:T(8,128)(2,1)S(1)} %get-tuple-element.61.refs_8_), channel_id=1, source_target_pairs={{0,8},{4,12},{8,0},{12,4},{16,24},{20,28},{24,16},{28,20},{32,40},... | collective-permute-start | bytes 4718600 | tf_op jit(solution)/shard_map/ppermute | solution.py:483
  6.9 15.0 %front.1 = (bf16[64,2048]{1,0:T(8,128)(2,1)S(1)}, bf16[64,2048]{1,0:T(8,128)(2,1)S(1)}, bf16[64,2048]{1,0:T(8,128)(2,1)S(1)}, bf16[64,2048]{1,0:T(8,128)(2,1)S(1...) custom-call(s32[2]{0:T(128)S(1)} %pad_add_fusion.place, s32[128]{0:T(128)S(1)} %copy-done.4, ...), custom_call_target="tpu_custom_call" | custom-call | tf_op jit(solution)/shard_map/front/pallas_call | solution.py:254
  23.6 2.9 %collective-permute-start.3 = (bf16[64,2048]{1,0:T(8,128)(2,1)S(1)}, bf16[64,2048]{1,0:T(8,128)(2,1)S(1)}, u32[]{:S(2)}, u32[]{:S(2)}) collective-permute-start(bf16[64,2048]{1,0:T(8,128)(2,1)S(1)} %get-tuple-element.48), channel_id=1, source_target_pairs={{0,2},{1,3},{2,0},{3,1},{4,6},{5,7},{6,4},{7,5},{8,10},{9,11},{10,... | collective-permute-start | bytes 786440 | tf_op jit(solution)/shard_map/ppermute | solution.py:540
  27.9 12.2 %collective-permute-done.5.refs_12_ = bf16[3072,256]{1,0:T(8,128)(2,1)} collective-permute-done((bf16[3072,256]{1,0:T(8,128)(2,1)S(1)}, bf16[3072,256]{1,0:T(8,128)(2,1)}, u32[]{:S(2)}, u32[]{:S(2)}) %collective-permute-start.5) | collective-permute-done | bytes 1572896 | tf_op jit(solution)/shard_map/ppermute | solution.py:483
  42.1 2.0 %mid.1 = (bf16[4,64,2048]{2,1,0:T(8,128)(2,1)S(1)}, bf16[64,2048]{1,0:T(8,128)(2,1)S(1)}) custom-call(f32[2,4]{1,0:T(2,128)S(1)} %copy-done.2, f32[2,4,4]{2,1,0:T(4,128)S(1)} %copy-done.1, f32[2,4]{1,0:T(2,128)S(1)} %copy-done.3, bf16[64,2048]{1,0:T(8,128)(2,1)S(1)} %get-tuple-element.46.p0, bf16[64,2048]{1,0:T(8,128)(2,1)S(1)} %collective-permute-done.2.p1, ...), custom_call_target="tpu_custom_call" | custom-call | tf_op jit(solution)/shard_map/mid/pallas_call | solution.py:342
  45.2 2.2 %collective-permute-done.8.refs_15_ = bf16[3072,256]{1,0:T(8,128)(2,1)S(1)} collective-permute-done((bf16[3072,256]{1,0:T(8,128)(2,1)}, bf16[3072,256]{1,0:T(8,128)(2,1)S(1)}, u32[]{:S(2)}, u32[]{:S(2)}) %collective-permute-start.8) | collective-permute-done | bytes 1572896 | tf_op jit(solution)/shard_map/ppermute | solution.py:483
  47.5 6.0 %collective-permute-start.15 = (bf16[64,2048]{1,0:T(8,128)(2,1)S(1)}, bf16[64,2048]{1,0:T(8,128)(2,1)S(1)}, u32[]{:S(2)}, u32[]{:S(2)}) collective-permute-start(bf16[64,2048]{1,0:T(8,128)(2,1)S(1)} %get-tuple-element.60.refs_0_), channel_id=1, source_target_pairs={{0,80},{4,84},{8,88},{12,92},{16,64},{20,68},{24,72},{28,76},{32,1... | collective-permute-start | bytes 786440 | tf_op jit(solution)/shard_map/ppermute | solution.py:483
  54.1 2.4 %collective-permute-start.12 = (bf16[64,2048]{1,0:T(8,128)(2,1)S(1)}, bf16[64,2048]{1,0:T(8,128)(2,1)S(1)}, u32[]{:S(2)}, u32[]{:S(2)}) collective-permute-start(bf16[64,2048]{1,0:T(8,128)(2,1)S(1)} %get-tuple-element.60.refs_0_), channel_id=1, source_target_pairs={{0,104},{4,108},{8,112},{12,116},{16,120},{20,124},{24,96},{28,100... | collective-permute-start | bytes 786440 | tf_op jit(solution)/shard_map/ppermute | solution.py:483
  56.5 1.8 %collective-permute-start.11 = (bf16[64,2048]{1,0:T(8,128)(2,1)S(1)}, bf16[64,2048]{1,0:T(8,128)(2,1)S(1)}, u32[]{:S(2)}, u32[]{:S(2)}) collective-permute-start(bf16[64,2048]{1,0:T(8,128)(2,1)S(1)} %get-tuple-element.60.refs_0_), channel_id=1, source_target_pairs={{0,56},{4,60},{8,32},{12,36},{16,40},{20,44},{24,48},{28,52},{32,8... | collective-permute-start | bytes 786440 | tf_op jit(solution)/shard_map/ppermute | solution.py:483
  58.2 2.1 %collective-permute-done.15.refs_7_ = bf16[64,2048]{1,0:T(8,128)(2,1)S(1)} collective-permute-done((bf16[64,2048]{1,0:T(8,128)(2,1)S(1)}, bf16[64,2048]{1,0:T(8,128)(2,1)S(1)}, u32[]{:S(2)}, u32[]{:S(2)}) %collective-permute-start.15) | collective-permute-done | bytes 262176 | tf_op jit(solution)/shard_map/ppermute | solution.py:483
  60.3 5.1 %collective-permute-start.10 = (bf16[64,2048]{1,0:T(8,128)(2,1)S(1)}, bf16[64,2048]{1,0:T(8,128)(2,1)S(1)}, u32[]{:S(2)}, u32[]{:S(2)}) collective-permute-start(bf16[64,2048]{1,0:T(8,128)(2,1)S(1)} %get-tuple-element.60.refs_0_), channel_id=1, source_target_pairs={{0,120},{4,124},{8,96},{12,100},{16,104},{20,108},{24,112},{28,116... | collective-permute-start | bytes 786440 | tf_op jit(solution)/shard_map/ppermute | solution.py:483
  65.4 5.3 %collective-permute-done.14.refs_6_ = bf16[64,2048]{1,0:T(8,128)(2,1)S(1)} collective-permute-done((bf16[64,2048]{1,0:T(8,128)(2,1)S(1)}, bf16[64,2048]{1,0:T(8,128)(2,1)S(1)}, u32[]{:S(2)}, u32[]{:S(2)}) %collective-permute-start.14) | collective-permute-done | bytes 262176 | tf_op jit(solution)/shard_map/ppermute | solution.py:483
  72.0 6.1 %collective-permute-done.10.refs_2_ = bf16[64,2048]{1,0:T(8,128)(2,1)S(1)} collective-permute-done((bf16[64,2048]{1,0:T(8,128)(2,1)S(1)}, bf16[64,2048]{1,0:T(8,128)(2,1)S(1)}, u32[]{:S(2)}, u32[]{:S(2)}) %collective-permute-start.10) | collective-permute-done | bytes 262176 | tf_op jit(solution)/shard_map/ppermute | solution.py:483
  78.1 4.1 %collective-permute-done.9.refs_1_ = bf16[64,2048]{1,0:T(8,128)(2,1)S(1)} collective-permute-done((bf16[64,2048]{1,0:T(8,128)(2,1)S(1)}, bf16[64,2048]{1,0:T(8,128)(2,1)S(1)}, u32[]{:S(2)}, u32[]{:S(2)}) %collective-permute-start.9) | collective-permute-done | bytes 262176 | tf_op jit(solution)/shard_map/ppermute | solution.py:483
  82.2 9.6 %ffn.1 = (bf16[64,2048]{1,0:T(8,128)(2,1)S(1)}, bf16[64,2048]{1,0:T(8,128)(2,1)S(1)}, bf16[64,2048]{1,0:T(8,128)(2,1)S(1)}, bf16[64,2048]{1,0:T(8,128)(2,1)S(1)}...) custom-call(bf16[64,2048]{1,0:T(8,128)(2,1)S(1)} %get-tuple-element., ...), custom_call_target="tpu_custom_call" | custom-call | flops 6442450944 | bytes 4194304 | tf_op jit(solution)/shard_map/ffn/pallas_call | solution.py:455
  91.9 2.9 %collective-permute-start.17 = (bf16[64,2048]{1,0:T(8,128)(2,1)S(1)}, bf16[64,2048]{1,0:T(8,128)(2,1)S(1)}, u32[]{:S(2)}, u32[]{:S(2)}) collective-permute-start(bf16[64,2048]{1,0:T(8,128)(2,1)S(1)} %get-tuple-element.71), channel_id=1, source_target_pairs={{0,40},{4,44},{8,48},{12,52},{16,56},{20,60},{24,32},{28,36},{32,7... | collective-permute-start | bytes 786440 | tf_op jit(solution)/shard_map/ppermute | solution.py:483
  96.4 2.5 %collective-permute-start.19 = (bf16[64,2048]{1,0:T(8,128)(2,1)S(1)}, bf16[64,2048]{1,0:T(8,128)(2,1)S(1)}, u32[]{:S(2)}, u32[]{:S(2)}) collective-permute-start(bf16[64,2048]{1,0:T(8,128)(2,1)S(1)} %get-tuple-element.73), channel_id=1, source_target_pairs={{0,56},{4,60},{8,32},{12,36},{16,40},{20,44},{24,48},{28,52},{32,8... | collective-permute-start | bytes 786440 | tf_op jit(solution)/shard_map/ppermute | solution.py:483
  98.9 1.9 %collective-permute-start.20 = (bf16[64,2048]{1,0:T(8,128)(2,1)S(1)}, bf16[64,2048]{1,0:T(8,128)(2,1)S(1)}, u32[]{:S(2)}, u32[]{:S(2)}) collective-permute-start(bf16[64,2048]{1,0:T(8,128)(2,1)S(1)} %get-tuple-element.74), channel_id=1, source_target_pairs={{0,64},{4,68},{8,72},{12,76},{16,80},{20,84},{24,88},{28,92},{32,9... | collective-permute-start | bytes 786440 | tf_op jit(solution)/shard_map/ppermute | solution.py:483
  102.1 5.0 %collective-permute-done.17.refs_2_ = bf16[64,2048]{1,0:T(8,128)(2,1)S(1)} collective-permute-done((bf16[64,2048]{1,0:T(8,128)(2,1)S(1)}, bf16[64,2048]{1,0:T(8,128)(2,1)S(1)}, u32[]{:S(2)}, u32[]{:S(2)}) %collective-permute-start.17) | collective-permute-done | bytes 262176 | tf_op jit(solution)/shard_map/ppermute | solution.py:483
  107.1 4.2 %collective-permute-done.18.refs_3_ = bf16[64,2048]{1,0:T(8,128)(2,1)S(1)} collective-permute-done((bf16[64,2048]{1,0:T(8,128)(2,1)S(1)}, bf16[64,2048]{1,0:T(8,128)(2,1)S(1)}, u32[]{:S(2)}, u32[]{:S(2)}) %collective-permute-start.18) | collective-permute-done | bytes 262176 | tf_op jit(solution)/shard_map/ppermute | solution.py:483
  111.3 6.7 %collective-permute-done.19.refs_4_ = bf16[64,2048]{1,0:T(8,128)(2,1)S(1)} collective-permute-done((bf16[64,2048]{1,0:T(8,128)(2,1)S(1)}, bf16[64,2048]{1,0:T(8,128)(2,1)S(1)}, u32[]{:S(2)}, u32[]{:S(2)}) %collective-permute-start.19) | collective-permute-done | bytes 262176 | tf_op jit(solution)/shard_map/ppermute | solution.py:483
  118.0 1.9 %collective-permute-done.21.refs_6_ = bf16[64,2048]{1,0:T(8,128)(2,1)S(1)} collective-permute-done((bf16[64,2048]{1,0:T(8,128)(2,1)S(1)}, bf16[64,2048]{1,0:T(8,128)(2,1)S(1)}, u32[]{:S(2)}, u32[]{:S(2)}) %collective-permute-start.21) | collective-permute-done | bytes 262176 | tf_op jit(solution)/shard_map/ppermute | solution.py:483
  119.9 2.9 %last.1 = bf16[4096,128]{1,0:T(8,128)(2,1)} custom-call(s32[2]{0:T(128)S(1)} %pad_add_fusion.place, s32[128]{0:T(128)S(1)} %copy-done.4, s32[128]{0:T(128)S(1)} %copy-done.5, f32[2,4,4]{2,1,0:T(4,128)S(1)} %copy-done.1, f32[2,4]{1,0:T(2,128)S(1)} %copy-done.3, bf16[4,64,2048]{2,1,0:T(8,128)(2,1)S(1)} %get-tuple-element.54.first, ...), custom_call_target="tpu_custom_call" | custom-call | tf_op jit(solution)/shard_map/last/pallas_call | solution.py:379
  (46 shorter events, 13.1 us)
Async XLA Ops:
  2.7 19.3 %collective-permute-start = (bf16[3072,256]{1,0:T(8,128)(2,1)S(1)}, bf16[3072,256]{1,0:T(8,128)(2,1)}, u32[]{:S(2)}, u32[]{:S(2)}) collective-permute-start(bf16[3072,256]{1,0:T(8,128)(2,1)S(1)} %get-tuple-element.61.refs_8_), channel_id=1, source_target_pairs={{0,4},{4,0},{8,12},{12,8},{16,20},{20,16},{24,28},{28,24},{32,36},... | collective-permute-start | bytes 4718600 | tf_op jit(solution)/shard_map/ppermute | solution.py:483
  2.8 19.2 %collective-permute-start.1 = (bf16[3072,256]{1,0:T(8,128)(2,1)S(1)}, bf16[3072,256]{1,0:T(8,128)(2,1)}, u32[]{:S(2)}, u32[]{:S(2)}) collective-permute-start(bf16[3072,256]{1,0:T(8,128)(2,1)S(1)} %get-tuple-element.62.refs_9_), channel_id=1, source_target_pairs={{0,4},{4,0},{8,12},{12,8},{16,20},{20,16},{24,28},{28,24},{32,36},... | collective-permute-start | bytes 4718600 | tf_op jit(solution)/shard_map/ppermute | solution.py:483
  3.3 36.8 %collective-permute-start.5 = (bf16[3072,256]{1,0:T(8,128)(2,1)S(1)}, bf16[3072,256]{1,0:T(8,128)(2,1)}, u32[]{:S(2)}, u32[]{:S(2)}) collective-permute-start(bf16[3072,256]{1,0:T(8,128)(2,1)S(1)} %get-tuple-element.61.refs_8_), channel_id=1, source_target_pairs={{0,8},{4,12},{8,0},{12,4},{16,24},{20,28},{24,16},{28,20},{32,40},... | collective-permute-start | bytes 4718600 | tf_op jit(solution)/shard_map/ppermute | solution.py:483
  5.3 36.2 %collective-permute-start.6 = (bf16[3072,256]{1,0:T(8,128)(2,1)S(1)}, bf16[3072,256]{1,0:T(8,128)(2,1)}, u32[]{:S(2)}, u32[]{:S(2)}) collective-permute-start(bf16[3072,256]{1,0:T(8,128)(2,1)S(1)} %get-tuple-element.62.refs_9_), channel_id=1, source_target_pairs={{0,32},{4,36},{8,40},{12,44},{16,48},{20,52},{24,56},{28,60},{32,0... | collective-permute-start | bytes 4718600 | tf_op jit(solution)/shard_map/ppermute | solution.py:483
  6.9 35.2 %copy-start.1 = (f32[2,4,4]{2,1,0:T(4,128)S(1)}, f32[2,4,4]{2,1,0:T(4,128)}, u32[]{:S(2)}) copy-start(f32[2,4,4]{2,1,0:T(4,128)} %hc_res.3) | copy-start | bytes 388
  22.0 19.5 %collective-permute-start.2 = (bf16[64,2048]{1,0:T(8,128)(2,1)S(1)}, bf16[64,2048]{1,0:T(8,128)(2,1)S(1)}, u32[]{:S(2)}, u32[]{:S(2)}) collective-permute-start(bf16[64,2048]{1,0:T(8,128)(2,1)S(1)} %get-tuple-element.47), channel_id=1, source_target_pairs={{0,1},{1,2},{2,3},{3,0},{4,5},{5,6},{6,7},{7,4},{8,9},{9,10},{10,1... | collective-permute-start | bytes 786440 | tf_op jit(solution)/shard_map/ppermute | solution.py:540
  23.6 17.9 %collective-permute-start.3 = (bf16[64,2048]{1,0:T(8,128)(2,1)S(1)}, bf16[64,2048]{1,0:T(8,128)(2,1)S(1)}, u32[]{:S(2)}, u32[]{:S(2)}) collective-permute-start(bf16[64,2048]{1,0:T(8,128)(2,1)S(1)} %get-tuple-element.48), channel_id=1, source_target_pairs={{0,2},{1,3},{2,0},{3,1},{4,6},{5,7},{6,4},{7,5},{8,10},{9,11},{10,... | collective-permute-start | bytes 786440 | tf_op jit(solution)/shard_map/ppermute | solution.py:540
  26.6 15.0 %collective-permute-start.4 = (bf16[64,2048]{1,0:T(8,128)(2,1)S(1)}, bf16[64,2048]{1,0:T(8,128)(2,1)S(1)}, u32[]{:S(2)}, u32[]{:S(2)}) collective-permute-start(bf16[64,2048]{1,0:T(8,128)(2,1)S(1)} %get-tuple-element.49), channel_id=1, source_target_pairs={{0,3},{1,0},{2,1},{3,2},{4,7},{5,4},{6,5},{7,6},{8,11},{9,8},{10,9... | collective-permute-start | bytes 786440 | tf_op jit(solution)/shard_map/ppermute | solution.py:540
  41.5 3.7 %collective-permute-start.7 = (bf16[3072,256]{1,0:T(8,128)(2,1)}, bf16[3072,256]{1,0:T(8,128)(2,1)S(1)}, u32[]{:S(2)}, u32[]{:S(2)}) collective-permute-start(bf16[3072,256]{1,0:T(8,128)(2,1)} %collective-permute-done.5.refs_12_), channel_id=1, source_target_pairs={{0,4},{4,0},{8,12},{12,8},{16,20},{20,16},{24,28},{28,24},{32,36},... | collective-permute-start | bytes 4718600 | tf_op jit(solution)/shard_map/ppermute | solution.py:483
  41.6 5.9 %collective-permute-start.8 = (bf16[3072,256]{1,0:T(8,128)(2,1)}, bf16[3072,256]{1,0:T(8,128)(2,1)S(1)}, u32[]{:S(2)}, u32[]{:S(2)}) collective-permute-start(bf16[3072,256]{1,0:T(8,128)(2,1)} %collective-permute-done.6.refs_13_), channel_id=1, source_target_pairs={{0,4},{4,0},{8,12},{12,8},{16,20},{20,16},{24,28},{28,24},{32,36},... | collective-permute-start | bytes 4718600 | tf_op jit(solution)/shard_map/ppermute | solution.py:483
  47.5 12.8 %collective-permute-start.15 = (bf16[64,2048]{1,0:T(8,128)(2,1)S(1)}, bf16[64,2048]{1,0:T(8,128)(2,1)S(1)}, u32[]{:S(2)}, u32[]{:S(2)}) collective-permute-start(bf16[64,2048]{1,0:T(8,128)(2,1)S(1)} %get-tuple-element.60.refs_0_), channel_id=1, source_target_pairs={{0,80},{4,84},{8,88},{12,92},{16,64},{20,68},{24,72},{28,76},{32,1... | collective-permute-start | bytes 786440 | tf_op jit(solution)/shard_map/ppermute | solution.py:483
  53.5 17.2 %collective-permute-start.14 = (bf16[64,2048]{1,0:T(8,128)(2,1)S(1)}, bf16[64,2048]{1,0:T(8,128)(2,1)S(1)}, u32[]{:S(2)}, u32[]{:S(2)}) collective-permute-start(bf16[64,2048]{1,0:T(8,128)(2,1)S(1)} %get-tuple-element.60.refs_0_), channel_id=1, source_target_pairs={{0,16},{4,20},{8,24},{12,28},{16,0},{20,4},{24,8},{28,12},{32,48},... | collective-permute-start | bytes 786440 | tf_op jit(solution)/shard_map/ppermute | solution.py:483
  53.5 17.2 %collective-permute-start.13 = (bf16[64,2048]{1,0:T(8,128)(2,1)S(1)}, bf16[64,2048]{1,0:T(8,128)(2,1)S(1)}, u32[]{:S(2)}, u32[]{:S(2)}) collective-permute-start(bf16[64,2048]{1,0:T(8,128)(2,1)S(1)} %get-tuple-element.60.refs_0_), channel_id=1, source_target_pairs={{0,64},{4,68},{8,72},{12,76},{16,80},{20,84},{24,88},{28,92},{32,9... | collective-permute-start | bytes 786440 | tf_op jit(solution)/shard_map/ppermute | solution.py:483
  54.1 17.9 %collective-permute-start.12 = (bf16[64,2048]{1,0:T(8,128)(2,1)S(1)}, bf16[64,2048]{1,0:T(8,128)(2,1)S(1)}, u32[]{:S(2)}, u32[]{:S(2)}) collective-permute-start(bf16[64,2048]{1,0:T(8,128)(2,1)S(1)} %get-tuple-element.60.refs_0_), channel_id=1, source_target_pairs={{0,104},{4,108},{8,112},{12,116},{16,120},{20,124},{24,96},{28,100... | collective-permute-start | bytes 786440 | tf_op jit(solution)/shard_map/ppermute | solution.py:483
  56.5 15.5 %collective-permute-start.11 = (bf16[64,2048]{1,0:T(8,128)(2,1)S(1)}, bf16[64,2048]{1,0:T(8,128)(2,1)S(1)}, u32[]{:S(2)}, u32[]{:S(2)}) collective-permute-start(bf16[64,2048]{1,0:T(8,128)(2,1)S(1)} %get-tuple-element.60.refs_0_), channel_id=1, source_target_pairs={{0,56},{4,60},{8,32},{12,36},{16,40},{20,44},{24,48},{28,52},{32,8... | collective-permute-start | bytes 786440 | tf_op jit(solution)/shard_map/ppermute | solution.py:483
  60.3 17.8 %collective-permute-start.10 = (bf16[64,2048]{1,0:T(8,128)(2,1)S(1)}, bf16[64,2048]{1,0:T(8,128)(2,1)S(1)}, u32[]{:S(2)}, u32[]{:S(2)}) collective-permute-start(bf16[64,2048]{1,0:T(8,128)(2,1)S(1)} %get-tuple-element.60.refs_0_), channel_id=1, source_target_pairs={{0,120},{4,124},{8,96},{12,100},{16,104},{20,108},{24,112},{28,116... | collective-permute-start | bytes 786440 | tf_op jit(solution)/shard_map/ppermute | solution.py:483
  70.7 11.4 %collective-permute-start.9 = (bf16[64,2048]{1,0:T(8,128)(2,1)S(1)}, bf16[64,2048]{1,0:T(8,128)(2,1)S(1)}, u32[]{:S(2)}, u32[]{:S(2)}) collective-permute-start(bf16[64,2048]{1,0:T(8,128)(2,1)S(1)} %get-tuple-element.60.refs_0_), channel_id=1, source_target_pairs={{0,40},{4,44},{8,48},{12,52},{16,56},{20,60},{24,32},{28,36},{32,7... | collective-permute-start | bytes 786440 | tf_op jit(solution)/shard_map/ppermute | solution.py:483
  91.8 10.3 %collective-permute-start.16 = (bf16[64,2048]{1,0:T(8,128)(2,1)S(1)}, bf16[64,2048]{1,0:T(8,128)(2,1)S(1)}, u32[]{:S(2)}, u32[]{:S(2)}) collective-permute-start(bf16[64,2048]{1,0:T(8,128)(2,1)S(1)} %get-tuple-element.70), channel_id=1, source_target_pairs={{0,120},{4,124},{8,96},{12,100},{16,104},{20,108},{24,112},{28,116... | collective-permute-start | bytes 786440 | tf_op jit(solution)/shard_map/ppermute | solution.py:483
  91.9 15.2 %collective-permute-start.17 = (bf16[64,2048]{1,0:T(8,128)(2,1)S(1)}, bf16[64,2048]{1,0:T(8,128)(2,1)S(1)}, u32[]{:S(2)}, u32[]{:S(2)}) collective-permute-start(bf16[64,2048]{1,0:T(8,128)(2,1)S(1)} %get-tuple-element.71), channel_id=1, source_target_pairs={{0,40},{4,44},{8,48},{12,52},{16,56},{20,60},{24,32},{28,36},{32,7... | collective-permute-start | bytes 786440 | tf_op jit(solution)/shard_map/ppermute | solution.py:483
  94.8 16.5 %collective-permute-start.18 = (bf16[64,2048]{1,0:T(8,128)(2,1)S(1)}, bf16[64,2048]{1,0:T(8,128)(2,1)S(1)}, u32[]{:S(2)}, u32[]{:S(2)}) collective-permute-start(bf16[64,2048]{1,0:T(8,128)(2,1)S(1)} %get-tuple-element.72), channel_id=1, source_target_pairs={{0,104},{4,108},{8,112},{12,116},{16,120},{20,124},{24,96},{28,100... | collective-permute-start | bytes 786440 | tf_op jit(solution)/shard_map/ppermute | solution.py:483
  96.4 21.6 %collective-permute-start.19 = (bf16[64,2048]{1,0:T(8,128)(2,1)S(1)}, bf16[64,2048]{1,0:T(8,128)(2,1)S(1)}, u32[]{:S(2)}, u32[]{:S(2)}) collective-permute-start(bf16[64,2048]{1,0:T(8,128)(2,1)S(1)} %get-tuple-element.73), channel_id=1, source_target_pairs={{0,56},{4,60},{8,32},{12,36},{16,40},{20,44},{24,48},{28,52},{32,8... | collective-permute-start | bytes 786440 | tf_op jit(solution)/shard_map/ppermute | solution.py:483
  98.9 19.1 %collective-permute-start.20 = (bf16[64,2048]{1,0:T(8,128)(2,1)S(1)}, bf16[64,2048]{1,0:T(8,128)(2,1)S(1)}, u32[]{:S(2)}, u32[]{:S(2)}) collective-permute-start(bf16[64,2048]{1,0:T(8,128)(2,1)S(1)} %get-tuple-element.74), channel_id=1, source_target_pairs={{0,64},{4,68},{8,72},{12,76},{16,80},{20,84},{24,88},{28,92},{32,9... | collective-permute-start | bytes 786440 | tf_op jit(solution)/shard_map/ppermute | solution.py:483
  102.1 17.8 %collective-permute-start.21 = (bf16[64,2048]{1,0:T(8,128)(2,1)S(1)}, bf16[64,2048]{1,0:T(8,128)(2,1)S(1)}, u32[]{:S(2)}, u32[]{:S(2)}) collective-permute-start(bf16[64,2048]{1,0:T(8,128)(2,1)S(1)} %get-tuple-element.75), channel_id=1, source_target_pairs={{0,16},{4,20},{8,24},{12,28},{16,0},{20,4},{24,8},{28,12},{32,48},... | collective-permute-start | bytes 786440 | tf_op jit(solution)/shard_map/ppermute | solution.py:483
  107.1 12.9 %collective-permute-start.22 = (bf16[64,2048]{1,0:T(8,128)(2,1)S(1)}, bf16[64,2048]{1,0:T(8,128)(2,1)S(1)}, u32[]{:S(2)}, u32[]{:S(2)}) collective-permute-start(bf16[64,2048]{1,0:T(8,128)(2,1)S(1)} %get-tuple-element.76), channel_id=1, source_target_pairs={{0,80},{4,84},{8,88},{12,92},{16,64},{20,68},{24,72},{28,76},{32,1... | collective-permute-start | bytes 786440 | tf_op jit(solution)/shard_map/ppermute | solution.py:483
  (8 other events, 78.7 us)

commit v5 on v4

--- a/solution.py
+++ b/solution.py
@@ -517,8 +517,8 @@
     freq = jnp.asarray(np.concatenate([freq, freq])[None, :])
     st = streams.reshape(SLOTS, DRAFT, NS, LT, 128).transpose(0, 1, 3, 2, 4).reshape(-1, 128)
     one, two = pack(w_gate, w_up, w_down)
-    one_z = send(one, lambda x, z, c: (x, z ^ 1, c))
-    two_x = send(two, lambda x, z, c: (x ^ 1, z, c))
+    one_z = send(one, lambda x, z, c: (x, z + 2 * c - 1, c))
+    two_x = send(two, lambda x, z, c: (x + 2 * c - 1, z, c))
     one_c, two_c = other_core(one), other_core(two)
     *out, own, kv = front(
         place,
@@ -538,16 +538,16 @@
         w_output,
     )
     turn = lambda v, k: lax.ppermute(v, "head", [(y, (y + k) % 4) for y in range(4)])
-    out, one_c, two_c = lax.optimization_barrier((out, one_c, two_c))
+    out, one_c, two_c, one_z, two_x = lax.optimization_barrier((out, one_c, two_c, one_z, two_x))
+    one_zc, two_xc = other_core(one_z), other_core(two_x)
     p1 = turn(out[1], 1)
     p3 = turn(out[3], 3)
     p2 = turn(out[2], 2)
-    p1, p2, p3, one_z, two_x = lax.optimization_barrier((p1, p2, p3, one_z, two_x))
-    weights = (one, two, one_c, two_c, one_z, two_x, other_core(one_z), other_core(two_x))
+    weights = (one, two, one_c, two_c, one_z, two_x, one_zc, two_xc)
     first, rows = mid(hc_in, hc_res, hc_out, [out[0], p1, p2, p3], own)
     rows, weights = lax.optimization_barrier((rows, weights))
     pieces = [rows] + [shift(rows, dx, dz) for dx, dz in OFFSETS]
-    sums = ffn(pieces, weights)
+    sums = ffn(pieces[:FIRST], weights) + ffn(pieces[FIRST:], weights)
     back = [sums[0]] + [shift(t, -dx, -dz) for t, (dx, dz) in zip(sums[1:], OFFSETS)]
     final = last(place, slot_owner, draft_len, hc_res, hc_out, first, back)
     new_streams = (

time: 123 us -> 125 us (1.016)
  waiting for transfers between devices: 54.8 us -> 47 us
  starting transfers between devices: 35.5 us -> 42.9 us
  Pallas kernels: 31.5 us -> 34.4 us
    ppermute x20, waiting for transfers between devices: 54.8 us -> 36.1 us  [send(): return lax.ppermute(v, 'req', pairs(move))]
    ppermute x3, waiting for transfers between devices: 0.01 us -> 10.9 us  [body(): lax.ppermute(v, 'head', [(y, (y + k) % 4) for y in range(4)])]
    ppermute x20, starting transfers between devices: 29.6 us -> 37.1 us  [send(): return lax.ppermute(v, 'req', pairs(move))]
    pallas_call x1 -> x2, Pallas kernels: 9.59 us -> 12.5 us  [ffn(): pl.pallas_call(functools.partial(ffn_kernel, n), name='ffn', out_shape=tu...]
  transfers between devices with their start and end apart: 23 -> 23, of which waited for: 14 -> 11; matrix products, arithmetic and copies ran while one was open for 0% -> 0% of each run, Pallas kernels for 14% -> 24%
where the time goes in v5:
time: 125 us
  waiting for transfers between devices  47 us (38%)
  starting transfers between devices  42.9 us (34%)
  Pallas kernels  34.4 us (28%)
    ppermute x20, starting transfers between devices, send(): return lax.ppermute(v, 'req', pairs(move))  37.1 us
    ppermute x20, waiting for transfers between devices, send(): return lax.ppermute(v, 'req', pairs(move))  36.1 us
    pallas_call x1, Pallas kernels, front(): pl.pallas_call(front_kernel, name='front', out_shape=(pltpu.VMEM((SLOTS *...  15 us
    pallas_call x2, Pallas kernels, ffn(): pl.pallas_call(functools.partial(ffn_kernel, n), name='ffn', out_shape=tu...  12.5 us
    ppermute x3, waiting for transfers between devices, body(): lax.ppermute(v, 'head', [(y, (y + k) % 4) for y in range(4)])  10.9 us
    ppermute x3, starting transfers between devices, body(): lax.ppermute(v, 'head', [(y, (y + k) % 4) for y in range(4)])  5.83 us
    pallas_call x1, Pallas kernels, last(): pl.pallas_call(last_kernel, name='last', out_shape=jax.ShapeDtypeStruct((...  2.88 us
  transfers between devices with their start and end apart: 23, of which 11 were waited for; matrix products, arithmetic and copies ran while one was open for 0% of the time, Pallas kernels for 24%

profile of v5, /device:TPU:0, one launch (start us, length us, event | category | flops | bytes accessed | tf_op | source)
XLA Modules:
  0.0 125.3 jit_solution(14308138729431111801)
XLA Ops:
  0.7 2.0 %pack.1 = (bf16[3072,256]{1,0:T(8,128)(2,1)S(1)}, bf16[3072,256]{1,0:T(8,128)(2,1)S(1)}) custom-call(bf16[2048,256]{1,0:T(8,128)(2,1)} %g.1, bf16[2048,256]{1,0:T(8,128)(2,1)} %u.1, bf16[256,2048]{1,0:T(8,128)(2,1)} %d.1), custom_call_target="tpu_custom_call" | custom-call | tf_op jit(solution)/shard_map/pack/pallas_call | solution.py:417
  2.7 4.2 %collective-permute-start.2 = (bf16[3072,256]{1,0:T(8,128)(2,1)S(1)}, bf16[3072,256]{1,0:T(8,128)(2,1)}, u32[]{:S(2)}, u32[]{:S(2)}) collective-permute-start(bf16[3072,256]{1,0:T(8,128)(2,1)S(1)} %get-tuple-element.55.refs_4_), channel_id=1, source_target_pairs={{0,24},{4,12},{8,0},{12,20},{16,8},{20,28},{24,16},{28,4},{32,56},... | collective-permute-start | bytes 4718600 | tf_op jit(solution)/shard_map/ppermute | solution.py:483
  6.9 2.8 %collective-permute-start.3 = (bf16[3072,256]{1,0:T(8,128)(2,1)S(1)}, bf16[3072,256]{1,0:T(8,128)(2,1)}, u32[]{:S(2)}, u32[]{:S(2)}) collective-permute-start(bf16[3072,256]{1,0:T(8,128)(2,1)S(1)} %get-tuple-element.56.refs_5_), channel_id=1, source_target_pairs={{0,96},{4,36},{8,104},{12,44},{16,112},{20,52},{24,120},{28,60},{3... | collective-permute-start | bytes 4718600 | tf_op jit(solution)/shard_map/ppermute | solution.py:483
  9.8 15.0 %front.1 = (bf16[64,2048]{1,0:T(8,128)(2,1)S(1)}, bf16[64,2048]{1,0:T(8,128)(2,1)S(1)}, bf16[64,2048]{1,0:T(8,128)(2,1)S(1)}, bf16[64,2048]{1,0:T(8,128)(2,1)S(1...) custom-call(s32[2]{0:T(128)S(1)} %pad_add_fusion.place, s32[128]{0:T(128)S(1)} %copy-done.4, ...), custom_call_target="tpu_custom_call" | custom-call | tf_op jit(solution)/shard_map/front/pallas_call | solution.py:254
  24.9 2.7 %collective-permute-done.3.refs_9_ = bf16[3072,256]{1,0:T(8,128)(2,1)} collective-permute-done((bf16[3072,256]{1,0:T(8,128)(2,1)S(1)}, bf16[3072,256]{1,0:T(8,128)(2,1)}, u32[]{:S(2)}, u32[]{:S(2)}) %collective-permute-start.3) | collective-permute-done | bytes 1572896 | tf_op jit(solution)/shard_map/ppermute | solution.py:483
  29.7 2.9 %collective-permute-start.5 = (bf16[64,2048]{1,0:T(8,128)(2,1)S(1)}, bf16[64,2048]{1,0:T(8,128)(2,1)S(1)}, u32[]{:S(2)}, u32[]{:S(2)}) collective-permute-start(bf16[64,2048]{1,0:T(8,128)(2,1)S(1)} %get-tuple-element.45), channel_id=1, source_target_pairs={{0,2},{1,3},{2,0},{3,1},{4,6},{5,7},{6,4},{7,5},{8,10},{9,11},{10,... | collective-permute-start | bytes 786440 | tf_op jit(solution)/shard_map/ppermute | solution.py:540
  33.9 4.1 %collective-permute-done.4.p1 = bf16[64,2048]{1,0:T(8,128)(2,1)S(1)} collective-permute-done((bf16[64,2048]{1,0:T(8,128)(2,1)S(1)}, bf16[64,2048]{1,0:T(8,128)(2,1)S(1)}, u32[]{:S(2)}, u32[]{:S(2)}) %collective-permute-start.4) | collective-permute-done | bytes 262176 | tf_op jit(solution)/shard_map/ppermute | solution.py:540
  38.0 6.8 %collective-permute-done.5.p2 = bf16[64,2048]{1,0:T(8,128)(2,1)S(1)} collective-permute-done((bf16[64,2048]{1,0:T(8,128)(2,1)S(1)}, bf16[64,2048]{1,0:T(8,128)(2,1)S(1)}, u32[]{:S(2)}, u32[]{:S(2)}) %collective-permute-start.5) | collective-permute-done | bytes 262176 | tf_op jit(solution)/shard_map/ppermute | solution.py:540
  44.8 2.0 %mid.1 = (bf16[4,64,2048]{2,1,0:T(8,128)(2,1)S(1)}, bf16[64,2048]{1,0:T(8,128)(2,1)S(1)}) custom-call(f32[2,4]{1,0:T(2,128)S(1)} %copy-done.2, f32[2,4,4]{2,1,0:T(4,128)S(1)} %copy-done.1, f32[2,4]{1,0:T(2,128)S(1)} %copy-done.3, bf16[64,2048]{1,0:T(8,128)(2,1)S(1)} %get-tuple-element.43.p0, bf16[64,2048]{1,0:T(8,128)(2,1)S(1)} %collective-permute-done.4.p1, ...), custom_call_target="tpu_custom_call" | custom-call | tf_op jit(solution)/shard_map/mid/pallas_call | solution.py:342
  46.9 3.1 %collective-permute-start.18 = (bf16[64,2048]{1,0:T(8,128)(2,1)S(1)}, bf16[64,2048]{1,0:T(8,128)(2,1)S(1)}, u32[]{:S(2)}, u32[]{:S(2)}) collective-permute-start(bf16[64,2048]{1,0:T(8,128)(2,1)S(1)} %get-tuple-element.54.refs_0_), channel_id=1, source_target_pairs={{0,80},{4,84},{8,88},{12,92},{16,64},{20,68},{24,72},{28,76},{32,1... | collective-permute-start | bytes 786440 | tf_op jit(solution)/shard_map/ppermute | solution.py:483
  50.0 2.5 %collective-permute-start.17 = (bf16[64,2048]{1,0:T(8,128)(2,1)S(1)}, bf16[64,2048]{1,0:T(8,128)(2,1)S(1)}, u32[]{:S(2)}, u32[]{:S(2)}) collective-permute-start(bf16[64,2048]{1,0:T(8,128)(2,1)S(1)} %get-tuple-element.54.refs_0_), channel_id=1, source_target_pairs={{0,16},{4,20},{8,24},{12,28},{16,0},{20,4},{24,8},{28,12},{32,48},... | collective-permute-start | bytes 786440 | tf_op jit(solution)/shard_map/ppermute | solution.py:483
  53.6 2.2 %collective-permute-start.15 = (bf16[64,2048]{1,0:T(8,128)(2,1)S(1)}, bf16[64,2048]{1,0:T(8,128)(2,1)S(1)}, u32[]{:S(2)}, u32[]{:S(2)}) collective-permute-start(bf16[64,2048]{1,0:T(8,128)(2,1)S(1)} %get-tuple-element.54.refs_0_), channel_id=1, source_target_pairs={{0,104},{4,108},{8,112},{12,116},{16,120},{20,124},{24,96},{28,100... | collective-permute-start | bytes 786440 | tf_op jit(solution)/shard_map/ppermute | solution.py:483
  57.8 2.5 %collective-permute-done.18.refs_3_ = bf16[64,2048]{1,0:T(8,128)(2,1)S(1)} collective-permute-done((bf16[64,2048]{1,0:T(8,128)(2,1)S(1)}, bf16[64,2048]{1,0:T(8,128)(2,1)S(1)}, u32[]{:S(2)}, u32[]{:S(2)}) %collective-permute-start.18) | collective-permute-done | bytes 262176 | tf_op jit(solution)/shard_map/ppermute | solution.py:483
  60.3 3.6 %collective-permute-start.10 = (bf16[64,2048]{1,0:T(8,128)(2,1)S(1)}, bf16[64,2048]{1,0:T(8,128)(2,1)S(1)}, u32[]{:S(2)}, u32[]{:S(2)}) collective-permute-start(bf16[64,2048]{1,0:T(8,128)(2,1)S(1)} %get-tuple-element.54.refs_0_), channel_id=1, source_target_pairs={{0,120},{4,124},{8,96},{12,100},{16,104},{20,108},{24,112},{28,116... | collective-permute-start | bytes 786440 | tf_op jit(solution)/shard_map/ppermute | solution.py:483
  63.9 2.7 %collective-permute-done.17.refs_2_ = bf16[64,2048]{1,0:T(8,128)(2,1)S(1)} collective-permute-done((bf16[64,2048]{1,0:T(8,128)(2,1)S(1)}, bf16[64,2048]{1,0:T(8,128)(2,1)S(1)}, u32[]{:S(2)}, u32[]{:S(2)}) %collective-permute-start.17) | collective-permute-done | bytes 262176 | tf_op jit(solution)/shard_map/ppermute | solution.py:483
  66.6 5.1 %collective-permute-done.15.refs_0_ = bf16[64,2048]{1,0:T(8,128)(2,1)S(1)} collective-permute-done((bf16[64,2048]{1,0:T(8,128)(2,1)S(1)}, bf16[64,2048]{1,0:T(8,128)(2,1)S(1)}, u32[]{:S(2)}, u32[]{:S(2)}) %collective-permute-start.15) | collective-permute-done | bytes 262176 | tf_op jit(solution)/shard_map/ppermute | solution.py:483
  71.6 6.3 %ffn.3 = (bf16[64,2048]{1,0:T(8,128)(2,1)S(1)}, bf16[64,2048]{1,0:T(8,128)(2,1)S(1)}, bf16[64,2048]{1,0:T(8,128)(2,1)S(1)}, bf16[64,2048]{1,0:T(8,128)(2,1)S(1)}) custom-call(bf16[64,2048]{1,0:T(8,128)(2,1)S(1)} %collective-permute-done.15.refs_0_, bf16[64,2048]{1,0:T(8,128)(2,1)S(1)} %collective-permute-done.16.refs_1_, ...), custom_call_target="tpu_custom_call" | custom-call | flops 3221225472 | bytes 2097152 | tf_op jit(solution)/shard_map/ffn/pallas_call | solution.py:455
  78.0 8.9 %collective-permute-start.20 = (bf16[64,2048]{1,0:T(8,128)(2,1)S(1)}, bf16[64,2048]{1,0:T(8,128)(2,1)S(1)}, u32[]{:S(2)}, u32[]{:S(2)}) collective-permute-start(bf16[64,2048]{1,0:T(8,128)(2,1)S(1)} %get-tuple-element.68), channel_id=1, source_target_pairs={{0,64},{4,68},{8,72},{12,76},{16,80},{20,84},{24,88},{28,92},{32,9... | collective-permute-start | bytes 786440 | tf_op jit(solution)/shard_map/ppermute | solution.py:483
  89.9 6.3 %ffn.2 = (bf16[64,2048]{1,0:T(8,128)(2,1)S(1)}, bf16[64,2048]{1,0:T(8,128)(2,1)S(1)}, bf16[64,2048]{1,0:T(8,128)(2,1)S(1)}, bf16[64,2048]{1,0:T(8,128)(2,1)S(1)}) custom-call(bf16[64,2048]{1,0:T(8,128)(2,1)S(1)} %get-tuple-element.54.refs_0_, bf16[64,2048]{1,0:T(8,128)(2,1)S(1)} %collective-permute-done.9.refs_1_, ...), custom_call_target="tpu_custom_call" | custom-call | flops 3221225472 | bytes 2097152 | tf_op jit(solution)/shard_map/ffn/pallas_call | solution.py:455
  96.2 3.1 %collective-permute-start.12 = (bf16[64,2048]{1,0:T(8,128)(2,1)S(1)}, bf16[64,2048]{1,0:T(8,128)(2,1)S(1)}, u32[]{:S(2)}, u32[]{:S(2)}) collective-permute-start(bf16[64,2048]{1,0:T(8,128)(2,1)S(1)} %get-tuple-element.64), channel_id=1, source_target_pairs={{0,120},{4,124},{8,96},{12,100},{16,104},{20,108},{24,112},{28,116... | collective-permute-start | bytes 786440 | tf_op jit(solution)/shard_map/ppermute | solution.py:483
  99.3 8.6 %collective-permute-done.19.refs_4_ = bf16[64,2048]{1,0:T(8,128)(2,1)S(1)} collective-permute-done((bf16[64,2048]{1,0:T(8,128)(2,1)S(1)}, bf16[64,2048]{1,0:T(8,128)(2,1)S(1)}, u32[]{:S(2)}, u32[]{:S(2)}) %collective-permute-start.19) | collective-permute-done | bytes 262176 | tf_op jit(solution)/shard_map/ppermute | solution.py:483
  108.0 3.6 %collective-permute-done.12.refs_1_ = bf16[64,2048]{1,0:T(8,128)(2,1)S(1)} collective-permute-done((bf16[64,2048]{1,0:T(8,128)(2,1)S(1)}, bf16[64,2048]{1,0:T(8,128)(2,1)S(1)}, u32[]{:S(2)}, u32[]{:S(2)}) %collective-permute-start.12) | collective-permute-done | bytes 262176 | tf_op jit(solution)/shard_map/ppermute | solution.py:483
  111.7 10.3 %collective-permute-done.13.refs_2_ = bf16[64,2048]{1,0:T(8,128)(2,1)S(1)} collective-permute-done((bf16[64,2048]{1,0:T(8,128)(2,1)S(1)}, bf16[64,2048]{1,0:T(8,128)(2,1)S(1)}, u32[]{:S(2)}, u32[]{:S(2)}) %collective-permute-start.13) | collective-permute-done | bytes 262176 | tf_op jit(solution)/shard_map/ppermute | solution.py:483
  122.4 2.9 %last.1 = bf16[4096,128]{1,0:T(8,128)(2,1)} custom-call(s32[2]{0:T(128)S(1)} %pad_add_fusion.place, s32[128]{0:T(128)S(1)} %copy-done.4, s32[128]{0:T(128)S(1)} %copy-done.5, f32[2,4,4]{2,1,0:T(4,128)S(1)} %copy-done.1, f32[2,4]{1,0:T(2,128)S(1)} %copy-done.3, bf16[4,64,2048]{2,1,0:T(8,128)(2,1)S(1)} %get-tuple-element.48.first, ...), custom_call_target="tpu_custom_call" | custom-call | tf_op jit(solution)/shard_map/last/pallas_call | solution.py:379
  (47 shorter events, 10.3 us)
Async XLA Ops:
  2.7 22.1 %collective-permute-start.2 = (bf16[3072,256]{1,0:T(8,128)(2,1)S(1)}, bf16[3072,256]{1,0:T(8,128)(2,1)}, u32[]{:S(2)}, u32[]{:S(2)}) collective-permute-start(bf16[3072,256]{1,0:T(8,128)(2,1)S(1)} %get-tuple-element.55.refs_4_), channel_id=1, source_target_pairs={{0,24},{4,12},{8,0},{12,20},{16,8},{20,28},{24,16},{28,4},{32,56},... | collective-permute-start | bytes 4718600 | tf_op jit(solution)/shard_map/ppermute | solution.py:483
  6.9 18.0 %collective-permute-start = (bf16[3072,256]{1,0:T(8,128)(2,1)S(1)}, bf16[3072,256]{1,0:T(8,128)(2,1)}, u32[]{:S(2)}, u32[]{:S(2)}) collective-permute-start(bf16[3072,256]{1,0:T(8,128)(2,1)S(1)} %get-tuple-element.55.refs_4_), channel_id=1, source_target_pairs={{0,4},{4,0},{8,12},{12,8},{16,20},{20,16},{24,28},{28,24},{32,36},... | collective-permute-start | bytes 4718600 | tf_op jit(solution)/shard_map/ppermute | solution.py:483
  6.9 20.7 %collective-permute-start.3 = (bf16[3072,256]{1,0:T(8,128)(2,1)S(1)}, bf16[3072,256]{1,0:T(8,128)(2,1)}, u32[]{:S(2)}, u32[]{:S(2)}) collective-permute-start(bf16[3072,256]{1,0:T(8,128)(2,1)S(1)} %get-tuple-element.56.refs_5_), channel_id=1, source_target_pairs={{0,96},{4,36},{8,104},{12,44},{16,112},{20,52},{24,120},{28,60},{3... | collective-permute-start | bytes 4718600 | tf_op jit(solution)/shard_map/ppermute | solution.py:483
  9.7 17.9 %collective-permute-start.1 = (bf16[3072,256]{1,0:T(8,128)(2,1)S(1)}, bf16[3072,256]{1,0:T(8,128)(2,1)}, u32[]{:S(2)}, u32[]{:S(2)}) collective-permute-start(bf16[3072,256]{1,0:T(8,128)(2,1)S(1)} %get-tuple-element.56.refs_5_), channel_id=1, source_target_pairs={{0,4},{4,0},{8,12},{12,8},{16,20},{20,16},{24,28},{28,24},{32,36},... | collective-permute-start | bytes 4718600 | tf_op jit(solution)/shard_map/ppermute | solution.py:483
  9.8 35.0 %copy-start.1 = (f32[2,4,4]{2,1,0:T(4,128)S(1)}, f32[2,4,4]{2,1,0:T(4,128)}, u32[]{:S(2)}) copy-start(f32[2,4,4]{2,1,0:T(4,128)} %hc_res.3) | copy-start | bytes 388
  27.6 19.2 %collective-permute-start.7 = (bf16[3072,256]{1,0:T(8,128)(2,1)}, bf16[3072,256]{1,0:T(8,128)(2,1)S(1)}, u32[]{:S(2)}, u32[]{:S(2)}) collective-permute-start(bf16[3072,256]{1,0:T(8,128)(2,1)} %collective-permute-done.2.refs_8_), channel_id=1, source_target_pairs={{0,4},{4,0},{8,12},{12,8},{16,20},{20,16},{24,28},{28,24},{32,36},... | collective-permute-start | bytes 4718600 | tf_op jit(solution)/shard_map/ppermute | solution.py:483
  28.0 18.9 %collective-permute-start.8 = (bf16[3072,256]{1,0:T(8,128)(2,1)}, bf16[3072,256]{1,0:T(8,128)(2,1)S(1)}, u32[]{:S(2)}, u32[]{:S(2)}) collective-permute-start(bf16[3072,256]{1,0:T(8,128)(2,1)} %collective-permute-done.3.refs_9_), channel_id=1, source_target_pairs={{0,4},{4,0},{8,12},{12,8},{16,20},{20,16},{24,28},{28,24},{32,36},... | collective-permute-start | bytes 4718600 | tf_op jit(solution)/shard_map/ppermute | solution.py:483
  28.1 9.9 %collective-permute-start.4 = (bf16[64,2048]{1,0:T(8,128)(2,1)S(1)}, bf16[64,2048]{1,0:T(8,128)(2,1)S(1)}, u32[]{:S(2)}, u32[]{:S(2)}) collective-permute-start(bf16[64,2048]{1,0:T(8,128)(2,1)S(1)} %get-tuple-element.44), channel_id=1, source_target_pairs={{0,1},{1,2},{2,3},{3,0},{4,5},{5,6},{6,7},{7,4},{8,9},{9,10},{10,1... | collective-permute-start | bytes 786440 | tf_op jit(solution)/shard_map/ppermute | solution.py:540
  29.7 15.1 %collective-permute-start.5 = (bf16[64,2048]{1,0:T(8,128)(2,1)S(1)}, bf16[64,2048]{1,0:T(8,128)(2,1)S(1)}, u32[]{:S(2)}, u32[]{:S(2)}) collective-permute-start(bf16[64,2048]{1,0:T(8,128)(2,1)S(1)} %get-tuple-element.45), channel_id=1, source_target_pairs={{0,2},{1,3},{2,0},{3,1},{4,6},{5,7},{6,4},{7,5},{8,10},{9,11},{10,... | collective-permute-start | bytes 786440 | tf_op jit(solution)/shard_map/ppermute | solution.py:540
  32.6 12.2 %collective-permute-start.6 = (bf16[64,2048]{1,0:T(8,128)(2,1)S(1)}, bf16[64,2048]{1,0:T(8,128)(2,1)S(1)}, u32[]{:S(2)}, u32[]{:S(2)}) collective-permute-start(bf16[64,2048]{1,0:T(8,128)(2,1)S(1)} %get-tuple-element.46), channel_id=1, source_target_pairs={{0,3},{1,0},{2,1},{3,2},{4,7},{5,4},{6,5},{7,6},{8,11},{9,8},{10,9... | collective-permute-start | bytes 786440 | tf_op jit(solution)/shard_map/ppermute | solution.py:540
  46.9 13.4 %collective-permute-start.18 = (bf16[64,2048]{1,0:T(8,128)(2,1)S(1)}, bf16[64,2048]{1,0:T(8,128)(2,1)S(1)}, u32[]{:S(2)}, u32[]{:S(2)}) collective-permute-start(bf16[64,2048]{1,0:T(8,128)(2,1)S(1)} %get-tuple-element.54.refs_0_), channel_id=1, source_target_pairs={{0,80},{4,84},{8,88},{12,92},{16,64},{20,68},{24,72},{28,76},{32,1... | collective-permute-start | bytes 786440 | tf_op jit(solution)/shard_map/ppermute | solution.py:483
  50.0 16.6 %collective-permute-start.17 = (bf16[64,2048]{1,0:T(8,128)(2,1)S(1)}, bf16[64,2048]{1,0:T(8,128)(2,1)S(1)}, u32[]{:S(2)}, u32[]{:S(2)}) collective-permute-start(bf16[64,2048]{1,0:T(8,128)(2,1)S(1)} %get-tuple-element.54.refs_0_), channel_id=1, source_target_pairs={{0,16},{4,20},{8,24},{12,28},{16,0},{20,4},{24,8},{28,12},{32,48},... | collective-permute-start | bytes 786440 | tf_op jit(solution)/shard_map/ppermute | solution.py:483
  52.5 14.1 %collective-permute-start.16 = (bf16[64,2048]{1,0:T(8,128)(2,1)S(1)}, bf16[64,2048]{1,0:T(8,128)(2,1)S(1)}, u32[]{:S(2)}, u32[]{:S(2)}) collective-permute-start(bf16[64,2048]{1,0:T(8,128)(2,1)S(1)} %get-tuple-element.54.refs_0_), channel_id=1, source_target_pairs={{0,64},{4,68},{8,72},{12,76},{16,80},{20,84},{24,88},{28,92},{32,9... | collective-permute-start | bytes 786440 | tf_op jit(solution)/shard_map/ppermute | solution.py:483
  53.6 18.0 %collective-permute-start.15 = (bf16[64,2048]{1,0:T(8,128)(2,1)S(1)}, bf16[64,2048]{1,0:T(8,128)(2,1)S(1)}, u32[]{:S(2)}, u32[]{:S(2)}) collective-permute-start(bf16[64,2048]{1,0:T(8,128)(2,1)S(1)} %get-tuple-element.54.refs_0_), channel_id=1, source_target_pairs={{0,104},{4,108},{8,112},{12,116},{16,120},{20,124},{24,96},{28,100... | collective-permute-start | bytes 786440 | tf_op jit(solution)/shard_map/ppermute | solution.py:483
  55.8 31.1 %collective-permute-start.11 = (bf16[64,2048]{1,0:T(8,128)(2,1)S(1)}, bf16[64,2048]{1,0:T(8,128)(2,1)S(1)}, u32[]{:S(2)}, u32[]{:S(2)}) collective-permute-start(bf16[64,2048]{1,0:T(8,128)(2,1)S(1)} %get-tuple-element.54.refs_0_), channel_id=1, source_target_pairs={{0,56},{4,60},{8,32},{12,36},{16,40},{20,44},{24,48},{28,52},{32,8... | collective-permute-start | bytes 786440 | tf_op jit(solution)/shard_map/ppermute | solution.py:483
  60.3 28.5 %collective-permute-start.10 = (bf16[64,2048]{1,0:T(8,128)(2,1)S(1)}, bf16[64,2048]{1,0:T(8,128)(2,1)S(1)}, u32[]{:S(2)}, u32[]{:S(2)}) collective-permute-start(bf16[64,2048]{1,0:T(8,128)(2,1)S(1)} %get-tuple-element.54.refs_0_), channel_id=1, source_target_pairs={{0,120},{4,124},{8,96},{12,100},{16,104},{20,108},{24,112},{28,116... | collective-permute-start | bytes 786440 | tf_op jit(solution)/shard_map/ppermute | solution.py:483
  66.6 23.3 %collective-permute-start.9 = (bf16[64,2048]{1,0:T(8,128)(2,1)S(1)}, bf16[64,2048]{1,0:T(8,128)(2,1)S(1)}, u32[]{:S(2)}, u32[]{:S(2)}) collective-permute-start(bf16[64,2048]{1,0:T(8,128)(2,1)S(1)} %get-tuple-element.54.refs_0_), channel_id=1, source_target_pairs={{0,40},{4,44},{8,48},{12,52},{16,56},{20,60},{24,32},{28,36},{32,7... | collective-permute-start | bytes 786440 | tf_op jit(solution)/shard_map/ppermute | solution.py:483
  77.9 30.0 %collective-permute-start.19 = (bf16[64,2048]{1,0:T(8,128)(2,1)S(1)}, bf16[64,2048]{1,0:T(8,128)(2,1)S(1)}, u32[]{:S(2)}, u32[]{:S(2)}) collective-permute-start(bf16[64,2048]{1,0:T(8,128)(2,1)S(1)} %get-tuple-element.67), channel_id=1, source_target_pairs={{0,56},{4,60},{8,32},{12,36},{16,40},{20,44},{24,48},{28,52},{32,8... | collective-permute-start | bytes 786440 | tf_op jit(solution)/shard_map/ppermute | solution.py:483
  78.0 29.9 %collective-permute-start.20 = (bf16[64,2048]{1,0:T(8,128)(2,1)S(1)}, bf16[64,2048]{1,0:T(8,128)(2,1)S(1)}, u32[]{:S(2)}, u32[]{:S(2)}) collective-permute-start(bf16[64,2048]{1,0:T(8,128)(2,1)S(1)} %get-tuple-element.68), channel_id=1, source_target_pairs={{0,64},{4,68},{8,72},{12,76},{16,80},{20,84},{24,88},{28,92},{32,9... | collective-permute-start | bytes 786440 | tf_op jit(solution)/shard_map/ppermute | solution.py:483
  86.9 21.1 %collective-permute-start.21 = (bf16[64,2048]{1,0:T(8,128)(2,1)S(1)}, bf16[64,2048]{1,0:T(8,128)(2,1)S(1)}, u32[]{:S(2)}, u32[]{:S(2)}) collective-permute-start(bf16[64,2048]{1,0:T(8,128)(2,1)S(1)} %get-tuple-element.69), channel_id=1, source_target_pairs={{0,16},{4,20},{8,24},{12,28},{16,0},{20,4},{24,8},{28,12},{32,48},... | collective-permute-start | bytes 786440 | tf_op jit(solution)/shard_map/ppermute | solution.py:483
  88.8 19.2 %collective-permute-start.22 = (bf16[64,2048]{1,0:T(8,128)(2,1)S(1)}, bf16[64,2048]{1,0:T(8,128)(2,1)S(1)}, u32[]{:S(2)}, u32[]{:S(2)}) collective-permute-start(bf16[64,2048]{1,0:T(8,128)(2,1)S(1)} %get-tuple-element.70), channel_id=1, source_target_pairs={{0,80},{4,84},{8,88},{12,92},{16,64},{20,68},{24,72},{28,76},{32,1... | collective-permute-start | bytes 786440 | tf_op jit(solution)/shard_map/ppermute | solution.py:483
  96.2 15.5 %collective-permute-start.12 = (bf16[64,2048]{1,0:T(8,128)(2,1)S(1)}, bf16[64,2048]{1,0:T(8,128)(2,1)S(1)}, u32[]{:S(2)}, u32[]{:S(2)}) collective-permute-start(bf16[64,2048]{1,0:T(8,128)(2,1)S(1)} %get-tuple-element.64), channel_id=1, source_target_pairs={{0,120},{4,124},{8,96},{12,100},{16,104},{20,108},{24,112},{28,116... | collective-permute-start | bytes 786440 | tf_op jit(solution)/shard_map/ppermute | solution.py:483
  107.9 14.0 %collective-permute-start.13 = (bf16[64,2048]{1,0:T(8,128)(2,1)S(1)}, bf16[64,2048]{1,0:T(8,128)(2,1)S(1)}, u32[]{:S(2)}, u32[]{:S(2)}) collective-permute-start(bf16[64,2048]{1,0:T(8,128)(2,1)S(1)} %get-tuple-element.65), channel_id=1, source_target_pairs={{0,40},{4,44},{8,48},{12,52},{16,56},{20,60},{24,32},{28,36},{32,7... | collective-permute-start | bytes 786440 | tf_op jit(solution)/shard_map/ppermute | solution.py:483
  107.9 14.5 %collective-permute-start.14 = (bf16[64,2048]{1,0:T(8,128)(2,1)S(1)}, bf16[64,2048]{1,0:T(8,128)(2,1)S(1)}, u32[]{:S(2)}, u32[]{:S(2)}) collective-permute-start(bf16[64,2048]{1,0:T(8,128)(2,1)S(1)} %get-tuple-element.66), channel_id=1, source_target_pairs={{0,104},{4,108},{8,112},{12,116},{16,120},{20,124},{24,96},{28,100... | collective-permute-start | bytes 786440 | tf_op jit(solution)/shard_map/ppermute | solution.py:483
  (8 other events, 98.7 us)

commit v6 on v5

--- a/solution.py
+++ b/solution.py
@@ -294,7 +294,7 @@
                 pltpu.SemaphoreType.DMA((2, 6)),
             ],
         ),
-        compiler_params=pltpu.CompilerParams(vmem_limit_bytes=40 * 2**20),
+        compiler_params=pltpu.CompilerParams(vmem_limit_bytes=29 * 2**20),
     )(
         place,
         owner,
@@ -427,7 +427,11 @@
 
 def ffn_kernel(n, *refs):
     xs, ws, ys = refs[:n], refs[n : n + BLOCKS], refs[n + BLOCKS : 2 * n + BLOCKS]
-    cat, inner = refs[2 * n + BLOCKS :]
+    cat, inner, wbuf, sems = refs[2 * n + BLOCKS :]
+    copies = [pltpu.make_async_copy(ws[4 + k], wbuf.at[k], sems.at[k]) for k in range(4)]
+    for c in copies:
+        c.start()
+    ws = list(ws[:4]) + [wbuf.at[k] for k in range(4)]
     rows = SLOTS * Q
     for k, x in enumerate(xs):
         cat[k * rows : (k + 1) * rows, :] = x[...]
@@ -435,6 +439,8 @@
     spans = [(o, min(o + step, n * rows)) for o in range(0, n * rows, step)]
     for lo, hi in spans:
         for k, w in enumerate(ws):
+            if k >= 4 and lo == 0:
+                copies[k - 4].wait()
             both = mm(cat[lo:hi, :], w[:D, :])
             gate = both[:, :128]
             inner[lo:hi, k * 128 : (k + 1) * 128] = (
@@ -456,17 +462,22 @@
         functools.partial(ffn_kernel, n),
         name="ffn",
         out_shape=tuple(pltpu.VMEM((SLOTS * Q, D), BF) for _ in xs),
-        in_specs=[vmem] * (n + BLOCKS),
+        in_specs=[vmem] * (n + 4) + [pl.BlockSpec(memory_space=pltpu.HBM)] * 4,
         out_specs=tuple([vmem] * n),
         scratch_shapes=[
             pltpu.VMEM((rows, D), BF),
             pltpu.VMEM((rows, 128 * BLOCKS), BF),
+            pltpu.VMEM((4, PACKED, 256), BF),
+            pltpu.SemaphoreType.DMA((4,)),
         ],
         cost_estimate=pl.CostEstimate(
             flops=rows * D * 1024 * 6, transcendentals=rows * 1024, bytes_accessed=rows * D * 4
         ),
         compiler_params=pltpu.CompilerParams(vmem_limit_bytes=24 * 2**20),
-    )(*[near(x) for x in xs], *[near(w) for w in weights])
+    )(
+        *[near(x) for x in list(xs) + list(weights[:4])],
+        *[pltpu.with_memory_space_constraint(w, pltpu.HBM) for w in weights[4:]],
+    )
 
 
 def pairs(move):
@@ -543,7 +554,7 @@
     p1 = turn(out[1], 1)
     p3 = turn(out[3], 3)
     p2 = turn(out[2], 2)
-    weights = (one, two, one_c, two_c, one_z, two_x, one_zc, two_xc)
+    weights = (one, two, one_zc, two_xc, one_c, two_c, one_z, two_x)
     first, rows = mid(hc_in, hc_res, hc_out, [out[0], p1, p2, p3], own)
     rows, weights = lax.optimization_barrier((rows, weights))
     pieces = [rows] + [shift(rows, dx, dz) for dx, dz in OFFSETS]

time: 125 us -> 125 us (level)
  transfers between devices with their start and end apart: 23 -> 23, of which waited for: 11 -> 11; matrix products, arithmetic and copies ran while one was open for 0% -> 0% of each run, Pallas kernels for 24% -> 23%
where the time goes in v6:
time: 125 us
  waiting for transfers between devices  47.3 us (38%)
  starting transfers between devices  42.9 us (34%)
  Pallas kernels  33.8 us (27%)
    ppermute x20, starting transfers between devices, send(): return lax.ppermute(v, 'req', pairs(move))  37.1 us
    ppermute x20, waiting for transfers between devices, send(): return lax.ppermute(v, 'req', pairs(move))  36.4 us
    pallas_call x1, Pallas kernels, front(): pl.pallas_call(front_kernel, name='front', out_shape=(pltpu.VMEM((SLOTS *...  15 us
    pallas_call x2, Pallas kernels, ffn(): pl.pallas_call(functools.partial(ffn_kernel, n), name='ffn', out_shape=tu...  11.9 us
    ppermute x3, waiting for transfers between devices, body(): lax.ppermute(v, 'head', [(y, (y + k) % 4) for y in range(4)])  10.9 us
    ppermute x3, starting transfers between devices, body(): lax.ppermute(v, 'head', [(y, (y + k) % 4) for y in range(4)])  5.83 us
    pallas_call x1, Pallas kernels, last(): pl.pallas_call(last_kernel, name='last', out_shape=jax.ShapeDtypeStruct((...  2.88 us
  transfers between devices with their start and end apart: 23, of which 11 were waited for; matrix products, arithmetic and copies ran while one was open for 0% of the time, Pallas kernels for 23%

profile of v6, /device:TPU:0, one launch (start us, length us, event | category | flops | bytes accessed | tf_op | source)
XLA Modules:
  0.0 125.0 jit_solution(12909034228575908486)
XLA Ops:
  0.7 2.0 %pack.1 = (bf16[3072,256]{1,0:T(8,128)(2,1)S(1)}, bf16[3072,256]{1,0:T(8,128)(2,1)S(1)}) custom-call(bf16[2048,256]{1,0:T(8,128)(2,1)} %g.1, bf16[2048,256]{1,0:T(8,128)(2,1)} %u.1, bf16[256,2048]{1,0:T(8,128)(2,1)} %d.1), custom_call_target="tpu_custom_call" | custom-call | tf_op jit(solution)/shard_map/pack/pallas_call | solution.py:417
  2.7 4.2 %collective-permute-start.2 = (bf16[3072,256]{1,0:T(8,128)(2,1)S(1)}, bf16[3072,256]{1,0:T(8,128)(2,1)}, u32[]{:S(2)}, u32[]{:S(2)}) collective-permute-start(bf16[3072,256]{1,0:T(8,128)(2,1)S(1)} %get-tuple-element.55.refs_4_), channel_id=1, source_target_pairs={{0,24},{4,12},{8,0},{12,20},{16,8},{20,28},{24,16},{28,4},{32,56},... | collective-permute-start | bytes 4718600 | tf_op jit(solution)/shard_map/ppermute | solution.py:494
  6.9 2.8 %collective-permute-start.3 = (bf16[3072,256]{1,0:T(8,128)(2,1)S(1)}, bf16[3072,256]{1,0:T(8,128)(2,1)}, u32[]{:S(2)}, u32[]{:S(2)}) collective-permute-start(bf16[3072,256]{1,0:T(8,128)(2,1)S(1)} %get-tuple-element.56.refs_5_), channel_id=1, source_target_pairs={{0,96},{4,36},{8,104},{12,44},{16,112},{20,52},{24,120},{28,60},{3... | collective-permute-start | bytes 4718600 | tf_op jit(solution)/shard_map/ppermute | solution.py:494
  9.8 15.0 %front.1 = (bf16[64,2048]{1,0:T(8,128)(2,1)S(1)}, bf16[64,2048]{1,0:T(8,128)(2,1)S(1)}, bf16[64,2048]{1,0:T(8,128)(2,1)S(1)}, bf16[64,2048]{1,0:T(8,128)(2,1)S(1...) custom-call(s32[2]{0:T(128)S(1)} %pad_add_fusion.place, s32[128]{0:T(128)S(1)} %copy-done.4, ...), custom_call_target="tpu_custom_call" | custom-call | tf_op jit(solution)/shard_map/front/pallas_call | solution.py:254
  24.9 2.7 %collective-permute-done.3.refs_11_ = bf16[3072,256]{1,0:T(8,128)(2,1)} collective-permute-done((bf16[3072,256]{1,0:T(8,128)(2,1)S(1)}, bf16[3072,256]{1,0:T(8,128)(2,1)}, u32[]{:S(2)}, u32[]{:S(2)}) %collective-permute-start.3) | collective-permute-done | bytes 1572896 | tf_op jit(solution)/shard_map/ppermute | solution.py:494
  29.7 2.9 %collective-permute-start.5 = (bf16[64,2048]{1,0:T(8,128)(2,1)S(1)}, bf16[64,2048]{1,0:T(8,128)(2,1)S(1)}, u32[]{:S(2)}, u32[]{:S(2)}) collective-permute-start(bf16[64,2048]{1,0:T(8,128)(2,1)S(1)} %get-tuple-element.45), channel_id=1, source_target_pairs={{0,2},{1,3},{2,0},{3,1},{4,6},{5,7},{6,4},{7,5},{8,10},{9,11},{10,... | collective-permute-start | bytes 786440 | tf_op jit(solution)/shard_map/ppermute | solution.py:551
  33.9 4.1 %collective-permute-done.4.p1 = bf16[64,2048]{1,0:T(8,128)(2,1)S(1)} collective-permute-done((bf16[64,2048]{1,0:T(8,128)(2,1)S(1)}, bf16[64,2048]{1,0:T(8,128)(2,1)S(1)}, u32[]{:S(2)}, u32[]{:S(2)}) %collective-permute-start.4) | collective-permute-done | bytes 262176 | tf_op jit(solution)/shard_map/ppermute | solution.py:551
  38.0 6.8 %collective-permute-done.5.p2 = bf16[64,2048]{1,0:T(8,128)(2,1)S(1)} collective-permute-done((bf16[64,2048]{1,0:T(8,128)(2,1)S(1)}, bf16[64,2048]{1,0:T(8,128)(2,1)S(1)}, u32[]{:S(2)}, u32[]{:S(2)}) %collective-permute-start.5) | collective-permute-done | bytes 262176 | tf_op jit(solution)/shard_map/ppermute | solution.py:551
  44.8 2.0 %mid.1 = (bf16[4,64,2048]{2,1,0:T(8,128)(2,1)S(1)}, bf16[64,2048]{1,0:T(8,128)(2,1)S(1)}) custom-call(f32[2,4]{1,0:T(2,128)S(1)} %copy-done.2, f32[2,4,4]{2,1,0:T(4,128)S(1)} %copy-done.1, f32[2,4]{1,0:T(2,128)S(1)} %copy-done.3, bf16[64,2048]{1,0:T(8,128)(2,1)S(1)} %get-tuple-element.43.p0, bf16[64,2048]{1,0:T(8,128)(2,1)S(1)} %collective-permute-done.4.p1, ...), custom_call_target="tpu_custom_call" | custom-call | tf_op jit(solution)/shard_map/mid/pallas_call | solution.py:342
  46.9 3.1 %collective-permute-start.18 = (bf16[64,2048]{1,0:T(8,128)(2,1)S(1)}, bf16[64,2048]{1,0:T(8,128)(2,1)S(1)}, u32[]{:S(2)}, u32[]{:S(2)}) collective-permute-start(bf16[64,2048]{1,0:T(8,128)(2,1)S(1)} %get-tuple-element.54.refs_0_), channel_id=1, source_target_pairs={{0,80},{4,84},{8,88},{12,92},{16,64},{20,68},{24,72},{28,76},{32,1... | collective-permute-start | bytes 786440 | tf_op jit(solution)/shard_map/ppermute | solution.py:494
  50.0 2.5 %collective-permute-start.17 = (bf16[64,2048]{1,0:T(8,128)(2,1)S(1)}, bf16[64,2048]{1,0:T(8,128)(2,1)S(1)}, u32[]{:S(2)}, u32[]{:S(2)}) collective-permute-start(bf16[64,2048]{1,0:T(8,128)(2,1)S(1)} %get-tuple-element.54.refs_0_), channel_id=1, source_target_pairs={{0,16},{4,20},{8,24},{12,28},{16,0},{20,4},{24,8},{28,12},{32,48},... | collective-permute-start | bytes 786440 | tf_op jit(solution)/shard_map/ppermute | solution.py:494
  53.6 2.2 %collective-permute-start.15 = (bf16[64,2048]{1,0:T(8,128)(2,1)S(1)}, bf16[64,2048]{1,0:T(8,128)(2,1)S(1)}, u32[]{:S(2)}, u32[]{:S(2)}) collective-permute-start(bf16[64,2048]{1,0:T(8,128)(2,1)S(1)} %get-tuple-element.54.refs_0_), channel_id=1, source_target_pairs={{0,104},{4,108},{8,112},{12,116},{16,120},{20,124},{24,96},{28,100... | collective-permute-start | bytes 786440 | tf_op jit(solution)/shard_map/ppermute | solution.py:494
  57.8 2.5 %collective-permute-done.18.refs_3_ = bf16[64,2048]{1,0:T(8,128)(2,1)S(1)} collective-permute-done((bf16[64,2048]{1,0:T(8,128)(2,1)S(1)}, bf16[64,2048]{1,0:T(8,128)(2,1)S(1)}, u32[]{:S(2)}, u32[]{:S(2)}) %collective-permute-start.18) | collective-permute-done | bytes 262176 | tf_op jit(solution)/shard_map/ppermute | solution.py:494
  60.3 3.6 %collective-permute-start.10 = (bf16[64,2048]{1,0:T(8,128)(2,1)S(1)}, bf16[64,2048]{1,0:T(8,128)(2,1)S(1)}, u32[]{:S(2)}, u32[]{:S(2)}) collective-permute-start(bf16[64,2048]{1,0:T(8,128)(2,1)S(1)} %get-tuple-element.54.refs_0_), channel_id=1, source_target_pairs={{0,120},{4,124},{8,96},{12,100},{16,104},{20,108},{24,112},{28,116... | collective-permute-start | bytes 786440 | tf_op jit(solution)/shard_map/ppermute | solution.py:494
  63.9 2.7 %collective-permute-done.17.refs_2_ = bf16[64,2048]{1,0:T(8,128)(2,1)S(1)} collective-permute-done((bf16[64,2048]{1,0:T(8,128)(2,1)S(1)}, bf16[64,2048]{1,0:T(8,128)(2,1)S(1)}, u32[]{:S(2)}, u32[]{:S(2)}) %collective-permute-start.17) | collective-permute-done | bytes 262176 | tf_op jit(solution)/shard_map/ppermute | solution.py:494
  66.6 5.1 %collective-permute-done.15.refs_0_ = bf16[64,2048]{1,0:T(8,128)(2,1)S(1)} collective-permute-done((bf16[64,2048]{1,0:T(8,128)(2,1)S(1)}, bf16[64,2048]{1,0:T(8,128)(2,1)S(1)}, u32[]{:S(2)}, u32[]{:S(2)}) %collective-permute-start.15) | collective-permute-done | bytes 262176 | tf_op jit(solution)/shard_map/ppermute | solution.py:494
  71.6 5.9 %ffn.3 = (bf16[64,2048]{1,0:T(8,128)(2,1)S(1)}, bf16[64,2048]{1,0:T(8,128)(2,1)S(1)}, bf16[64,2048]{1,0:T(8,128)(2,1)S(1)}, bf16[64,2048]{1,0:T(8,128)(2,1)S(1)}) custom-call(bf16[64,2048]{1,0:T(8,128)(2,1)S(1)} %collective-permute-done.15.refs_0_, bf16[64,2048]{1,0:T(8,128)(2,1)S(1)} %collective-permute-done.16.refs_1_, ...), custom_call_target="tpu_custom_call" | custom-call | flops 3221225472 | bytes 2097152 | tf_op jit(solution)/shard_map/ffn/pallas_call | solution.py:461
  77.7 8.9 %collective-permute-start.20 = (bf16[64,2048]{1,0:T(8,128)(2,1)S(1)}, bf16[64,2048]{1,0:T(8,128)(2,1)S(1)}, u32[]{:S(2)}, u32[]{:S(2)}) collective-permute-start(bf16[64,2048]{1,0:T(8,128)(2,1)S(1)} %get-tuple-element.68), channel_id=1, source_target_pairs={{0,64},{4,68},{8,72},{12,76},{16,80},{20,84},{24,88},{28,92},{32,9... | collective-permute-start | bytes 786440 | tf_op jit(solution)/shard_map/ppermute | solution.py:494
  89.6 5.9 %ffn.2 = (bf16[64,2048]{1,0:T(8,128)(2,1)S(1)}, bf16[64,2048]{1,0:T(8,128)(2,1)S(1)}, bf16[64,2048]{1,0:T(8,128)(2,1)S(1)}, bf16[64,2048]{1,0:T(8,128)(2,1)S(1)}) custom-call(bf16[64,2048]{1,0:T(8,128)(2,1)S(1)} %get-tuple-element.54.refs_0_, bf16[64,2048]{1,0:T(8,128)(2,1)S(1)} %collective-permute-done.9.refs_1_, ...), custom_call_target="tpu_custom_call" | custom-call | flops 3221225472 | bytes 2097152 | tf_op jit(solution)/shard_map/ffn/pallas_call | solution.py:461
  95.6 3.1 %collective-permute-start.12 = (bf16[64,2048]{1,0:T(8,128)(2,1)S(1)}, bf16[64,2048]{1,0:T(8,128)(2,1)S(1)}, u32[]{:S(2)}, u32[]{:S(2)}) collective-permute-start(bf16[64,2048]{1,0:T(8,128)(2,1)S(1)} %get-tuple-element.64), channel_id=1, source_target_pairs={{0,120},{4,124},{8,96},{12,100},{16,104},{20,108},{24,112},{28,116... | collective-permute-start | bytes 786440 | tf_op jit(solution)/shard_map/ppermute | solution.py:494
  98.7 8.9 %collective-permute-done.19.refs_4_ = bf16[64,2048]{1,0:T(8,128)(2,1)S(1)} collective-permute-done((bf16[64,2048]{1,0:T(8,128)(2,1)S(1)}, bf16[64,2048]{1,0:T(8,128)(2,1)S(1)}, u32[]{:S(2)}, u32[]{:S(2)}) %collective-permute-start.19) | collective-permute-done | bytes 262176 | tf_op jit(solution)/shard_map/ppermute | solution.py:494
  107.8 3.4 %collective-permute-done.12.refs_1_ = bf16[64,2048]{1,0:T(8,128)(2,1)S(1)} collective-permute-done((bf16[64,2048]{1,0:T(8,128)(2,1)S(1)}, bf16[64,2048]{1,0:T(8,128)(2,1)S(1)}, u32[]{:S(2)}, u32[]{:S(2)}) %collective-permute-start.12) | collective-permute-done | bytes 262176 | tf_op jit(solution)/shard_map/ppermute | solution.py:494
  111.2 10.4 %collective-permute-done.13.refs_2_ = bf16[64,2048]{1,0:T(8,128)(2,1)S(1)} collective-permute-done((bf16[64,2048]{1,0:T(8,128)(2,1)S(1)}, bf16[64,2048]{1,0:T(8,128)(2,1)S(1)}, u32[]{:S(2)}, u32[]{:S(2)}) %collective-permute-start.13) | collective-permute-done | bytes 262176 | tf_op jit(solution)/shard_map/ppermute | solution.py:494
  122.1 2.9 %last.1 = bf16[4096,128]{1,0:T(8,128)(2,1)} custom-call(s32[2]{0:T(128)S(1)} %pad_add_fusion.place, s32[128]{0:T(128)S(1)} %copy-done.4, s32[128]{0:T(128)S(1)} %copy-done.5, f32[2,4,4]{2,1,0:T(4,128)S(1)} %copy-done.1, f32[2,4]{1,0:T(2,128)S(1)} %copy-done.3, bf16[4,64,2048]{2,1,0:T(8,128)(2,1)S(1)} %get-tuple-element.48.first, ...), custom_call_target="tpu_custom_call" | custom-call | tf_op jit(solution)/shard_map/last/pallas_call | solution.py:379
  (47 shorter events, 10.4 us)
Async XLA Ops:
  2.7 22.1 %collective-permute-start.2 = (bf16[3072,256]{1,0:T(8,128)(2,1)S(1)}, bf16[3072,256]{1,0:T(8,128)(2,1)}, u32[]{:S(2)}, u32[]{:S(2)}) collective-permute-start(bf16[3072,256]{1,0:T(8,128)(2,1)S(1)} %get-tuple-element.55.refs_4_), channel_id=1, source_target_pairs={{0,24},{4,12},{8,0},{12,20},{16,8},{20,28},{24,16},{28,4},{32,56},... | collective-permute-start | bytes 4718600 | tf_op jit(solution)/shard_map/ppermute | solution.py:494
  6.9 18.0 %collective-permute-start = (bf16[3072,256]{1,0:T(8,128)(2,1)S(1)}, bf16[3072,256]{1,0:T(8,128)(2,1)}, u32[]{:S(2)}, u32[]{:S(2)}) collective-permute-start(bf16[3072,256]{1,0:T(8,128)(2,1)S(1)} %get-tuple-element.55.refs_4_), channel_id=1, source_target_pairs={{0,4},{4,0},{8,12},{12,8},{16,20},{20,16},{24,28},{28,24},{32,36},... | collective-permute-start | bytes 4718600 | tf_op jit(solution)/shard_map/ppermute | solution.py:494
  6.9 20.7 %collective-permute-start.3 = (bf16[3072,256]{1,0:T(8,128)(2,1)S(1)}, bf16[3072,256]{1,0:T(8,128)(2,1)}, u32[]{:S(2)}, u32[]{:S(2)}) collective-permute-start(bf16[3072,256]{1,0:T(8,128)(2,1)S(1)} %get-tuple-element.56.refs_5_), channel_id=1, source_target_pairs={{0,96},{4,36},{8,104},{12,44},{16,112},{20,52},{24,120},{28,60},{3... | collective-permute-start | bytes 4718600 | tf_op jit(solution)/shard_map/ppermute | solution.py:494
  9.7 17.9 %collective-permute-start.1 = (bf16[3072,256]{1,0:T(8,128)(2,1)S(1)}, bf16[3072,256]{1,0:T(8,128)(2,1)}, u32[]{:S(2)}, u32[]{:S(2)}) collective-permute-start(bf16[3072,256]{1,0:T(8,128)(2,1)S(1)} %get-tuple-element.56.refs_5_), channel_id=1, source_target_pairs={{0,4},{4,0},{8,12},{12,8},{16,20},{20,16},{24,28},{28,24},{32,36},... | collective-permute-start | bytes 4718600 | tf_op jit(solution)/shard_map/ppermute | solution.py:494
  9.8 35.0 %copy-start.1 = (f32[2,4,4]{2,1,0:T(4,128)S(1)}, f32[2,4,4]{2,1,0:T(4,128)}, u32[]{:S(2)}) copy-start(f32[2,4,4]{2,1,0:T(4,128)} %hc_res.3) | copy-start | bytes 388
  27.6 19.2 %collective-permute-start.7 = (bf16[3072,256]{1,0:T(8,128)(2,1)}, bf16[3072,256]{1,0:T(8,128)(2,1)S(1)}, u32[]{:S(2)}, u32[]{:S(2)}) collective-permute-start(bf16[3072,256]{1,0:T(8,128)(2,1)} %collective-permute-done.2.refs_10_), channel_id=1, source_target_pairs={{0,4},{4,0},{8,12},{12,8},{16,20},{20,16},{24,28},{28,24},{32,36},... | collective-permute-start | bytes 4718600 | tf_op jit(solution)/shard_map/ppermute | solution.py:494
  28.0 18.9 %collective-permute-start.8 = (bf16[3072,256]{1,0:T(8,128)(2,1)}, bf16[3072,256]{1,0:T(8,128)(2,1)S(1)}, u32[]{:S(2)}, u32[]{:S(2)}) collective-permute-start(bf16[3072,256]{1,0:T(8,128)(2,1)} %collective-permute-done.3.refs_11_), channel_id=1, source_target_pairs={{0,4},{4,0},{8,12},{12,8},{16,20},{20,16},{24,28},{28,24},{32,36},... | collective-permute-start | bytes 4718600 | tf_op jit(solution)/shard_map/ppermute | solution.py:494
  28.1 9.9 %collective-permute-start.4 = (bf16[64,2048]{1,0:T(8,128)(2,1)S(1)}, bf16[64,2048]{1,0:T(8,128)(2,1)S(1)}, u32[]{:S(2)}, u32[]{:S(2)}) collective-permute-start(bf16[64,2048]{1,0:T(8,128)(2,1)S(1)} %get-tuple-element.44), channel_id=1, source_target_pairs={{0,1},{1,2},{2,3},{3,0},{4,5},{5,6},{6,7},{7,4},{8,9},{9,10},{10,1... | collective-permute-start | bytes 786440 | tf_op jit(solution)/shard_map/ppermute | solution.py:551
  29.7 15.1 %collective-permute-start.5 = (bf16[64,2048]{1,0:T(8,128)(2,1)S(1)}, bf16[64,2048]{1,0:T(8,128)(2,1)S(1)}, u32[]{:S(2)}, u32[]{:S(2)}) collective-permute-start(bf16[64,2048]{1,0:T(8,128)(2,1)S(1)} %get-tuple-element.45), channel_id=1, source_target_pairs={{0,2},{1,3},{2,0},{3,1},{4,6},{5,7},{6,4},{7,5},{8,10},{9,11},{10,... | collective-permute-start | bytes 786440 | tf_op jit(solution)/shard_map/ppermute | solution.py:551
  32.6 12.2 %collective-permute-start.6 = (bf16[64,2048]{1,0:T(8,128)(2,1)S(1)}, bf16[64,2048]{1,0:T(8,128)(2,1)S(1)}, u32[]{:S(2)}, u32[]{:S(2)}) collective-permute-start(bf16[64,2048]{1,0:T(8,128)(2,1)S(1)} %get-tuple-element.46), channel_id=1, source_target_pairs={{0,3},{1,0},{2,1},{3,2},{4,7},{5,4},{6,5},{7,6},{8,11},{9,8},{10,9... | collective-permute-start | bytes 786440 | tf_op jit(solution)/shard_map/ppermute | solution.py:551
  46.9 13.4 %collective-permute-start.18 = (bf16[64,2048]{1,0:T(8,128)(2,1)S(1)}, bf16[64,2048]{1,0:T(8,128)(2,1)S(1)}, u32[]{:S(2)}, u32[]{:S(2)}) collective-permute-start(bf16[64,2048]{1,0:T(8,128)(2,1)S(1)} %get-tuple-element.54.refs_0_), channel_id=1, source_target_pairs={{0,80},{4,84},{8,88},{12,92},{16,64},{20,68},{24,72},{28,76},{32,1... | collective-permute-start | bytes 786440 | tf_op jit(solution)/shard_map/ppermute | solution.py:494
  50.0 16.6 %collective-permute-start.17 = (bf16[64,2048]{1,0:T(8,128)(2,1)S(1)}, bf16[64,2048]{1,0:T(8,128)(2,1)S(1)}, u32[]{:S(2)}, u32[]{:S(2)}) collective-permute-start(bf16[64,2048]{1,0:T(8,128)(2,1)S(1)} %get-tuple-element.54.refs_0_), channel_id=1, source_target_pairs={{0,16},{4,20},{8,24},{12,28},{16,0},{20,4},{24,8},{28,12},{32,48},... | collective-permute-start | bytes 786440 | tf_op jit(solution)/shard_map/ppermute | solution.py:494
  52.5 14.1 %collective-permute-start.16 = (bf16[64,2048]{1,0:T(8,128)(2,1)S(1)}, bf16[64,2048]{1,0:T(8,128)(2,1)S(1)}, u32[]{:S(2)}, u32[]{:S(2)}) collective-permute-start(bf16[64,2048]{1,0:T(8,128)(2,1)S(1)} %get-tuple-element.54.refs_0_), channel_id=1, source_target_pairs={{0,64},{4,68},{8,72},{12,76},{16,80},{20,84},{24,88},{28,92},{32,9... | collective-permute-start | bytes 786440 | tf_op jit(solution)/shard_map/ppermute | solution.py:494
  53.6 18.0 %collective-permute-start.15 = (bf16[64,2048]{1,0:T(8,128)(2,1)S(1)}, bf16[64,2048]{1,0:T(8,128)(2,1)S(1)}, u32[]{:S(2)}, u32[]{:S(2)}) collective-permute-start(bf16[64,2048]{1,0:T(8,128)(2,1)S(1)} %get-tuple-element.54.refs_0_), channel_id=1, source_target_pairs={{0,104},{4,108},{8,112},{12,116},{16,120},{20,124},{24,96},{28,100... | collective-permute-start | bytes 786440 | tf_op jit(solution)/shard_map/ppermute | solution.py:494
  55.8 30.8 %collective-permute-start.11 = (bf16[64,2048]{1,0:T(8,128)(2,1)S(1)}, bf16[64,2048]{1,0:T(8,128)(2,1)S(1)}, u32[]{:S(2)}, u32[]{:S(2)}) collective-permute-start(bf16[64,2048]{1,0:T(8,128)(2,1)S(1)} %get-tuple-element.54.refs_0_), channel_id=1, source_target_pairs={{0,56},{4,60},{8,32},{12,36},{16,40},{20,44},{24,48},{28,52},{32,8... | collective-permute-start | bytes 786440 | tf_op jit(solution)/shard_map/ppermute | solution.py:494
  60.3 28.2 %collective-permute-start.10 = (bf16[64,2048]{1,0:T(8,128)(2,1)S(1)}, bf16[64,2048]{1,0:T(8,128)(2,1)S(1)}, u32[]{:S(2)}, u32[]{:S(2)}) collective-permute-start(bf16[64,2048]{1,0:T(8,128)(2,1)S(1)} %get-tuple-element.54.refs_0_), channel_id=1, source_target_pairs={{0,120},{4,124},{8,96},{12,100},{16,104},{20,108},{24,112},{28,116... | collective-permute-start | bytes 786440 | tf_op jit(solution)/shard_map/ppermute | solution.py:494
  66.6 23.0 %collective-permute-start.9 = (bf16[64,2048]{1,0:T(8,128)(2,1)S(1)}, bf16[64,2048]{1,0:T(8,128)(2,1)S(1)}, u32[]{:S(2)}, u32[]{:S(2)}) collective-permute-start(bf16[64,2048]{1,0:T(8,128)(2,1)S(1)} %get-tuple-element.54.refs_0_), channel_id=1, source_target_pairs={{0,40},{4,44},{8,48},{12,52},{16,56},{20,60},{24,32},{28,36},{32,7... | collective-permute-start | bytes 786440 | tf_op jit(solution)/shard_map/ppermute | solution.py:494
  77.6 30.0 %collective-permute-start.19 = (bf16[64,2048]{1,0:T(8,128)(2,1)S(1)}, bf16[64,2048]{1,0:T(8,128)(2,1)S(1)}, u32[]{:S(2)}, u32[]{:S(2)}) collective-permute-start(bf16[64,2048]{1,0:T(8,128)(2,1)S(1)} %get-tuple-element.67), channel_id=1, source_target_pairs={{0,56},{4,60},{8,32},{12,36},{16,40},{20,44},{24,48},{28,52},{32,8... | collective-permute-start | bytes 786440 | tf_op jit(solution)/shard_map/ppermute | solution.py:494
  77.7 30.0 %collective-permute-start.20 = (bf16[64,2048]{1,0:T(8,128)(2,1)S(1)}, bf16[64,2048]{1,0:T(8,128)(2,1)S(1)}, u32[]{:S(2)}, u32[]{:S(2)}) collective-permute-start(bf16[64,2048]{1,0:T(8,128)(2,1)S(1)} %get-tuple-element.68), channel_id=1, source_target_pairs={{0,64},{4,68},{8,72},{12,76},{16,80},{20,84},{24,88},{28,92},{32,9... | collective-permute-start | bytes 786440 | tf_op jit(solution)/shard_map/ppermute | solution.py:494
  86.5 21.1 %collective-permute-start.21 = (bf16[64,2048]{1,0:T(8,128)(2,1)S(1)}, bf16[64,2048]{1,0:T(8,128)(2,1)S(1)}, u32[]{:S(2)}, u32[]{:S(2)}) collective-permute-start(bf16[64,2048]{1,0:T(8,128)(2,1)S(1)} %get-tuple-element.69), channel_id=1, source_target_pairs={{0,16},{4,20},{8,24},{12,28},{16,0},{20,4},{24,8},{28,12},{32,48},... | collective-permute-start | bytes 786440 | tf_op jit(solution)/shard_map/ppermute | solution.py:494
  88.5 19.2 %collective-permute-start.22 = (bf16[64,2048]{1,0:T(8,128)(2,1)S(1)}, bf16[64,2048]{1,0:T(8,128)(2,1)S(1)}, u32[]{:S(2)}, u32[]{:S(2)}) collective-permute-start(bf16[64,2048]{1,0:T(8,128)(2,1)S(1)} %get-tuple-element.70), channel_id=1, source_target_pairs={{0,80},{4,84},{8,88},{12,92},{16,64},{20,68},{24,72},{28,76},{32,1... | collective-permute-start | bytes 786440 | tf_op jit(solution)/shard_map/ppermute | solution.py:494
  95.6 15.6 %collective-permute-start.12 = (bf16[64,2048]{1,0:T(8,128)(2,1)S(1)}, bf16[64,2048]{1,0:T(8,128)(2,1)S(1)}, u32[]{:S(2)}, u32[]{:S(2)}) collective-permute-start(bf16[64,2048]{1,0:T(8,128)(2,1)S(1)} %get-tuple-element.64), channel_id=1, source_target_pairs={{0,120},{4,124},{8,96},{12,100},{16,104},{20,108},{24,112},{28,116... | collective-permute-start | bytes 786440 | tf_op jit(solution)/shard_map/ppermute | solution.py:494
  107.6 14.0 %collective-permute-start.13 = (bf16[64,2048]{1,0:T(8,128)(2,1)S(1)}, bf16[64,2048]{1,0:T(8,128)(2,1)S(1)}, u32[]{:S(2)}, u32[]{:S(2)}) collective-permute-start(bf16[64,2048]{1,0:T(8,128)(2,1)S(1)} %get-tuple-element.65), channel_id=1, source_target_pairs={{0,40},{4,44},{8,48},{12,52},{16,56},{20,60},{24,32},{28,36},{32,7... | collective-permute-start | bytes 786440 | tf_op jit(solution)/shard_map/ppermute | solution.py:494
  107.6 14.4 %collective-permute-start.14 = (bf16[64,2048]{1,0:T(8,128)(2,1)S(1)}, bf16[64,2048]{1,0:T(8,128)(2,1)S(1)}, u32[]{:S(2)}, u32[]{:S(2)}) collective-permute-start(bf16[64,2048]{1,0:T(8,128)(2,1)S(1)} %get-tuple-element.66), channel_id=1, source_target_pairs={{0,104},{4,108},{8,112},{12,116},{16,120},{20,124},{24,96},{28,100... | collective-permute-start | bytes 786440 | tf_op jit(solution)/shard_map/ppermute | solution.py:494
  (8 other events, 98.7 us)

commit v7 on v6

--- a/solution.py
+++ b/solution.py
@@ -24,7 +24,6 @@
 PACKED = 3072
 OFFSETS = ((1, 1), (-1, -1), (1, -1), (-1, 1), (2, 0), (0, 2), (2, 2))
 MEMBERS = len(OFFSETS) + 1
-FIRST = 4
 CH = 4
 NT = (((1,), (1,)), ((), ()))
 
@@ -558,7 +557,7 @@
     first, rows = mid(hc_in, hc_res, hc_out, [out[0], p1, p2, p3], own)
     rows, weights = lax.optimization_barrier((rows, weights))
     pieces = [rows] + [shift(rows, dx, dz) for dx, dz in OFFSETS]
-    sums = ffn(pieces[:FIRST], weights) + ffn(pieces[FIRST:], weights)
+    sums = ffn(pieces, weights)
     back = [sums[0]] + [shift(t, -dx, -dz) for t, (dx, dz) in zip(sums[1:], OFFSETS)]
     final = last(place, slot_owner, draft_len, hc_res, hc_out, first, back)
     new_streams = (

time: 125 us -> 132 us (1.056); the launches traced: 125 us -> 130 us
  starting transfers between devices: 42.9 us -> 53.6 us
  Pallas kernels: 33.8 us -> 30.7 us
  waiting for transfers between devices: 47.3 us -> 44.8 us
    ppermute x20, starting transfers between devices: 37.1 us -> 47.8 us  [send(): return lax.ppermute(v, 'req', pairs(move))]
    pallas_call x2 -> x1, Pallas kernels: 11.9 us -> 8.77 us  [ffn(): pl.pallas_call(functools.partial(ffn_kernel, n), name='ffn', out_shape=tu...]
    ppermute x20, waiting for transfers between devices: 36.4 us -> 34 us  [send(): return lax.ppermute(v, 'req', pairs(move))]
  transfers between devices with their start and end apart: 23 -> 23, of which waited for: 11 -> 11; matrix products, arithmetic and copies ran while one was open for 0% -> 0% of each run, Pallas kernels for 23% -> 13%
where the time goes in v7:
time: 132 us; the launch traced here: 130 us
  starting transfers between devices  53.6 us (41%)
  waiting for transfers between devices  44.8 us (34%)
  Pallas kernels  30.7 us (23%)
    ppermute x20, starting transfers between devices, send(): return lax.ppermute(v, 'req', pairs(move))  47.8 us
    ppermute x20, waiting for transfers between devices, send(): return lax.ppermute(v, 'req', pairs(move))  34 us
    pallas_call x1, Pallas kernels, front(): pl.pallas_call(front_kernel, name='front', out_shape=(pltpu.VMEM((SLOTS *...  15 us
    ppermute x3, waiting for transfers between devices, body(): lax.ppermute(v, 'head', [(y, (y + k) % 4) for y in range(4)])  10.9 us
    pallas_call x1, Pallas kernels, ffn(): pl.pallas_call(functools.partial(ffn_kernel, n), name='ffn', out_shape=tu...  8.77 us
    ppermute x3, starting transfers between devices, body(): lax.ppermute(v, 'head', [(y, (y + k) % 4) for y in range(4)])  5.83 us
    pallas_call x1, Pallas kernels, last(): pl.pallas_call(last_kernel, name='last', out_shape=jax.ShapeDtypeStruct((...  2.88 us
  transfers between devices with their start and end apart: 23, of which 11 were waited for; matrix products, arithmetic and copies ran while one was open for 0% of the time, Pallas kernels for 13%

profile of v7, /device:TPU:0, one launch (start us, length us, event | category | flops | bytes accessed | tf_op | source)
XLA Modules:
  0.0 130.1 jit_solution(11599826012478719286)
XLA Ops:
  2.7 4.2 %collective-permute-start.2 = (bf16[3072,256]{1,0:T(8,128)(2,1)S(1)}, bf16[3072,256]{1,0:T(8,128)(2,1)}, u32[]{:S(2)}, u32[]{:S(2)}) collective-permute-start(bf16[3072,256]{1,0:T(8,128)(2,1)S(1)} %get-tuple-element.55.refs_8_), channel_id=1, source_target_pairs={{0,24},{4,12},{8,0},{12,20},{16,8},{20,28},{24,16},{28,4},{32,56},... | collective-permute-start | bytes 4718600 | tf_op jit(solution)/shard_map/ppermute | solution.py:493
  6.9 2.8 %collective-permute-start.3 = (bf16[3072,256]{1,0:T(8,128)(2,1)S(1)}, bf16[3072,256]{1,0:T(8,128)(2,1)}, u32[]{:S(2)}, u32[]{:S(2)}) collective-permute-start(bf16[3072,256]{1,0:T(8,128)(2,1)S(1)} %get-tuple-element.56.refs_9_), channel_id=1, source_target_pairs={{0,96},{4,36},{8,104},{12,44},{16,112},{20,52},{24,120},{28,60},{3... | collective-permute-start | bytes 4718600 | tf_op jit(solution)/shard_map/ppermute | solution.py:493
  9.8 15.0 %front.1 = (bf16[64,2048]{1,0:T(8,128)(2,1)S(1)}, bf16[64,2048]{1,0:T(8,128)(2,1)S(1)}, bf16[64,2048]{1,0:T(8,128)(2,1)S(1)}, bf16[64,2048]{1,0:T(8,128)(2,1)S(1...) custom-call(s32[2]{0:T(128)S(1)} %pad_add_fusion.place, s32[128]{0:T(128)S(1)} %copy-done.4, ...), custom_call_target="tpu_custom_call" | custom-call | tf_op jit(solution)/shard_map/front/pallas_call | solution.py:253
  24.9 2.7 %collective-permute-done.3.refs_15_ = bf16[3072,256]{1,0:T(8,128)(2,1)} collective-permute-done((bf16[3072,256]{1,0:T(8,128)(2,1)S(1)}, bf16[3072,256]{1,0:T(8,128)(2,1)}, u32[]{:S(2)}, u32[]{:S(2)}) %collective-permute-start.3) | collective-permute-done | bytes 1572896 | tf_op jit(solution)/shard_map/ppermute | solution.py:493
  29.7 2.9 %collective-permute-start.5 = (bf16[64,2048]{1,0:T(8,128)(2,1)S(1)}, bf16[64,2048]{1,0:T(8,128)(2,1)S(1)}, u32[]{:S(2)}, u32[]{:S(2)}) collective-permute-start(bf16[64,2048]{1,0:T(8,128)(2,1)S(1)} %get-tuple-element.45), channel_id=1, source_target_pairs={{0,2},{1,3},{2,0},{3,1},{4,6},{5,7},{6,4},{7,5},{8,10},{9,11},{10,... | collective-permute-start | bytes 786440 | tf_op jit(solution)/shard_map/ppermute | solution.py:550
  33.9 4.1 %collective-permute-done.4.p1 = bf16[64,2048]{1,0:T(8,128)(2,1)S(1)} collective-permute-done((bf16[64,2048]{1,0:T(8,128)(2,1)S(1)}, bf16[64,2048]{1,0:T(8,128)(2,1)S(1)}, u32[]{:S(2)}, u32[]{:S(2)}) %collective-permute-start.4) | collective-permute-done | bytes 262176 | tf_op jit(solution)/shard_map/ppermute | solution.py:550
  38.0 6.8 %collective-permute-done.5.p2 = bf16[64,2048]{1,0:T(8,128)(2,1)S(1)} collective-permute-done((bf16[64,2048]{1,0:T(8,128)(2,1)S(1)}, bf16[64,2048]{1,0:T(8,128)(2,1)S(1)}, u32[]{:S(2)}, u32[]{:S(2)}) %collective-permute-start.5) | collective-permute-done | bytes 262176 | tf_op jit(solution)/shard_map/ppermute | solution.py:550
  44.8 2.0 %mid.1 = (bf16[4,64,2048]{2,1,0:T(8,128)(2,1)S(1)}, bf16[64,2048]{1,0:T(8,128)(2,1)S(1)}) custom-call(f32[2,4]{1,0:T(2,128)S(1)} %copy-done.2, f32[2,4,4]{2,1,0:T(4,128)S(1)} %copy-done.1, f32[2,4]{1,0:T(2,128)S(1)} %copy-done.3, bf16[64,2048]{1,0:T(8,128)(2,1)S(1)} %get-tuple-element.43.p0, bf16[64,2048]{1,0:T(8,128)(2,1)S(1)} %collective-permute-done.4.p1, ...), custom_call_target="tpu_custom_call" | custom-call | tf_op jit(solution)/shard_map/mid/pallas_call | solution.py:341
  46.9 3.1 %collective-permute-start.15 = (bf16[64,2048]{1,0:T(8,128)(2,1)S(1)}, bf16[64,2048]{1,0:T(8,128)(2,1)S(1)}, u32[]{:S(2)}, u32[]{:S(2)}) collective-permute-start(bf16[64,2048]{1,0:T(8,128)(2,1)S(1)} %get-tuple-element.54.refs_0_), channel_id=1, source_target_pairs={{0,80},{4,84},{8,88},{12,92},{16,64},{20,68},{24,72},{28,76},{32,1... | collective-permute-start | bytes 786440 | tf_op jit(solution)/shard_map/ppermute | solution.py:493
  50.0 2.5 %collective-permute-start.14 = (bf16[64,2048]{1,0:T(8,128)(2,1)S(1)}, bf16[64,2048]{1,0:T(8,128)(2,1)S(1)}, u32[]{:S(2)}, u32[]{:S(2)}) collective-permute-start(bf16[64,2048]{1,0:T(8,128)(2,1)S(1)} %get-tuple-element.54.refs_0_), channel_id=1, source_target_pairs={{0,16},{4,20},{8,24},{12,28},{16,0},{20,4},{24,8},{28,12},{32,48},... | collective-permute-start | bytes 786440 | tf_op jit(solution)/shard_map/ppermute | solution.py:493
  53.6 2.2 %collective-permute-start.12 = (bf16[64,2048]{1,0:T(8,128)(2,1)S(1)}, bf16[64,2048]{1,0:T(8,128)(2,1)S(1)}, u32[]{:S(2)}, u32[]{:S(2)}) collective-permute-start(bf16[64,2048]{1,0:T(8,128)(2,1)S(1)} %get-tuple-element.54.refs_0_), channel_id=1, source_target_pairs={{0,104},{4,108},{8,112},{12,116},{16,120},{20,124},{24,96},{28,100... | collective-permute-start | bytes 786440 | tf_op jit(solution)/shard_map/ppermute | solution.py:493
  57.8 2.5 %collective-permute-done.15.refs_7_ = bf16[64,2048]{1,0:T(8,128)(2,1)S(1)} collective-permute-done((bf16[64,2048]{1,0:T(8,128)(2,1)S(1)}, bf16[64,2048]{1,0:T(8,128)(2,1)S(1)}, u32[]{:S(2)}, u32[]{:S(2)}) %collective-permute-start.15) | collective-permute-done | bytes 262176 | tf_op jit(solution)/shard_map/ppermute | solution.py:493
  60.3 3.6 %collective-permute-start.10 = (bf16[64,2048]{1,0:T(8,128)(2,1)S(1)}, bf16[64,2048]{1,0:T(8,128)(2,1)S(1)}, u32[]{:S(2)}, u32[]{:S(2)}) collective-permute-start(bf16[64,2048]{1,0:T(8,128)(2,1)S(1)} %get-tuple-element.54.refs_0_), channel_id=1, source_target_pairs={{0,120},{4,124},{8,96},{12,100},{16,104},{20,108},{24,112},{28,116... | collective-permute-start | bytes 786440 | tf_op jit(solution)/shard_map/ppermute | solution.py:493
  63.9 2.7 %collective-permute-done.14.refs_6_ = bf16[64,2048]{1,0:T(8,128)(2,1)S(1)} collective-permute-done((bf16[64,2048]{1,0:T(8,128)(2,1)S(1)}, bf16[64,2048]{1,0:T(8,128)(2,1)S(1)}, u32[]{:S(2)}, u32[]{:S(2)}) %collective-permute-start.14) | collective-permute-done | bytes 262176 | tf_op jit(solution)/shard_map/ppermute | solution.py:493
  66.6 5.1 %collective-permute-done.12.refs_4_ = bf16[64,2048]{1,0:T(8,128)(2,1)S(1)} collective-permute-done((bf16[64,2048]{1,0:T(8,128)(2,1)S(1)}, bf16[64,2048]{1,0:T(8,128)(2,1)S(1)}, u32[]{:S(2)}, u32[]{:S(2)}) %collective-permute-start.12) | collective-permute-done | bytes 262176 | tf_op jit(solution)/shard_map/ppermute | solution.py:493
  71.7 2.1 %collective-permute-done.10.refs_2_ = bf16[64,2048]{1,0:T(8,128)(2,1)S(1)} collective-permute-done((bf16[64,2048]{1,0:T(8,128)(2,1)S(1)}, bf16[64,2048]{1,0:T(8,128)(2,1)S(1)}, u32[]{:S(2)}, u32[]{:S(2)}) %collective-permute-start.10) | collective-permute-done | bytes 262176 | tf_op jit(solution)/shard_map/ppermute | solution.py:493
  73.8 8.2 %collective-permute-done.9.refs_1_ = bf16[64,2048]{1,0:T(8,128)(2,1)S(1)} collective-permute-done((bf16[64,2048]{1,0:T(8,128)(2,1)S(1)}, bf16[64,2048]{1,0:T(8,128)(2,1)S(1)}, u32[]{:S(2)}, u32[]{:S(2)}) %collective-permute-start.9) | collective-permute-done | bytes 262176 | tf_op jit(solution)/shard_map/ppermute | solution.py:493
  82.0 8.8 %ffn.1 = (bf16[64,2048]{1,0:T(8,128)(2,1)S(1)}, bf16[64,2048]{1,0:T(8,128)(2,1)S(1)}, bf16[64,2048]{1,0:T(8,128)(2,1)S(1)}, bf16[64,2048]{1,0:T(8,128)(2,1)S(1)}...) custom-call(bf16[64,2048]{1,0:T(8,128)(2,1)S(1)} %get-tuple-element., ...), custom_call_target="tpu_custom_call" | custom-call | flops 6442450944 | bytes 4194304 | tf_op jit(solution)/shard_map/ffn/pallas_call | solution.py:460
  90.7 3.0 %collective-permute-start.16 = (bf16[64,2048]{1,0:T(8,128)(2,1)S(1)}, bf16[64,2048]{1,0:T(8,128)(2,1)S(1)}, u32[]{:S(2)}, u32[]{:S(2)}) collective-permute-start(bf16[64,2048]{1,0:T(8,128)(2,1)S(1)} %get-tuple-element.64), channel_id=1, source_target_pairs={{0,120},{4,124},{8,96},{12,100},{16,104},{20,108},{24,112},{28,116... | collective-permute-start | bytes 786440 | tf_op jit(solution)/shard_map/ppermute | solution.py:493
  93.7 7.2 %collective-permute-start.18 = (bf16[64,2048]{1,0:T(8,128)(2,1)S(1)}, bf16[64,2048]{1,0:T(8,128)(2,1)S(1)}, u32[]{:S(2)}, u32[]{:S(2)}) collective-permute-start(bf16[64,2048]{1,0:T(8,128)(2,1)S(1)} %get-tuple-element.66), channel_id=1, source_target_pairs={{0,104},{4,108},{8,112},{12,116},{16,120},{20,124},{24,96},{28,100... | collective-permute-start | bytes 786440 | tf_op jit(solution)/shard_map/ppermute | solution.py:493
  102.5 14.1 %collective-permute-start.21 = (bf16[64,2048]{1,0:T(8,128)(2,1)S(1)}, bf16[64,2048]{1,0:T(8,128)(2,1)S(1)}, u32[]{:S(2)}, u32[]{:S(2)}) collective-permute-start(bf16[64,2048]{1,0:T(8,128)(2,1)S(1)} %get-tuple-element.69), channel_id=1, source_target_pairs={{0,16},{4,20},{8,24},{12,28},{16,0},{20,4},{24,8},{28,12},{32,48},... | collective-permute-start | bytes 786440 | tf_op jit(solution)/shard_map/ppermute | solution.py:493
  117.0 5.6 %collective-permute-done.19.refs_4_ = bf16[64,2048]{1,0:T(8,128)(2,1)S(1)} collective-permute-done((bf16[64,2048]{1,0:T(8,128)(2,1)S(1)}, bf16[64,2048]{1,0:T(8,128)(2,1)S(1)}, u32[]{:S(2)}, u32[]{:S(2)}) %collective-permute-start.19) | collective-permute-done | bytes 262176 | tf_op jit(solution)/shard_map/ppermute | solution.py:493
  122.6 4.7 %collective-permute-done.22.refs_7_ = bf16[64,2048]{1,0:T(8,128)(2,1)S(1)} collective-permute-done((bf16[64,2048]{1,0:T(8,128)(2,1)S(1)}, bf16[64,2048]{1,0:T(8,128)(2,1)S(1)}, u32[]{:S(2)}, u32[]{:S(2)}) %collective-permute-start.22) | collective-permute-done | bytes 262176 | tf_op jit(solution)/shard_map/ppermute | solution.py:493
  127.2 2.9 %last.1 = bf16[4096,128]{1,0:T(8,128)(2,1)} custom-call(s32[2]{0:T(128)S(1)} %pad_add_fusion.place, s32[128]{0:T(128)S(1)} %copy-done.4, s32[128]{0:T(128)S(1)} %copy-done.5, f32[2,4,4]{2,1,0:T(4,128)S(1)} %copy-done.1, f32[2,4]{1,0:T(2,128)S(1)} %copy-done.3, bf16[4,64,2048]{2,1,0:T(8,128)(2,1)S(1)} %get-tuple-element.48.first, ...), custom_call_target="tpu_custom_call" | custom-call | tf_op jit(solution)/shard_map/last/pallas_call | solution.py:378
  (46 shorter events, 10.5 us)
Async XLA Ops:
  2.7 22.1 %collective-permute-start.2 = (bf16[3072,256]{1,0:T(8,128)(2,1)S(1)}, bf16[3072,256]{1,0:T(8,128)(2,1)}, u32[]{:S(2)}, u32[]{:S(2)}) collective-permute-start(bf16[3072,256]{1,0:T(8,128)(2,1)S(1)} %get-tuple-element.55.refs_8_), channel_id=1, source_target_pairs={{0,24},{4,12},{8,0},{12,20},{16,8},{20,28},{24,16},{28,4},{32,56},... | collective-permute-start | bytes 4718600 | tf_op jit(solution)/shard_map/ppermute | solution.py:493
  6.9 18.0 %collective-permute-start = (bf16[3072,256]{1,0:T(8,128)(2,1)S(1)}, bf16[3072,256]{1,0:T(8,128)(2,1)}, u32[]{:S(2)}, u32[]{:S(2)}) collective-permute-start(bf16[3072,256]{1,0:T(8,128)(2,1)S(1)} %get-tuple-element.55.refs_8_), channel_id=1, source_target_pairs={{0,4},{4,0},{8,12},{12,8},{16,20},{20,16},{24,28},{28,24},{32,36},... | collective-permute-start | bytes 4718600 | tf_op jit(solution)/shard_map/ppermute | solution.py:493
  6.9 20.7 %collective-permute-start.3 = (bf16[3072,256]{1,0:T(8,128)(2,1)S(1)}, bf16[3072,256]{1,0:T(8,128)(2,1)}, u32[]{:S(2)}, u32[]{:S(2)}) collective-permute-start(bf16[3072,256]{1,0:T(8,128)(2,1)S(1)} %get-tuple-element.56.refs_9_), channel_id=1, source_target_pairs={{0,96},{4,36},{8,104},{12,44},{16,112},{20,52},{24,120},{28,60},{3... | collective-permute-start | bytes 4718600 | tf_op jit(solution)/shard_map/ppermute | solution.py:493
  9.7 17.9 %collective-permute-start.1 = (bf16[3072,256]{1,0:T(8,128)(2,1)S(1)}, bf16[3072,256]{1,0:T(8,128)(2,1)}, u32[]{:S(2)}, u32[]{:S(2)}) collective-permute-start(bf16[3072,256]{1,0:T(8,128)(2,1)S(1)} %get-tuple-element.56.refs_9_), channel_id=1, source_target_pairs={{0,4},{4,0},{8,12},{12,8},{16,20},{20,16},{24,28},{28,24},{32,36},... | collective-permute-start | bytes 4718600 | tf_op jit(solution)/shard_map/ppermute | solution.py:493
  9.8 35.0 %copy-start.1 = (f32[2,4,4]{2,1,0:T(4,128)S(1)}, f32[2,4,4]{2,1,0:T(4,128)}, u32[]{:S(2)}) copy-start(f32[2,4,4]{2,1,0:T(4,128)} %hc_res.3) | copy-start | bytes 388
  27.6 19.2 %collective-permute-start.7 = (bf16[3072,256]{1,0:T(8,128)(2,1)}, bf16[3072,256]{1,0:T(8,128)(2,1)S(1)}, u32[]{:S(2)}, u32[]{:S(2)}) collective-permute-start(bf16[3072,256]{1,0:T(8,128)(2,1)} %collective-permute-done.2.refs_14_), channel_id=1, source_target_pairs={{0,4},{4,0},{8,12},{12,8},{16,20},{20,16},{24,28},{28,24},{32,36},... | collective-permute-start | bytes 4718600 | tf_op jit(solution)/shard_map/ppermute | solution.py:493
  28.0 18.9 %collective-permute-start.8 = (bf16[3072,256]{1,0:T(8,128)(2,1)}, bf16[3072,256]{1,0:T(8,128)(2,1)S(1)}, u32[]{:S(2)}, u32[]{:S(2)}) collective-permute-start(bf16[3072,256]{1,0:T(8,128)(2,1)} %collective-permute-done.3.refs_15_), channel_id=1, source_target_pairs={{0,4},{4,0},{8,12},{12,8},{16,20},{20,16},{24,28},{28,24},{32,36},... | collective-permute-start | bytes 4718600 | tf_op jit(solution)/shard_map/ppermute | solution.py:493
  28.1 9.9 %collective-permute-start.4 = (bf16[64,2048]{1,0:T(8,128)(2,1)S(1)}, bf16[64,2048]{1,0:T(8,128)(2,1)S(1)}, u32[]{:S(2)}, u32[]{:S(2)}) collective-permute-start(bf16[64,2048]{1,0:T(8,128)(2,1)S(1)} %get-tuple-element.44), channel_id=1, source_target_pairs={{0,1},{1,2},{2,3},{3,0},{4,5},{5,6},{6,7},{7,4},{8,9},{9,10},{10,1... | collective-permute-start | bytes 786440 | tf_op jit(solution)/shard_map/ppermute | solution.py:550
  29.7 15.1 %collective-permute-start.5 = (bf16[64,2048]{1,0:T(8,128)(2,1)S(1)}, bf16[64,2048]{1,0:T(8,128)(2,1)S(1)}, u32[]{:S(2)}, u32[]{:S(2)}) collective-permute-start(bf16[64,2048]{1,0:T(8,128)(2,1)S(1)} %get-tuple-element.45), channel_id=1, source_target_pairs={{0,2},{1,3},{2,0},{3,1},{4,6},{5,7},{6,4},{7,5},{8,10},{9,11},{10,... | collective-permute-start | bytes 786440 | tf_op jit(solution)/shard_map/ppermute | solution.py:550
  32.6 12.2 %collective-permute-start.6 = (bf16[64,2048]{1,0:T(8,128)(2,1)S(1)}, bf16[64,2048]{1,0:T(8,128)(2,1)S(1)}, u32[]{:S(2)}, u32[]{:S(2)}) collective-permute-start(bf16[64,2048]{1,0:T(8,128)(2,1)S(1)} %get-tuple-element.46), channel_id=1, source_target_pairs={{0,3},{1,0},{2,1},{3,2},{4,7},{5,4},{6,5},{7,6},{8,11},{9,8},{10,9... | collective-permute-start | bytes 786440 | tf_op jit(solution)/shard_map/ppermute | solution.py:550
  46.9 13.4 %collective-permute-start.15 = (bf16[64,2048]{1,0:T(8,128)(2,1)S(1)}, bf16[64,2048]{1,0:T(8,128)(2,1)S(1)}, u32[]{:S(2)}, u32[]{:S(2)}) collective-permute-start(bf16[64,2048]{1,0:T(8,128)(2,1)S(1)} %get-tuple-element.54.refs_0_), channel_id=1, source_target_pairs={{0,80},{4,84},{8,88},{12,92},{16,64},{20,68},{24,72},{28,76},{32,1... | collective-permute-start | bytes 786440 | tf_op jit(solution)/shard_map/ppermute | solution.py:493
  50.0 16.6 %collective-permute-start.14 = (bf16[64,2048]{1,0:T(8,128)(2,1)S(1)}, bf16[64,2048]{1,0:T(8,128)(2,1)S(1)}, u32[]{:S(2)}, u32[]{:S(2)}) collective-permute-start(bf16[64,2048]{1,0:T(8,128)(2,1)S(1)} %get-tuple-element.54.refs_0_), channel_id=1, source_target_pairs={{0,16},{4,20},{8,24},{12,28},{16,0},{20,4},{24,8},{28,12},{32,48},... | collective-permute-start | bytes 786440 | tf_op jit(solution)/shard_map/ppermute | solution.py:493
  52.5 14.1 %collective-permute-start.13 = (bf16[64,2048]{1,0:T(8,128)(2,1)S(1)}, bf16[64,2048]{1,0:T(8,128)(2,1)S(1)}, u32[]{:S(2)}, u32[]{:S(2)}) collective-permute-start(bf16[64,2048]{1,0:T(8,128)(2,1)S(1)} %get-tuple-element.54.refs_0_), channel_id=1, source_target_pairs={{0,64},{4,68},{8,72},{12,76},{16,80},{20,84},{24,88},{28,92},{32,9... | collective-permute-start | bytes 786440 | tf_op jit(solution)/shard_map/ppermute | solution.py:493
  53.6 18.0 %collective-permute-start.12 = (bf16[64,2048]{1,0:T(8,128)(2,1)S(1)}, bf16[64,2048]{1,0:T(8,128)(2,1)S(1)}, u32[]{:S(2)}, u32[]{:S(2)}) collective-permute-start(bf16[64,2048]{1,0:T(8,128)(2,1)S(1)} %get-tuple-element.54.refs_0_), channel_id=1, source_target_pairs={{0,104},{4,108},{8,112},{12,116},{16,120},{20,124},{24,96},{28,100... | collective-permute-start | bytes 786440 | tf_op jit(solution)/shard_map/ppermute | solution.py:493
  55.8 15.9 %collective-permute-start.11 = (bf16[64,2048]{1,0:T(8,128)(2,1)S(1)}, bf16[64,2048]{1,0:T(8,128)(2,1)S(1)}, u32[]{:S(2)}, u32[]{:S(2)}) collective-permute-start(bf16[64,2048]{1,0:T(8,128)(2,1)S(1)} %get-tuple-element.54.refs_0_), channel_id=1, source_target_pairs={{0,56},{4,60},{8,32},{12,36},{16,40},{20,44},{24,48},{28,52},{32,8... | collective-permute-start | bytes 786440 | tf_op jit(solution)/shard_map/ppermute | solution.py:493
  60.3 13.4 %collective-permute-start.10 = (bf16[64,2048]{1,0:T(8,128)(2,1)S(1)}, bf16[64,2048]{1,0:T(8,128)(2,1)S(1)}, u32[]{:S(2)}, u32[]{:S(2)}) collective-permute-start(bf16[64,2048]{1,0:T(8,128)(2,1)S(1)} %get-tuple-element.54.refs_0_), channel_id=1, source_target_pairs={{0,120},{4,124},{8,96},{12,100},{16,104},{20,108},{24,112},{28,116... | collective-permute-start | bytes 786440 | tf_op jit(solution)/shard_map/ppermute | solution.py:493
  66.6 15.4 %collective-permute-start.9 = (bf16[64,2048]{1,0:T(8,128)(2,1)S(1)}, bf16[64,2048]{1,0:T(8,128)(2,1)S(1)}, u32[]{:S(2)}, u32[]{:S(2)}) collective-permute-start(bf16[64,2048]{1,0:T(8,128)(2,1)S(1)} %get-tuple-element.54.refs_0_), channel_id=1, source_target_pairs={{0,40},{4,44},{8,48},{12,52},{16,56},{20,60},{24,32},{28,36},{32,7... | collective-permute-start | bytes 786440 | tf_op jit(solution)/shard_map/ppermute | solution.py:493
  90.7 11.8 %collective-permute-start.16 = (bf16[64,2048]{1,0:T(8,128)(2,1)S(1)}, bf16[64,2048]{1,0:T(8,128)(2,1)S(1)}, u32[]{:S(2)}, u32[]{:S(2)}) collective-permute-start(bf16[64,2048]{1,0:T(8,128)(2,1)S(1)} %get-tuple-element.64), channel_id=1, source_target_pairs={{0,120},{4,124},{8,96},{12,100},{16,104},{20,108},{24,112},{28,116... | collective-permute-start | bytes 786440 | tf_op jit(solution)/shard_map/ppermute | solution.py:493
  93.7 23.2 %collective-permute-start.17 = (bf16[64,2048]{1,0:T(8,128)(2,1)S(1)}, bf16[64,2048]{1,0:T(8,128)(2,1)S(1)}, u32[]{:S(2)}, u32[]{:S(2)}) collective-permute-start(bf16[64,2048]{1,0:T(8,128)(2,1)S(1)} %get-tuple-element.65), channel_id=1, source_target_pairs={{0,40},{4,44},{8,48},{12,52},{16,56},{20,60},{24,32},{28,36},{32,7... | collective-permute-start | bytes 786440 | tf_op jit(solution)/shard_map/ppermute | solution.py:493
  93.7 23.2 %collective-permute-start.18 = (bf16[64,2048]{1,0:T(8,128)(2,1)S(1)}, bf16[64,2048]{1,0:T(8,128)(2,1)S(1)}, u32[]{:S(2)}, u32[]{:S(2)}) collective-permute-start(bf16[64,2048]{1,0:T(8,128)(2,1)S(1)} %get-tuple-element.66), channel_id=1, source_target_pairs={{0,104},{4,108},{8,112},{12,116},{16,120},{20,124},{24,96},{28,100... | collective-permute-start | bytes 786440 | tf_op jit(solution)/shard_map/ppermute | solution.py:493
  101.0 21.6 %collective-permute-start.19 = (bf16[64,2048]{1,0:T(8,128)(2,1)S(1)}, bf16[64,2048]{1,0:T(8,128)(2,1)S(1)}, u32[]{:S(2)}, u32[]{:S(2)}) collective-permute-start(bf16[64,2048]{1,0:T(8,128)(2,1)S(1)} %get-tuple-element.67), channel_id=1, source_target_pairs={{0,56},{4,60},{8,32},{12,36},{16,40},{20,44},{24,48},{28,52},{32,8... | collective-permute-start | bytes 786440 | tf_op jit(solution)/shard_map/ppermute | solution.py:493
  101.0 21.6 %collective-permute-start.20 = (bf16[64,2048]{1,0:T(8,128)(2,1)S(1)}, bf16[64,2048]{1,0:T(8,128)(2,1)S(1)}, u32[]{:S(2)}, u32[]{:S(2)}) collective-permute-start(bf16[64,2048]{1,0:T(8,128)(2,1)S(1)} %get-tuple-element.68), channel_id=1, source_target_pairs={{0,64},{4,68},{8,72},{12,76},{16,80},{20,84},{24,88},{28,92},{32,9... | collective-permute-start | bytes 786440 | tf_op jit(solution)/shard_map/ppermute | solution.py:493
  102.5 20.1 %collective-permute-start.21 = (bf16[64,2048]{1,0:T(8,128)(2,1)S(1)}, bf16[64,2048]{1,0:T(8,128)(2,1)S(1)}, u32[]{:S(2)}, u32[]{:S(2)}) collective-permute-start(bf16[64,2048]{1,0:T(8,128)(2,1)S(1)} %get-tuple-element.69), channel_id=1, source_target_pairs={{0,16},{4,20},{8,24},{12,28},{16,0},{20,4},{24,8},{28,12},{32,48},... | collective-permute-start | bytes 786440 | tf_op jit(solution)/shard_map/ppermute | solution.py:493
  117.0 10.3 %collective-permute-start.22 = (bf16[64,2048]{1,0:T(8,128)(2,1)S(1)}, bf16[64,2048]{1,0:T(8,128)(2,1)S(1)}, u32[]{:S(2)}, u32[]{:S(2)}) collective-permute-start(bf16[64,2048]{1,0:T(8,128)(2,1)S(1)} %get-tuple-element.70), channel_id=1, source_target_pairs={{0,80},{4,84},{8,88},{12,92},{16,64},{20,68},{24,72},{28,76},{32,1... | collective-permute-start | bytes 786440 | tf_op jit(solution)/shard_map/ppermute | solution.py:493
  (8 other events, 98.7 us)

commit v8 on v7

--- a/solution.py
+++ b/solution.py
@@ -24,6 +24,7 @@
 PACKED = 3072
 OFFSETS = ((1, 1), (-1, -1), (1, -1), (-1, 1), (2, 0), (0, 2), (2, 2))
 MEMBERS = len(OFFSETS) + 1
+FIRST = 4
 CH = 4
 NT = (((1,), (1,)), ((), ()))
 
@@ -527,8 +528,8 @@
     freq = jnp.asarray(np.concatenate([freq, freq])[None, :])
     st = streams.reshape(SLOTS, DRAFT, NS, LT, 128).transpose(0, 1, 3, 2, 4).reshape(-1, 128)
     one, two = pack(w_gate, w_up, w_down)
-    one_z = send(one, lambda x, z, c: (x, z + 2 * c - 1, c))
-    two_x = send(two, lambda x, z, c: (x + 2 * c - 1, z, c))
+    one_z = send(one, lambda x, z, c: (x, z ^ 1, c))
+    two_x = send(two, lambda x, z, c: (x ^ 1, z, c))
     one_c, two_c = other_core(one), other_core(two)
     *out, own, kv = front(
         place,
@@ -548,12 +549,12 @@
         w_output,
     )
     turn = lambda v, k: lax.ppermute(v, "head", [(y, (y + k) % 4) for y in range(4)])
-    out, one_c, two_c, one_z, two_x = lax.optimization_barrier((out, one_c, two_c, one_z, two_x))
-    one_zc, two_xc = other_core(one_z), other_core(two_x)
+    out, one_c, two_c = lax.optimization_barrier((out, one_c, two_c))
     p1 = turn(out[1], 1)
     p3 = turn(out[3], 3)
     p2 = turn(out[2], 2)
-    weights = (one, two, one_zc, two_xc, one_c, two_c, one_z, two_x)
+    p1, p2, p3, one_z, two_x = lax.optimization_barrier((p1, p2, p3, one_z, two_x))
+    weights = (one, two, other_core(one_z), other_core(two_x), one_c, two_c, one_z, two_x)
     first, rows = mid(hc_in, hc_res, hc_out, [out[0], p1, p2, p3], own)
     rows, weights = lax.optimization_barrier((rows, weights))
     pieces = [rows] + [shift(rows, dx, dz) for dx, dz in OFFSETS]

time: 132 us -> 122 us (0.924); the launches traced: 130 us -> 122 us
  starting transfers between devices: 53.6 us -> 35.5 us
  waiting for transfers between devices: 44.8 us -> 54.8 us
    ppermute x20, waiting for transfers between devices: 34 us -> 54.8 us  [send(): return lax.ppermute(v, 'req', pairs(move))]
    ppermute x20, starting transfers between devices: 47.8 us -> 29.6 us  [send(): return lax.ppermute(v, 'req', pairs(move))]
    ppermute x3, waiting for transfers between devices: 10.9 us -> 0.01 us  [body(): lax.ppermute(v, 'head', [(y, (y + k) % 4) for y in range(4)])]
  transfers between devices with their start and end apart: 23 -> 23, of which waited for: 11 -> 14; matrix products, arithmetic and copies ran while one was open for 0% -> 0% of each run, Pallas kernels for 13% -> 14%
where the time goes in v8:
time: 122 us
  waiting for transfers between devices  54.8 us (45%)
  starting transfers between devices  35.5 us (29%)
  Pallas kernels  30.7 us (25%)
    ppermute x20, waiting for transfers between devices, send(): return lax.ppermute(v, 'req', pairs(move))  54.8 us
    ppermute x20, starting transfers between devices, send(): return lax.ppermute(v, 'req', pairs(move))  29.6 us
    pallas_call x1, Pallas kernels, front(): pl.pallas_call(front_kernel, name='front', out_shape=(pltpu.VMEM((SLOTS *...  15 us
    pallas_call x1, Pallas kernels, ffn(): pl.pallas_call(functools.partial(ffn_kernel, n), name='ffn', out_shape=tu...  8.77 us
    ppermute x3, starting transfers between devices, body(): lax.ppermute(v, 'head', [(y, (y + k) % 4) for y in range(4)])  5.9 us
    pallas_call x1, Pallas kernels, last(): pl.pallas_call(last_kernel, name='last', out_shape=jax.ShapeDtypeStruct((...  2.88 us
  transfers between devices with their start and end apart: 23, of which 14 were waited for; matrix products, arithmetic and copies ran while one was open for 0% of the time, Pallas kernels for 14%

profile of v8, /device:TPU:0, one launch (start us, length us, event | category | flops | bytes accessed | tf_op | source)
XLA Modules:
  0.0 122.0 jit_solution(17211781322874831353)
XLA Ops:
  0.7 2.0 %pack.1 = (bf16[3072,256]{1,0:T(8,128)(2,1)S(1)}, bf16[3072,256]{1,0:T(8,128)(2,1)S(1)}) custom-call(bf16[2048,256]{1,0:T(8,128)(2,1)} %g.1, bf16[2048,256]{1,0:T(8,128)(2,1)} %u.1, bf16[256,2048]{1,0:T(8,128)(2,1)} %d.1), custom_call_target="tpu_custom_call" | custom-call | tf_op jit(solution)/shard_map/pack/pallas_call | solution.py:417
  3.3 2.0 %collective-permute-start.5 = (bf16[3072,256]{1,0:T(8,128)(2,1)S(1)}, bf16[3072,256]{1,0:T(8,128)(2,1)}, u32[]{:S(2)}, u32[]{:S(2)}) collective-permute-start(bf16[3072,256]{1,0:T(8,128)(2,1)S(1)} %get-tuple-element.61.refs_8_), channel_id=1, source_target_pairs={{0,8},{4,12},{8,0},{12,4},{16,24},{20,28},{24,16},{28,20},{32,40},... | collective-permute-start | bytes 4718600 | tf_op jit(solution)/shard_map/ppermute | solution.py:494
  6.9 15.0 %front.1 = (bf16[64,2048]{1,0:T(8,128)(2,1)S(1)}, bf16[64,2048]{1,0:T(8,128)(2,1)S(1)}, bf16[64,2048]{1,0:T(8,128)(2,1)S(1)}, bf16[64,2048]{1,0:T(8,128)(2,1)S(1...) custom-call(s32[2]{0:T(128)S(1)} %pad_add_fusion.place, s32[128]{0:T(128)S(1)} %copy-done.4, ...), custom_call_target="tpu_custom_call" | custom-call | tf_op jit(solution)/shard_map/front/pallas_call | solution.py:254
  23.6 2.9 %collective-permute-start.3 = (bf16[64,2048]{1,0:T(8,128)(2,1)S(1)}, bf16[64,2048]{1,0:T(8,128)(2,1)S(1)}, u32[]{:S(2)}, u32[]{:S(2)}) collective-permute-start(bf16[64,2048]{1,0:T(8,128)(2,1)S(1)} %get-tuple-element.48), channel_id=1, source_target_pairs={{0,2},{1,3},{2,0},{3,1},{4,6},{5,7},{6,4},{7,5},{8,10},{9,11},{10,... | collective-permute-start | bytes 786440 | tf_op jit(solution)/shard_map/ppermute | solution.py:551
  27.9 12.2 %collective-permute-done.5.refs_14_ = bf16[3072,256]{1,0:T(8,128)(2,1)} collective-permute-done((bf16[3072,256]{1,0:T(8,128)(2,1)S(1)}, bf16[3072,256]{1,0:T(8,128)(2,1)}, u32[]{:S(2)}, u32[]{:S(2)}) %collective-permute-start.5) | collective-permute-done | bytes 1572896 | tf_op jit(solution)/shard_map/ppermute | solution.py:494
  42.1 2.0 %mid.1 = (bf16[4,64,2048]{2,1,0:T(8,128)(2,1)S(1)}, bf16[64,2048]{1,0:T(8,128)(2,1)S(1)}) custom-call(f32[2,4]{1,0:T(2,128)S(1)} %copy-done.2, f32[2,4,4]{2,1,0:T(4,128)S(1)} %copy-done.1, f32[2,4]{1,0:T(2,128)S(1)} %copy-done.3, bf16[64,2048]{1,0:T(8,128)(2,1)S(1)} %get-tuple-element.46.p0, bf16[64,2048]{1,0:T(8,128)(2,1)S(1)} %collective-permute-done.2.p1, ...), custom_call_target="tpu_custom_call" | custom-call | tf_op jit(solution)/shard_map/mid/pallas_call | solution.py:342
  45.2 2.2 %collective-permute-done.8.refs_11_ = bf16[3072,256]{1,0:T(8,128)(2,1)S(1)} collective-permute-done((bf16[3072,256]{1,0:T(8,128)(2,1)}, bf16[3072,256]{1,0:T(8,128)(2,1)S(1)}, u32[]{:S(2)}, u32[]{:S(2)}) %collective-permute-start.8) | collective-permute-done | bytes 1572896 | tf_op jit(solution)/shard_map/ppermute | solution.py:494
  47.5 6.0 %collective-permute-start.15 = (bf16[64,2048]{1,0:T(8,128)(2,1)S(1)}, bf16[64,2048]{1,0:T(8,128)(2,1)S(1)}, u32[]{:S(2)}, u32[]{:S(2)}) collective-permute-start(bf16[64,2048]{1,0:T(8,128)(2,1)S(1)} %get-tuple-element.60.refs_0_), channel_id=1, source_target_pairs={{0,80},{4,84},{8,88},{12,92},{16,64},{20,68},{24,72},{28,76},{32,1... | collective-permute-start | bytes 786440 | tf_op jit(solution)/shard_map/ppermute | solution.py:494
  54.1 2.4 %collective-permute-start.12 = (bf16[64,2048]{1,0:T(8,128)(2,1)S(1)}, bf16[64,2048]{1,0:T(8,128)(2,1)S(1)}, u32[]{:S(2)}, u32[]{:S(2)}) collective-permute-start(bf16[64,2048]{1,0:T(8,128)(2,1)S(1)} %get-tuple-element.60.refs_0_), channel_id=1, source_target_pairs={{0,104},{4,108},{8,112},{12,116},{16,120},{20,124},{24,96},{28,100... | collective-permute-start | bytes 786440 | tf_op jit(solution)/shard_map/ppermute | solution.py:494
  56.5 1.8 %collective-permute-start.11 = (bf16[64,2048]{1,0:T(8,128)(2,1)S(1)}, bf16[64,2048]{1,0:T(8,128)(2,1)S(1)}, u32[]{:S(2)}, u32[]{:S(2)}) collective-permute-start(bf16[64,2048]{1,0:T(8,128)(2,1)S(1)} %get-tuple-element.60.refs_0_), channel_id=1, source_target_pairs={{0,56},{4,60},{8,32},{12,36},{16,40},{20,44},{24,48},{28,52},{32,8... | collective-permute-start | bytes 786440 | tf_op jit(solution)/shard_map/ppermute | solution.py:494
  58.2 2.1 %collective-permute-done.15.refs_7_ = bf16[64,2048]{1,0:T(8,128)(2,1)S(1)} collective-permute-done((bf16[64,2048]{1,0:T(8,128)(2,1)S(1)}, bf16[64,2048]{1,0:T(8,128)(2,1)S(1)}, u32[]{:S(2)}, u32[]{:S(2)}) %collective-permute-start.15) | collective-permute-done | bytes 262176 | tf_op jit(solution)/shard_map/ppermute | solution.py:494
  60.3 5.1 %collective-permute-start.10 = (bf16[64,2048]{1,0:T(8,128)(2,1)S(1)}, bf16[64,2048]{1,0:T(8,128)(2,1)S(1)}, u32[]{:S(2)}, u32[]{:S(2)}) collective-permute-start(bf16[64,2048]{1,0:T(8,128)(2,1)S(1)} %get-tuple-element.60.refs_0_), channel_id=1, source_target_pairs={{0,120},{4,124},{8,96},{12,100},{16,104},{20,108},{24,112},{28,116... | collective-permute-start | bytes 786440 | tf_op jit(solution)/shard_map/ppermute | solution.py:494
  65.4 5.3 %collective-permute-done.14.refs_6_ = bf16[64,2048]{1,0:T(8,128)(2,1)S(1)} collective-permute-done((bf16[64,2048]{1,0:T(8,128)(2,1)S(1)}, bf16[64,2048]{1,0:T(8,128)(2,1)S(1)}, u32[]{:S(2)}, u32[]{:S(2)}) %collective-permute-start.14) | collective-permute-done | bytes 262176 | tf_op jit(solution)/shard_map/ppermute | solution.py:494
  72.0 6.1 %collective-permute-done.10.refs_2_ = bf16[64,2048]{1,0:T(8,128)(2,1)S(1)} collective-permute-done((bf16[64,2048]{1,0:T(8,128)(2,1)S(1)}, bf16[64,2048]{1,0:T(8,128)(2,1)S(1)}, u32[]{:S(2)}, u32[]{:S(2)}) %collective-permute-start.10) | collective-permute-done | bytes 262176 | tf_op jit(solution)/shard_map/ppermute | solution.py:494
  78.1 4.1 %collective-permute-done.9.refs_1_ = bf16[64,2048]{1,0:T(8,128)(2,1)S(1)} collective-permute-done((bf16[64,2048]{1,0:T(8,128)(2,1)S(1)}, bf16[64,2048]{1,0:T(8,128)(2,1)S(1)}, u32[]{:S(2)}, u32[]{:S(2)}) %collective-permute-start.9) | collective-permute-done | bytes 262176 | tf_op jit(solution)/shard_map/ppermute | solution.py:494
  82.2 8.8 %ffn.1 = (bf16[64,2048]{1,0:T(8,128)(2,1)S(1)}, bf16[64,2048]{1,0:T(8,128)(2,1)S(1)}, bf16[64,2048]{1,0:T(8,128)(2,1)S(1)}, bf16[64,2048]{1,0:T(8,128)(2,1)S(1)}...) custom-call(bf16[64,2048]{1,0:T(8,128)(2,1)S(1)} %get-tuple-element., ...), custom_call_target="tpu_custom_call" | custom-call | flops 6442450944 | bytes 4194304 | tf_op jit(solution)/shard_map/ffn/pallas_call | solution.py:461
  91.0 2.9 %collective-permute-start.17 = (bf16[64,2048]{1,0:T(8,128)(2,1)S(1)}, bf16[64,2048]{1,0:T(8,128)(2,1)S(1)}, u32[]{:S(2)}, u32[]{:S(2)}) collective-permute-start(bf16[64,2048]{1,0:T(8,128)(2,1)S(1)} %get-tuple-element.71), channel_id=1, source_target_pairs={{0,40},{4,44},{8,48},{12,52},{16,56},{20,60},{24,32},{28,36},{32,7... | collective-permute-start | bytes 786440 | tf_op jit(solution)/shard_map/ppermute | solution.py:494
  95.6 2.5 %collective-permute-start.19 = (bf16[64,2048]{1,0:T(8,128)(2,1)S(1)}, bf16[64,2048]{1,0:T(8,128)(2,1)S(1)}, u32[]{:S(2)}, u32[]{:S(2)}) collective-permute-start(bf16[64,2048]{1,0:T(8,128)(2,1)S(1)} %get-tuple-element.73), channel_id=1, source_target_pairs={{0,56},{4,60},{8,32},{12,36},{16,40},{20,44},{24,48},{28,52},{32,8... | collective-permute-start | bytes 786440 | tf_op jit(solution)/shard_map/ppermute | solution.py:494
  98.1 2.0 %collective-permute-start.20 = (bf16[64,2048]{1,0:T(8,128)(2,1)S(1)}, bf16[64,2048]{1,0:T(8,128)(2,1)S(1)}, u32[]{:S(2)}, u32[]{:S(2)}) collective-permute-start(bf16[64,2048]{1,0:T(8,128)(2,1)S(1)} %get-tuple-element.74), channel_id=1, source_target_pairs={{0,64},{4,68},{8,72},{12,76},{16,80},{20,84},{24,88},{28,92},{32,9... | collective-permute-start | bytes 786440 | tf_op jit(solution)/shard_map/ppermute | solution.py:494
  101.3 4.9 %collective-permute-done.17.refs_2_ = bf16[64,2048]{1,0:T(8,128)(2,1)S(1)} collective-permute-done((bf16[64,2048]{1,0:T(8,128)(2,1)S(1)}, bf16[64,2048]{1,0:T(8,128)(2,1)S(1)}, u32[]{:S(2)}, u32[]{:S(2)}) %collective-permute-start.17) | collective-permute-done | bytes 262176 | tf_op jit(solution)/shard_map/ppermute | solution.py:494
  106.2 4.2 %collective-permute-done.18.refs_3_ = bf16[64,2048]{1,0:T(8,128)(2,1)S(1)} collective-permute-done((bf16[64,2048]{1,0:T(8,128)(2,1)S(1)}, bf16[64,2048]{1,0:T(8,128)(2,1)S(1)}, u32[]{:S(2)}, u32[]{:S(2)}) %collective-permute-start.18) | collective-permute-done | bytes 262176 | tf_op jit(solution)/shard_map/ppermute | solution.py:494
  110.5 6.7 %collective-permute-done.19.refs_4_ = bf16[64,2048]{1,0:T(8,128)(2,1)S(1)} collective-permute-done((bf16[64,2048]{1,0:T(8,128)(2,1)S(1)}, bf16[64,2048]{1,0:T(8,128)(2,1)S(1)}, u32[]{:S(2)}, u32[]{:S(2)}) %collective-permute-start.19) | collective-permute-done | bytes 262176 | tf_op jit(solution)/shard_map/ppermute | solution.py:494
  117.2 1.9 %collective-permute-done.21.refs_6_ = bf16[64,2048]{1,0:T(8,128)(2,1)S(1)} collective-permute-done((bf16[64,2048]{1,0:T(8,128)(2,1)S(1)}, bf16[64,2048]{1,0:T(8,128)(2,1)S(1)}, u32[]{:S(2)}, u32[]{:S(2)}) %collective-permute-start.21) | collective-permute-done | bytes 262176 | tf_op jit(solution)/shard_map/ppermute | solution.py:494
  119.1 2.9 %last.1 = bf16[4096,128]{1,0:T(8,128)(2,1)} custom-call(s32[2]{0:T(128)S(1)} %pad_add_fusion.place, s32[128]{0:T(128)S(1)} %copy-done.4, s32[128]{0:T(128)S(1)} %copy-done.5, f32[2,4,4]{2,1,0:T(4,128)S(1)} %copy-done.1, f32[2,4]{1,0:T(2,128)S(1)} %copy-done.3, bf16[4,64,2048]{2,1,0:T(8,128)(2,1)S(1)} %get-tuple-element.54.first, ...), custom_call_target="tpu_custom_call" | custom-call | tf_op jit(solution)/shard_map/last/pallas_call | solution.py:379
  (46 shorter events, 13.1 us)
Async XLA Ops:
  2.7 19.3 %collective-permute-start = (bf16[3072,256]{1,0:T(8,128)(2,1)S(1)}, bf16[3072,256]{1,0:T(8,128)(2,1)}, u32[]{:S(2)}, u32[]{:S(2)}) collective-permute-start(bf16[3072,256]{1,0:T(8,128)(2,1)S(1)} %get-tuple-element.61.refs_8_), channel_id=1, source_target_pairs={{0,4},{4,0},{8,12},{12,8},{16,20},{20,16},{24,28},{28,24},{32,36},... | collective-permute-start | bytes 4718600 | tf_op jit(solution)/shard_map/ppermute | solution.py:494
  2.8 19.2 %collective-permute-start.1 = (bf16[3072,256]{1,0:T(8,128)(2,1)S(1)}, bf16[3072,256]{1,0:T(8,128)(2,1)}, u32[]{:S(2)}, u32[]{:S(2)}) collective-permute-start(bf16[3072,256]{1,0:T(8,128)(2,1)S(1)} %get-tuple-element.62.refs_9_), channel_id=1, source_target_pairs={{0,4},{4,0},{8,12},{12,8},{16,20},{20,16},{24,28},{28,24},{32,36},... | collective-permute-start | bytes 4718600 | tf_op jit(solution)/shard_map/ppermute | solution.py:494
  3.3 36.8 %collective-permute-start.5 = (bf16[3072,256]{1,0:T(8,128)(2,1)S(1)}, bf16[3072,256]{1,0:T(8,128)(2,1)}, u32[]{:S(2)}, u32[]{:S(2)}) collective-permute-start(bf16[3072,256]{1,0:T(8,128)(2,1)S(1)} %get-tuple-element.61.refs_8_), channel_id=1, source_target_pairs={{0,8},{4,12},{8,0},{12,4},{16,24},{20,28},{24,16},{28,20},{32,40},... | collective-permute-start | bytes 4718600 | tf_op jit(solution)/shard_map/ppermute | solution.py:494
  5.3 36.2 %collective-permute-start.6 = (bf16[3072,256]{1,0:T(8,128)(2,1)S(1)}, bf16[3072,256]{1,0:T(8,128)(2,1)}, u32[]{:S(2)}, u32[]{:S(2)}) collective-permute-start(bf16[3072,256]{1,0:T(8,128)(2,1)S(1)} %get-tuple-element.62.refs_9_), channel_id=1, source_target_pairs={{0,32},{4,36},{8,40},{12,44},{16,48},{20,52},{24,56},{28,60},{32,0... | collective-permute-start | bytes 4718600 | tf_op jit(solution)/shard_map/ppermute | solution.py:494
  6.9 35.2 %copy-start.1 = (f32[2,4,4]{2,1,0:T(4,128)S(1)}, f32[2,4,4]{2,1,0:T(4,128)}, u32[]{:S(2)}) copy-start(f32[2,4,4]{2,1,0:T(4,128)} %hc_res.3) | copy-start | bytes 388
  22.0 19.5 %collective-permute-start.2 = (bf16[64,2048]{1,0:T(8,128)(2,1)S(1)}, bf16[64,2048]{1,0:T(8,128)(2,1)S(1)}, u32[]{:S(2)}, u32[]{:S(2)}) collective-permute-start(bf16[64,2048]{1,0:T(8,128)(2,1)S(1)} %get-tuple-element.47), channel_id=1, source_target_pairs={{0,1},{1,2},{2,3},{3,0},{4,5},{5,6},{6,7},{7,4},{8,9},{9,10},{10,1... | collective-permute-start | bytes 786440 | tf_op jit(solution)/shard_map/ppermute | solution.py:551
  23.6 17.9 %collective-permute-start.3 = (bf16[64,2048]{1,0:T(8,128)(2,1)S(1)}, bf16[64,2048]{1,0:T(8,128)(2,1)S(1)}, u32[]{:S(2)}, u32[]{:S(2)}) collective-permute-start(bf16[64,2048]{1,0:T(8,128)(2,1)S(1)} %get-tuple-element.48), channel_id=1, source_target_pairs={{0,2},{1,3},{2,0},{3,1},{4,6},{5,7},{6,4},{7,5},{8,10},{9,11},{10,... | collective-permute-start | bytes 786440 | tf_op jit(solution)/shard_map/ppermute | solution.py:551
  26.6 15.0 %collective-permute-start.4 = (bf16[64,2048]{1,0:T(8,128)(2,1)S(1)}, bf16[64,2048]{1,0:T(8,128)(2,1)S(1)}, u32[]{:S(2)}, u32[]{:S(2)}) collective-permute-start(bf16[64,2048]{1,0:T(8,128)(2,1)S(1)} %get-tuple-element.49), channel_id=1, source_target_pairs={{0,3},{1,0},{2,1},{3,2},{4,7},{5,4},{6,5},{7,6},{8,11},{9,8},{10,9... | collective-permute-start | bytes 786440 | tf_op jit(solution)/shard_map/ppermute | solution.py:551
  41.5 3.7 %collective-permute-start.7 = (bf16[3072,256]{1,0:T(8,128)(2,1)}, bf16[3072,256]{1,0:T(8,128)(2,1)S(1)}, u32[]{:S(2)}, u32[]{:S(2)}) collective-permute-start(bf16[3072,256]{1,0:T(8,128)(2,1)} %collective-permute-done.5.refs_14_), channel_id=1, source_target_pairs={{0,4},{4,0},{8,12},{12,8},{16,20},{20,16},{24,28},{28,24},{32,36},... | collective-permute-start | bytes 4718600 | tf_op jit(solution)/shard_map/ppermute | solution.py:494
  41.6 5.9 %collective-permute-start.8 = (bf16[3072,256]{1,0:T(8,128)(2,1)}, bf16[3072,256]{1,0:T(8,128)(2,1)S(1)}, u32[]{:S(2)}, u32[]{:S(2)}) collective-permute-start(bf16[3072,256]{1,0:T(8,128)(2,1)} %collective-permute-done.6.refs_15_), channel_id=1, source_target_pairs={{0,4},{4,0},{8,12},{12,8},{16,20},{20,16},{24,28},{28,24},{32,36},... | collective-permute-start | bytes 4718600 | tf_op jit(solution)/shard_map/ppermute | solution.py:494
  47.5 12.8 %collective-permute-start.15 = (bf16[64,2048]{1,0:T(8,128)(2,1)S(1)}, bf16[64,2048]{1,0:T(8,128)(2,1)S(1)}, u32[]{:S(2)}, u32[]{:S(2)}) collective-permute-start(bf16[64,2048]{1,0:T(8,128)(2,1)S(1)} %get-tuple-element.60.refs_0_), channel_id=1, source_target_pairs={{0,80},{4,84},{8,88},{12,92},{16,64},{20,68},{24,72},{28,76},{32,1... | collective-permute-start | bytes 786440 | tf_op jit(solution)/shard_map/ppermute | solution.py:494
  53.5 17.2 %collective-permute-start.14 = (bf16[64,2048]{1,0:T(8,128)(2,1)S(1)}, bf16[64,2048]{1,0:T(8,128)(2,1)S(1)}, u32[]{:S(2)}, u32[]{:S(2)}) collective-permute-start(bf16[64,2048]{1,0:T(8,128)(2,1)S(1)} %get-tuple-element.60.refs_0_), channel_id=1, source_target_pairs={{0,16},{4,20},{8,24},{12,28},{16,0},{20,4},{24,8},{28,12},{32,48},... | collective-permute-start | bytes 786440 | tf_op jit(solution)/shard_map/ppermute | solution.py:494
  53.5 17.2 %collective-permute-start.13 = (bf16[64,2048]{1,0:T(8,128)(2,1)S(1)}, bf16[64,2048]{1,0:T(8,128)(2,1)S(1)}, u32[]{:S(2)}, u32[]{:S(2)}) collective-permute-start(bf16[64,2048]{1,0:T(8,128)(2,1)S(1)} %get-tuple-element.60.refs_0_), channel_id=1, source_target_pairs={{0,64},{4,68},{8,72},{12,76},{16,80},{20,84},{24,88},{28,92},{32,9... | collective-permute-start | bytes 786440 | tf_op jit(solution)/shard_map/ppermute | solution.py:494
  54.1 17.9 %collective-permute-start.12 = (bf16[64,2048]{1,0:T(8,128)(2,1)S(1)}, bf16[64,2048]{1,0:T(8,128)(2,1)S(1)}, u32[]{:S(2)}, u32[]{:S(2)}) collective-permute-start(bf16[64,2048]{1,0:T(8,128)(2,1)S(1)} %get-tuple-element.60.refs_0_), channel_id=1, source_target_pairs={{0,104},{4,108},{8,112},{12,116},{16,120},{20,124},{24,96},{28,100... | collective-permute-start | bytes 786440 | tf_op jit(solution)/shard_map/ppermute | solution.py:494
  56.5 15.5 %collective-permute-start.11 = (bf16[64,2048]{1,0:T(8,128)(2,1)S(1)}, bf16[64,2048]{1,0:T(8,128)(2,1)S(1)}, u32[]{:S(2)}, u32[]{:S(2)}) collective-permute-start(bf16[64,2048]{1,0:T(8,128)(2,1)S(1)} %get-tuple-element.60.refs_0_), channel_id=1, source_target_pairs={{0,56},{4,60},{8,32},{12,36},{16,40},{20,44},{24,48},{28,52},{32,8... | collective-permute-start | bytes 786440 | tf_op jit(solution)/shard_map/ppermute | solution.py:494
  60.3 17.8 %collective-permute-start.10 = (bf16[64,2048]{1,0:T(8,128)(2,1)S(1)}, bf16[64,2048]{1,0:T(8,128)(2,1)S(1)}, u32[]{:S(2)}, u32[]{:S(2)}) collective-permute-start(bf16[64,2048]{1,0:T(8,128)(2,1)S(1)} %get-tuple-element.60.refs_0_), channel_id=1, source_target_pairs={{0,120},{4,124},{8,96},{12,100},{16,104},{20,108},{24,112},{28,116... | collective-permute-start | bytes 786440 | tf_op jit(solution)/shard_map/ppermute | solution.py:494
  70.7 11.4 %collective-permute-start.9 = (bf16[64,2048]{1,0:T(8,128)(2,1)S(1)}, bf16[64,2048]{1,0:T(8,128)(2,1)S(1)}, u32[]{:S(2)}, u32[]{:S(2)}) collective-permute-start(bf16[64,2048]{1,0:T(8,128)(2,1)S(1)} %get-tuple-element.60.refs_0_), channel_id=1, source_target_pairs={{0,40},{4,44},{8,48},{12,52},{16,56},{20,60},{24,32},{28,36},{32,7... | collective-permute-start | bytes 786440 | tf_op jit(solution)/shard_map/ppermute | solution.py:494
  91.0 10.3 %collective-permute-start.16 = (bf16[64,2048]{1,0:T(8,128)(2,1)S(1)}, bf16[64,2048]{1,0:T(8,128)(2,1)S(1)}, u32[]{:S(2)}, u32[]{:S(2)}) collective-permute-start(bf16[64,2048]{1,0:T(8,128)(2,1)S(1)} %get-tuple-element.70), channel_id=1, source_target_pairs={{0,120},{4,124},{8,96},{12,100},{16,104},{20,108},{24,112},{28,116... | collective-permute-start | bytes 786440 | tf_op jit(solution)/shard_map/ppermute | solution.py:494
  91.0 15.2 %collective-permute-start.17 = (bf16[64,2048]{1,0:T(8,128)(2,1)S(1)}, bf16[64,2048]{1,0:T(8,128)(2,1)S(1)}, u32[]{:S(2)}, u32[]{:S(2)}) collective-permute-start(bf16[64,2048]{1,0:T(8,128)(2,1)S(1)} %get-tuple-element.71), channel_id=1, source_target_pairs={{0,40},{4,44},{8,48},{12,52},{16,56},{20,60},{24,32},{28,36},{32,7... | collective-permute-start | bytes 786440 | tf_op jit(solution)/shard_map/ppermute | solution.py:494
  94.0 16.5 %collective-permute-start.18 = (bf16[64,2048]{1,0:T(8,128)(2,1)S(1)}, bf16[64,2048]{1,0:T(8,128)(2,1)S(1)}, u32[]{:S(2)}, u32[]{:S(2)}) collective-permute-start(bf16[64,2048]{1,0:T(8,128)(2,1)S(1)} %get-tuple-element.72), channel_id=1, source_target_pairs={{0,104},{4,108},{8,112},{12,116},{16,120},{20,124},{24,96},{28,100... | collective-permute-start | bytes 786440 | tf_op jit(solution)/shard_map/ppermute | solution.py:494
  95.6 21.6 %collective-permute-start.19 = (bf16[64,2048]{1,0:T(8,128)(2,1)S(1)}, bf16[64,2048]{1,0:T(8,128)(2,1)S(1)}, u32[]{:S(2)}, u32[]{:S(2)}) collective-permute-start(bf16[64,2048]{1,0:T(8,128)(2,1)S(1)} %get-tuple-element.73), channel_id=1, source_target_pairs={{0,56},{4,60},{8,32},{12,36},{16,40},{20,44},{24,48},{28,52},{32,8... | collective-permute-start | bytes 786440 | tf_op jit(solution)/shard_map/ppermute | solution.py:494
  98.1 19.1 %collective-permute-start.20 = (bf16[64,2048]{1,0:T(8,128)(2,1)S(1)}, bf16[64,2048]{1,0:T(8,128)(2,1)S(1)}, u32[]{:S(2)}, u32[]{:S(2)}) collective-permute-start(bf16[64,2048]{1,0:T(8,128)(2,1)S(1)} %get-tuple-element.74), channel_id=1, source_target_pairs={{0,64},{4,68},{8,72},{12,76},{16,80},{20,84},{24,88},{28,92},{32,9... | collective-permute-start | bytes 786440 | tf_op jit(solution)/shard_map/ppermute | solution.py:494
  101.3 17.8 %collective-permute-start.21 = (bf16[64,2048]{1,0:T(8,128)(2,1)S(1)}, bf16[64,2048]{1,0:T(8,128)(2,1)S(1)}, u32[]{:S(2)}, u32[]{:S(2)}) collective-permute-start(bf16[64,2048]{1,0:T(8,128)(2,1)S(1)} %get-tuple-element.75), channel_id=1, source_target_pairs={{0,16},{4,20},{8,24},{12,28},{16,0},{20,4},{24,8},{28,12},{32,48},... | collective-permute-start | bytes 786440 | tf_op jit(solution)/shard_map/ppermute | solution.py:494
  106.2 12.9 %collective-permute-start.22 = (bf16[64,2048]{1,0:T(8,128)(2,1)S(1)}, bf16[64,2048]{1,0:T(8,128)(2,1)S(1)}, u32[]{:S(2)}, u32[]{:S(2)}) collective-permute-start(bf16[64,2048]{1,0:T(8,128)(2,1)S(1)} %get-tuple-element.76), channel_id=1, source_target_pairs={{0,80},{4,84},{8,88},{12,92},{16,64},{20,68},{24,72},{28,76},{32,1... | collective-permute-start | bytes 786440 | tf_op jit(solution)/shard_map/ppermute | solution.py:494
  (8 other events, 78.7 us)
